TPU v7x, 128 devices: a whole 4x4x4 slice. The times are simulated.
128 devices in a mesh: facet: 8 (over z, core), vis: 16 (over y, x).
Axes of the slice: x: 4, y: 4, z: 4, core: 2. Of those that a mesh axis runs over, the one named last changes fastest.
Arguments:
- vis_obs: float32 [16384, 2, 4, 1024], P(('facet', 'vis')), may hold values from -6 to 6
- uv_coords: float32 [16384, 2, 1024], P(('facet', 'vis')), may hold values from -16 to 16
- vis_weight: float32 [16384, 1024], P(('facet', 'vis')), may hold values from 0.5 to 900, as said below
- block_group: int32 [16384, 1], P(('facet', 'vis')), may hold values from 0 to 127; in each aligned block of 128 rows (0 to 127, 128 to 255, ...) at most 2 rows name the same one
- tile_slot: int32 [16384], P(('facet', 'vis')), may hold values from 0 to 63
- w_plane: int32 [16384], P(('facet', 'vis')), may hold values from 0 to 31
- model_tiles: bfloat16 [8192, 2, 32, 128], P(('facet', 'vis')), may hold values from -6 to 6
- w_kernels: bfloat16 [32, 2, 32, 32], replicated, may hold values from -0.75 to 0.75
Outputs:
- residual_vis: float32 [16384, 2, 4, 1024], P(('facet', 'vis'))
- residual_tiles: float32 [8192, 2, 32, 128], P(('facet', 'vis'))
Inputs may be any that keep to these rules, and one draw needn't show every extreme that they name: `block_group`: in the 128 rows of one device (aligned blocks of 128 rows) no group is named by more than 2 rows, a bound that some block reaches. `vis_weight`: Positive.
All inputs are finite; a program needn't handle non-finite values.
Results may differ from a plain program's by a relative error of at most 0.0045.
Values may be sent and summed in bfloat16 or wider, within the bound.
A program may use at most 128 MiB of HBM per device.

v0:
```python
import functools
import math

import jax
import jax.numpy as jnp
from jax import lax
from jax.sharding import Mesh
from jax.sharding import PartitionSpec as P

FACET_VIS = ("facet_0", "facet_1", "vis_0", "vis_1")


def by_axis(shard, axes):
    return functools.reduce(lax.psum, axes, shard)


def complex_product(form_text, left_side, right_side):
    real_part = jnp.einsum(
        form_text, left_side[:, 0], right_side[:, 0], preferred_element_type=jnp.float32
    ) - jnp.einsum(form_text, left_side[:, 1], right_side[:, 1], preferred_element_type=jnp.float32)
    imag_part = jnp.einsum(
        form_text, left_side[:, 0], right_side[:, 1], preferred_element_type=jnp.float32
    ) + jnp.einsum(form_text, left_side[:, 1], right_side[:, 0], preferred_element_type=jnp.float32)
    return jnp.stack((real_part, imag_part), axis=1)


def conjugate(operand):
    return jnp.stack((operand[:, 0], -operand[:, 1]), axis=1)


def phasors(coordinates, sub_width):
    offsets = (jnp.arange(sub_width) - sub_width // 2).astype(jnp.float32) * (
        -2.0 * math.pi / sub_width
    )
    angles = coordinates[:, :, None, :] * offsets[None, None, :, None]
    return (jnp.cos(angles), jnp.sin(angles))


def degrid_grid(tile_rows, kernels, coordinates, observed, weights):
    block_count = tile_rows.shape[0]
    sub_width = tile_rows.shape[2]
    span_width = tile_rows.shape[3]
    pol_count = span_width // sub_width
    vis_count = coordinates.shape[-1]
    left_prod = complex_product("nij,njq->niq", kernels, tile_rows).astype(jnp.bfloat16)
    left_prod = left_prod.reshape(block_count, 2, sub_width, pol_count, sub_width)
    kerneled = (
        complex_product("nlpm,nkm->nlpk", left_prod, kernels)
        .reshape(block_count, 2, sub_width, span_width)
        .astype(jnp.bfloat16)
    )
    cosine, sine_part = phasors(coordinates, sub_width)
    along_u = jnp.stack((cosine[:, 0], sine_part[:, 0]), axis=1).astype(jnp.bfloat16)
    phase_real = cosine[:, 1][:, None]
    phase_imag = sine_part[:, 1][:, None]
    spread = complex_product("nlq,nlk->nqk", kerneled, along_u).reshape(
        block_count, 2, pol_count, sub_width, vis_count
    )
    predicted_real = (
        jnp.sum(spread[:, 0] * phase_real - spread[:, 1] * phase_imag, axis=2) / sub_width
    )
    predicted_imag = (
        jnp.sum(spread[:, 0] * phase_imag + spread[:, 1] * phase_real, axis=2) / sub_width
    )
    residual = observed - jnp.stack((predicted_real, predicted_imag), axis=1)
    factor = (weights / sub_width)[:, None, None, :]
    residual_real = residual[:, 0][:, :, None, :]
    residual_imag = residual[:, 1][:, :, None, :]
    weighted_real = (residual_real * phase_real + residual_imag * phase_imag) * factor
    weighted_imag = (residual_imag * phase_real - residual_real * phase_imag) * factor
    weighted = (
        jnp.stack((weighted_real, weighted_imag), axis=1)
        .reshape(block_count, 2, span_width, vis_count)
        .astype(jnp.bfloat16)
    )
    gridded = complex_product("nlk,nqk->nlq", conjugate(along_u), weighted).astype(jnp.bfloat16)
    back_prod = complex_product("nji,njq->niq", conjugate(kernels), gridded).astype(jnp.bfloat16)
    back_prod = back_prod.reshape(block_count, 2, sub_width, pol_count, sub_width)
    contribution = complex_product("nlpm,nmk->nlpk", back_prod, conjugate(kernels)).reshape(
        block_count, 2, sub_width, span_width
    )
    return (residual, contribution)


def shards(vis_obs, uv_coords, vis_weight, block_group, tile_slot, w_plane, model_tiles, w_kernels):
    blocks = vis_obs.shape[0]
    groups = lax.axis_size(FACET_VIS)
    owned_tiles = model_tiles.shape[0]
    tile_shape = model_tiles.shape[1:]
    capacity = max(2, 2 * blocks // groups)
    target = block_group[:, 0]
    markers = (target[:, None] == jnp.arange(groups, dtype=jnp.int32)[None, :]).astype(jnp.int32)
    before = jnp.cumsum(markers, axis=0) - markers
    slot_rank = jnp.sum(before * markers, axis=1)
    position = target * capacity + slot_rank
    wanted = jnp.full((groups * capacity,), -1, jnp.int32).at[position].set(tile_slot)
    requested = lax.all_to_all(
        wanted.reshape(groups, capacity), FACET_VIS, split_axis=0, concat_axis=0, tiled=True
    )
    chosen = jnp.take(model_tiles, jnp.maximum(requested, 0).reshape(-1), axis=0)
    chosen = chosen.reshape((groups, capacity) + tile_shape)
    arrived = lax.all_to_all(chosen, FACET_VIS, split_axis=0, concat_axis=0, tiled=True)
    arrived = arrived.reshape((groups * capacity,) + tile_shape)
    tile_rows = jnp.take(arrived, position, axis=0)
    kernels = jnp.take(w_kernels, w_plane, axis=0)
    batch_size = math.gcd(blocks, 8)

    def split_blocks(operand):
        return operand.reshape((blocks // batch_size, batch_size) + operand.shape[1:])

    def process(inputs):
        return degrid_grid(inputs[0], inputs[1], inputs[2], inputs[3], inputs[4])

    residual, contribution = lax.map(
        process,
        (
            split_blocks(tile_rows),
            split_blocks(kernels),
            split_blocks(uv_coords),
            split_blocks(vis_obs),
            split_blocks(vis_weight),
        ),
    )
    residual = residual.reshape(vis_obs.shape)
    contribution = contribution.reshape((blocks,) + tile_shape)
    outgoing = (
        jnp.zeros((groups * capacity,) + tile_shape, jnp.float32).at[position].set(contribution)
    )
    outgoing = outgoing.reshape((groups, capacity) + tile_shape)
    returned = lax.all_to_all(outgoing, FACET_VIS, split_axis=0, concat_axis=0, tiled=True)
    returned = returned.reshape(groups * capacity, -1)
    selector = (
        requested.reshape(-1)[None, :] == jnp.arange(owned_tiles, dtype=jnp.int32)[:, None]
    ).astype(jnp.float32)
    summed = jnp.dot(
        selector, returned, precision=lax.Precision.HIGHEST, preferred_element_type=jnp.float32
    )
    summed = summed.reshape(model_tiles.shape)
    weight_sum = by_axis(jnp.sum(vis_weight), FACET_VIS)
    scaling = blocks * groups * vis_obs.shape[-1] / weight_sum
    return (residual, summed * scaling)


def solution(mesh):
    split = Mesh(mesh.devices.reshape(4, 2, 4, 4), ("facet_0", "facet_1", "vis_0", "vis_1"))
    return jax.shard_map(
        shards,
        mesh=split,
        in_specs=(
            P(FACET_VIS, None, None, None),
            P(FACET_VIS, None, None),
            P(FACET_VIS, None),
            P(FACET_VIS, None),
            P(FACET_VIS),
            P(FACET_VIS),
            P(FACET_VIS, None, None, None),
            P(),
        ),
        out_specs=(P(FACET_VIS, None, None, None), P(FACET_VIS, None, None, None)),
        check_vma=False,
    )
```

profile of v0, /device:TPU:1, one launch (start us, length us, event | category | flops | bytes accessed | tf_op | source)
XLA Modules:
  0.0 763.1 jit_solution(1024174097948574699)
XLA Ops:
  4.4 20.9 %all_to_all.22 = s32[128,1,2]{2,1,0:T(1,128)S(1)} all-to-all(s32[128,1,2]{2,1,0:T(1,128)S(1)} %bitcast.279), channel_id=1, replica_groups=mesh['facet_0'=4,'facet_1'=2,'vis_0'=4,'vis_1'=4] {'facet_0','facet_1','..., dimensions={0} | all-to-all | bytes 2048 | tf_op jit(solution)/shard_map/all_to_all | solution.py:97
  43.3 48.8 %all-to-all-done.1 = bf16[128,2,2,32,128]{4,3,2,1,0:T(8,128)(2,1)} async-done(((bf16[128,2,2,32,128]{4,3,2,1,0:T(8,128)(2,1)}), bf16[128,2,2,32,128]{4,3,2,1,0:T(8,128)(2,1)}, u32[]{:S(2)}, u32[]{:S(2)}) %all-to-all-start.1) | async-done | bytes 4194336 | tf_op jit(solution)/shard_map/all_to_all | solution.py:102
  96.9 493.5 %while.14 = (s32[]{:T(128)}, f32[16,8,2,4,1024]{4,3,2,1,0:T(4,128)}, f32[16,8,2,32,128]{4,3,2,1,0:T(8,128)}, f32[16,8,2,4,1024]{4,3,2,1,0:T(4,128)}, bf16[16,8,2...) while((s32[]{:T(128)}, ...), condition=%wide.region_6.7_spmd, body=%wide.region_3.6_spmd.sunk | while | flops 593404032 | bytes 89195904 | solution.py:114
  102.7 7.3 multiply_cosine_fusion.2
  133.6 7.3 multiply_cosine_fusion.2
  164.4 7.3 multiply_cosine_fusion.2
  195.3 7.3 multiply_cosine_fusion.2
  226.1 7.3 multiply_cosine_fusion.2
  257.0 7.3 multiply_cosine_fusion.2
  287.8 7.3 multiply_cosine_fusion.2
  318.6 7.3 multiply_cosine_fusion.2
  349.5 7.3 multiply_cosine_fusion.2
  380.4 7.3 multiply_cosine_fusion.2
  411.2 7.3 multiply_cosine_fusion.2
  472.9 7.3 multiply_cosine_fusion.2
  503.7 7.3 multiply_cosine_fusion.2
  534.6 7.3 multiply_cosine_fusion.2
  594.7 19.3 %scatter_fusion = f32[256,2,32,128]{3,2,1,0:T(8,128)} fusion(f32[256,2,32,128]{3,2,1,0:T(8,128)} %broadcast_in_dim.71, s32[128]{0:T(128)S(1)} %bitcast.285, f32[128,2,32,128]{3,2,1,0:T(8,128)} %bitcast.277), kind=kCustom, calls=%fused_computation.4 | custom fusion | bytes 12583424 | tf_op jit(solution)/shard_map/scatter | solution.py:127
  621.5 52.3 %psum.28 = f32[]{:T(128)} all-reduce(f32[]{:T(128)} %reduce_sum.46), channel_id=1, replica_groups=mesh['facet_0'=4,'facet_1'=2,'vis_0'=4,'vis_1'=4] {'facet_0'}, use_global_device_ids=true, to_apply=%region_9.10 | all-reduce | flops 1 | bytes 8 | tf_op jit(solution)/shard_map/psum | solution.py:14
  673.8 24.4 %psum.29 = f32[]{:T(128)} all-reduce(f32[]{:T(128)} %psum.28), channel_id=1, replica_groups=mesh['facet_0'=4,'facet_1'=2,'vis_0'=4,'vis_1'=4] {'facet_1'}, use_global_device_ids=true, to_apply=%region_10.11 | all-reduce | flops 1 | bytes 8 | tf_op jit(solution)/shard_map/psum | solution.py:14
  698.2 26.7 %psum.30 = f32[]{:T(128)} all-reduce(f32[]{:T(128)} %psum.29), channel_id=1, replica_groups=mesh['facet_0'=4,'facet_1'=2,'vis_0'=4,'vis_1'=4] {'vis_0'}, use_global_device_ids=true, to_apply=%region_11.12 | all-reduce | flops 1 | bytes 8 | tf_op jit(solution)/shard_map/psum | solution.py:14
  725.0 9.5 %psum.31 = f32[]{:T(128)} all-reduce(f32[]{:T(128)} %psum.30), channel_id=1, replica_groups=mesh['facet_0'=4,'facet_1'=2,'vis_0'=4,'vis_1'=4] {'vis_1'}, use_global_device_ids=true, to_apply=%region_12.13 | all-reduce | flops 1 | bytes 8 | tf_op jit(solution)/shard_map/psum | solution.py:14
  735.3 9.4 %reshape.351 = f32[256,8192]{1,0:T(8,128)} reshape(f32[128,2,2,32,128]{4,3,2,1,0:T(8,128)} %all-to-all-done.2) | data formatting | bytes 16777216 | tf_op jit(solution)/shard_map/reshape | solution.py:131
  744.7 9.0 %copy.129 = f32[8192,256]{1,0:T(8,128)} copy(f32[8192,256]{0,1:T(8,128)} %bitcast.272) | data formatting | bytes 16777216 | tf_op jit(solution)/shard_map/dot_general | solution.py:135
  (879 shorter events, 435.2 us)
Async XLA Ops:
  0.6 27.2 %copy-start = (bf16[64,2,32,128]{3,2,1,0:T(8,128)(2,1)S(1)}, bf16[64,2,32,128]{3,2,1,0:T(8,128)(2,1)}, u32[]{:S(2)}) copy-start(bf16[64,2,32,128]{3,2,1,0:T(8,128)(2,1)} %param.16) | copy-start | bytes 3145732
  34.8 5.7 copy-start.4
  34.8 5.9 copy-start.2
  34.8 57.3 %all-to-all-start.1 = ((bf16[128,2,2,32,128]{4,3,2,1,0:T(8,128)(2,1)}), bf16[128,2,2,32,128]{4,3,2,1,0:T(8,128)(2,1)}, u32[]{:S(2)}, u32[]{:S(2)}) async-start(bf16[128,2,2,32,128]{4,3,2,1,0:T(8,128)(2,1)} %broadcast_select_fusion), calls=%async_computation.1 | async-start | bytes 8388608 | tf_op jit(solution)/shard_map/all_to_all | solution.py:102
  614.0 121.1 %copy-start.3 = (s32[128,2]{1,0:T(8,128)S(1)}, s32[128,2]{1,0:T(8,128)}, u32[]{:S(2)}) copy-start(s32[128,2]{1,0:T(8,128)} %get-tuple-element.150) | copy-start | bytes 3076
  614.0 121.3 %all-to-all-start.2 = ((f32[128,2,2,32,128]{4,3,2,1,0:T(8,128)}), f32[128,2,2,32,128]{4,3,2,1,0:T(8,128)}, u32[]{:S(2)}, u32[]{:S(2)}) async-start(f32[128,2,2,32,128]{4,3,2,1,0:T(8,128)} %bitcast.270), calls=%async_computation.2 | async-start | bytes 16777216 | tf_op jit(solution)/shard_map/all_to_all | solution.py:130
  753.7 9.4 %copy-start.1 = (bf16[64,2,32,128]{3,2,1,0:T(8,128)(2,1)S(1)}, bf16[64,2,32,128]{3,2,1,0:T(8,128)(2,1)}, u32[]{:S(2)}) copy-start(bf16[64,2,32,128]{3,2,1,0:T(8,128)(2,1)} %param.16) | copy-start | bytes 3145732
where the time goes:
time: 771 us; the launch traced here: 763 us
  other arithmetic  241 us (31%)
  matrix products  182 us (24%)
  local copies, waits for them, and re-layouts  141 us (18%)
  blocking collectives  134 us (17%)
  waiting for transfers between devices  48.8 us (6%)
  starting transfers between devices  11.3 us (1%)
    cos x16, other arithmetic, phasors(): return (jnp.cos(angles), jnp.sin(angles))  117 us
    psum x4, blocking collectives, by_axis(): return functools.reduce(lax.psum, axes, shard)  113 us
    dot_general x96, matrix products, complex_product(): jnp.einsum(form_text, left_side[:, 1], right_side[:, 0], preferred_elemen...  63.1 us
    all_to_all x1, waiting for transfers between devices, shards(): lax.all_to_all(chosen, FACET_VIS, split_axis=0, concat_axis=0, tiled=True)  48.8 us
    dynamic_update_slice x32, other arithmetic, shards(): lax.map(process, (split_blocks(tile_rows), split_blocks(kernels), split_b...  39.7 us
    dot_general x96, matrix products, complex_product(): jnp.einsum(form_text, left_side[:, 1], right_side[:, 1], preferred_elemen...  38 us
    dot_general x96, matrix products, complex_product(): jnp.einsum(form_text, left_side[:, 0], right_side[:, 0], preferred_elemen...  37 us
    dot_general x96, matrix products, complex_product(): jnp.einsum(form_text, left_side[:, 0], right_side[:, 1], preferred_elemen...  36.6 us
  transfers between devices with their start and end apart: 2, of which 1 were waited for; matrix products, arithmetic and copies ran while one was open for 1% of the time, Pallas kernels for 0%

commit v1 on v0

v1 whole, which is shorter than its diff:
```python
import jax
import jax.numpy as jnp
import numpy as np
from jax import lax
from jax.experimental import pallas as pl
from jax.experimental.pallas import tpu as pltpu
from jax.sharding import PartitionSpec as P

AXES = ("facet", "vis")
CAP = 2

BF = jnp.bfloat16
F32 = jnp.float32
STEP = 8
CHUNK = 256


def even_fit(func, terms):
    nodes = np.cos(np.pi * (np.arange(200) + 0.5) / 200) * 0.25
    squares = (nodes + 0.25) / 2
    powers = squares[:, None] ** np.arange(terms)[None, :]
    scale = powers.max(axis=0)
    solved = np.linalg.lstsq(powers / scale, func(np.sqrt(squares)), rcond=None)[0]
    return [float(value) for value in solved / scale]


COS_TERMS = even_fit(lambda t: np.cos(np.pi * t), 7)
SIN_TERMS = even_fit(lambda t: np.sin(np.pi * t) / t, 6)


def half_turn(t):
    square = t * t
    cosine = jnp.full_like(t, COS_TERMS[-1])
    for term in COS_TERMS[-2::-1]:
        cosine = cosine * square + term
    sine = jnp.full_like(t, SIN_TERMS[-1])
    for term in SIN_TERMS[-2::-1]:
        sine = sine * square + term
    return cosine, sine * t


def nt_dot(left, right):
    return lax.dot_general(left, right, (((1,), (1,)), ((), ())), preferred_element_type=F32)


def tn_dot(left, right):
    return lax.dot_general(left, right, (((0,), (0,)), ((), ())), preferred_element_type=F32)


def nn_dot(left, right):
    return jnp.dot(left, right, preferred_element_type=F32)


def lay(table, row, pitch, value):
    for t in range(value.shape[1] // 128):
        table[t, pl.ds(row, STEP, stride=pitch), :] = value[:, 128 * t:128 * t + 128]


def rows_of(table, first, count, start, out_rows):
    pieces = [
        jnp.broadcast_to(table[start // 128 + t, first:first + count, :], (out_rows, 128))
        for t in range(CHUNK // 128)
    ]
    return jnp.concatenate(pieces, axis=1)


def split(value):
    top = value.astype(BF)
    return top, (value - top.astype(F32)).astype(BF)


def tables(uv_ref, u_tab, v_tab, width):
    scale = -1.0 / width
    a_one, b_one = half_turn(uv_ref[:, 0, :] * scale)
    c_one, d_one = half_turn(uv_ref[:, 1, :] * scale)
    phase_r = a_one * c_one - b_one * d_one
    phase_i = -a_one * d_one - b_one * c_one
    half = width // 2
    twice = 4.0 * a_one * a_one - 2.0
    before, now = a_one, a_one
    before_s, now_s = -b_one, b_one
    for j in range(half):
        lay(u_tab, j, width, now)
        lay(u_tab, half + j, width, now_s)
        before, now = now, twice * now - before
        before_s, now_s = now_s, twice * now_s - before_s

    def put(row, value):
        lay(v_tab, row, 16, value)

    c_square = c_one * c_one
    turn = 4.0 * c_square - 2.0
    put(0, c_one)
    put(2, d_one)
    put(1, turn * c_one - c_one)
    put(3, turn * d_one + d_one)
    r_one, i_one = 2.0 * c_square - 1.0, 2.0 * c_one * d_one
    r_two, i_two = 2.0 * r_one * r_one - 1.0, 2.0 * r_one * i_one
    turn = 8.0 * r_two * r_two - 4.0
    turn = 0.5 * turn
    before, now = r_two, r_two
    before_s, now_s = -i_two, i_two
    for n in range(4):
        put(4 + n, now)
        put(8 + n, now_s)
        before, now = now, turn * now - before
        before_s, now_s = now_s, turn * now_s - before_s
    put(12, phase_r)
    put(13, phase_i)


def swap_parts(value):
    return jnp.concatenate([value[4:8], value[0:4]], axis=0)


def block_kernel(pos_ref, plane_ref, obs_ref, uv_ref, wgt_ref, tile_ref, left_ref, leftt_ref, right_ref,
                 res_ref, out_ref, u_tab, v_tab, prod, grown, coef, vis):
    width = 32
    step = pl.program_id(0)
    tables(uv_ref, u_tab, v_tab, width)
    sign = jnp.where(lax.broadcasted_iota(jnp.int32, (8, CHUNK), 0) < 4, -1.0, 1.0).astype(F32)
    for b in range(STEP):
        index = step * STEP + b
        plane = plane_ref[index]
        tile = tile_ref[pos_ref[index]].reshape(64, 128)
        left = nn_dot(left_ref[plane], tile)
        r_up, r_lo, i_up, i_lo = left[0:16], left[16:32], left[32:48], left[48:64]
        left = jnp.concatenate(
            [
                jnp.concatenate([r_up + r_lo, i_lo - i_up], axis=0),
                jnp.concatenate([i_up + i_lo, r_up - r_lo], axis=0),
            ],
            axis=1,
        )
        top, rest = split(left)
        both = jnp.concatenate([top, rest], axis=0)
        for r in range(4):
            found = nn_dot(both, right_ref[plane, r])
            found = found[:32] + found[32:] + nn_dot(top, right_ref[plane, 4 + r])
            coef[b, 32 * r:32 * r + 32, :] = found.astype(BF)
    for b in range(STEP):
        for start in range(0, 1024, CHUNK):
            lanes = slice(start, start + CHUNK)
            table = rows_of(u_tab, width * b, width, start, width)
            for r in range(4):
                row = rows_of(v_tab, 16 * b + r, 1, start, width)
                prod[b, width * r:width * r + width, lanes] = (table * row).astype(BF)
        spread_rows = coef[b]
        for start in range(0, 1024, CHUNK):
            lanes = slice(start, start + CHUNK)
            spread = tn_dot(spread_rows, prod[b, :, lanes])

            def row_of(r):
                return rows_of(v_tab, 16 * b + r, 1, start, 8)

            total = spread[0:8] * row_of(4)
            for g in range(1, 8):
                total = total + spread[8 * g:8 * g + 8] * row_of(4 + g)
            phase_r, phase_i = row_of(12), row_of(13) * sign
            total = (total * phase_r + swap_parts(total) * phase_i) * (1.0 / width)
            seen = jnp.concatenate([obs_ref[b, 0, :, lanes], obs_ref[b, 1, :, lanes]], axis=0)
            resid = seen - total
            res_ref[b, 0, :, lanes] = resid[0:4]
            res_ref[b, 1, :, lanes] = resid[4:8]
            scaled = resid * (jnp.broadcast_to(wgt_ref[b:b + 1, lanes], (8, CHUNK)) * (1.0 / width))
            turned = scaled * phase_r - swap_parts(scaled) * phase_i
            for g in range(0, 8, 2):
                pair = jnp.concatenate([turned * row_of(4 + g), turned * row_of(5 + g)], axis=0)
                vis[b, 8 * g:8 * g + 16, lanes] = pair.astype(BF)
        grown[b] = nt_dot(prod[b], vis[b])
    for b in range(STEP):
        index = step * STEP + b
        plane = plane_ref[index]
        back = None
        for r in range(4):
            top, rest = split(grown[b, 32 * r:32 * r + 32, :])
            both = jnp.concatenate([top, rest], axis=0)
            found = nt_dot(both, right_ref[plane, r])
            found = found[:32] + found[32:] + nt_dot(top, right_ref[plane, 4 + r])
            back = found if back is None else back + found
        a_r, b_r, a_i, b_i = back[:16, :128], back[16:, :128], back[:16, 128:], back[16:, 128:]
        back = jnp.concatenate([a_r + b_i, a_r - b_i, a_i - b_r, a_i + b_r], axis=0)
        top, rest = split(back)
        contrib = nn_dot(leftt_ref[plane], jnp.concatenate([top, rest], axis=1))
        contrib = contrib[:, :128] + contrib[:, 128:]
        out_ref[pos_ref[index]] = contrib.astype(BF).reshape(2, 32, 128)


def plane_matrices(w_kernels):
    planes, _, width, _ = w_kernels.shape
    half = width // 2
    turned = jnp.concatenate([w_kernels[:, :, half:], w_kernels[:, :, half - 1::-1]], axis=2)
    kr, ki = turned[:, 0], turned[:, 1]
    left = jnp.concatenate([jnp.concatenate([kr, -ki], axis=2), jnp.concatenate([ki, kr], axis=2)], axis=1)
    mix = np.zeros((4, 8, width), np.complex64)
    for r in range(4):
        for g in range(8):
            for s1 in (1, -1):
                for s3 in (1, -1):
                    i, n = r % 2, g % 4
                    m1 = 4 + n if s1 > 0 else 3 - n
                    m2 = 2 + i if s3 > 0 else 1 - i
                    mix[r, g, 4 * m1 + m2] = (1j * s3 if r >= 2 else 1) * (1j * s1 if g >= 4 else 1)
    spread = np.zeros((2, width, 4, 2, 8, 2, 4), np.float32)
    for into in range(2):
        for outof in range(2):
            for src in range(2):
                unit = 1j if src else 1
                factor = mix * unit
                if into == 0 and outof == 0:
                    value = factor.real
                elif into == 0 and outof == 1:
                    value = factor.imag
                elif into == 1 and outof == 0:
                    value = -factor.imag
                else:
                    value = factor.real
                spread[src, :, :, into, :, outof, :] = value.transpose(2, 0, 1)[:, :, :, None]
    spread = spread.reshape(2, width, 4 * 2 * 64)
    grid = jnp.einsum("zcmk,cmq->zkq", w_kernels, jnp.asarray(spread, BF), preferred_element_type=F32)
    top = lax.reduce_precision(grid, 8, 7)
    grid = jnp.stack([top.astype(BF), (grid - top).astype(BF)], axis=1).reshape(planes, 2, width, 4, 2, 64).transpose(0, 1, 3, 4, 2, 5)
    grid = grid.reshape(planes, 8, 2, width, 64)
    pol = np.arange(64) % 4
    mask = (pol[None, :] == np.arange(4)[:, None])[None, None, None, :, None, :]
    right = jnp.where(jnp.asarray(mask), grid[:, :, :, None, :, :], jnp.zeros((), BF))
    right = right.reshape(planes, 8, 256, 64)
    return left, left.transpose(0, 2, 1), right


def degrid_grid(position, w_plane, vis_obs, uv_coords, vis_weight, arrived, left, leftt, right):
    blocks = vis_obs.shape[0]
    grid = blocks // STEP
    whole = lambda *shape: pl.BlockSpec(shape, lambda i, *_: (0,) * len(shape), pipeline_mode=pl.Buffered(1))
    return pl.pallas_call(
        block_kernel,
        grid_spec=pltpu.PrefetchScalarGridSpec(
            num_scalar_prefetch=2,
            grid=(grid,),
            in_specs=[
                pl.BlockSpec((STEP, 2, 4, 1024), lambda i, *_: (i, 0, 0, 0)),
                pl.BlockSpec((STEP, 2, 1024), lambda i, *_: (i, 0, 0)),
                pl.BlockSpec((STEP, 1024), lambda i, *_: (i, 0)),
                whole(*arrived.shape),
                whole(*left.shape),
                whole(*leftt.shape),
                whole(*right.shape),
            ],
            out_specs=[
                pl.BlockSpec((STEP, 2, 4, 1024), lambda i, *_: (i, 0, 0, 0)),
                whole(*arrived.shape),
            ],
            scratch_shapes=[
                pltpu.VMEM((8, STEP * 32, 128), F32),
                pltpu.VMEM((8, STEP * 16, 128), F32),
                pltpu.VMEM((STEP, 128, 1024), BF),
                pltpu.VMEM((STEP, 128, 64), F32),
                pltpu.VMEM((STEP, 128, 64), BF),
                pltpu.VMEM((STEP, 64, 1024), BF),
            ],
        ),
        out_shape=[
            jax.ShapeDtypeStruct(vis_obs.shape, F32),
            jax.ShapeDtypeStruct(arrived.shape, BF),
        ],
        compiler_params=pltpu.CompilerParams(vmem_limit_bytes=60 << 20),
        name="degrid_grid",
    )(position, w_plane, vis_obs, uv_coords, vis_weight, arrived, left, leftt, right)


def sum_kernel(slot_ref, scale_ref, part_ref, out_ref, total):
    step = pl.program_id(0)
    count = part_ref.shape[0]

    @pl.when(step == 0)
    def _():
        total[...] = jnp.zeros_like(total)

    def add(i, carry):
        slot = slot_ref[step * count + i]
        total[slot] = total[slot] + part_ref[i].astype(F32)
        return carry

    lax.fori_loop(0, count, add, 0, unroll=4)

    @pl.when(step == pl.num_programs(0) - 1)
    def _():
        out_ref[...] = total[: out_ref.shape[0]] * scale_ref[0]


def sum_slots(slots, scale, parts, owned):
    count = parts.shape[0] // 8
    shape = parts.shape[1:]
    return pl.pallas_call(
        sum_kernel,
        grid_spec=pltpu.PrefetchScalarGridSpec(
            num_scalar_prefetch=2,
            grid=(8,),
            in_specs=[pl.BlockSpec((count,) + shape, lambda i, *_: (i, 0, 0, 0))],
            out_specs=pl.BlockSpec((owned,) + shape, lambda i, *_: (0, 0, 0, 0)),
            scratch_shapes=[pltpu.VMEM((owned + 1,) + shape, F32)],
        ),
        out_shape=jax.ShapeDtypeStruct((owned,) + shape, F32),
        compiler_params=pltpu.CompilerParams(vmem_limit_bytes=32 << 20),
        name="sum_slots",
    )(slots, scale, parts)


def shards(vis_obs, uv_coords, vis_weight, block_group, tile_slot, w_plane, model_tiles, w_kernels):
    blocks, nvis = vis_weight.shape
    groups = lax.axis_size(AXES)
    owned = model_tiles.shape[0]
    tile_shape = model_tiles.shape[1:]
    target = block_group[:, 0]
    same = target[:, None] == target[None, :]
    earlier = np.arange(blocks)[:, None] > np.arange(blocks)[None, :]
    rank = jnp.sum(same & earlier, axis=1, dtype=jnp.int32)
    position = target * CAP + rank
    wanted = jnp.max(
        jnp.where(
            position[:, None] == jnp.arange(groups * CAP, dtype=jnp.int32)[None, :], tile_slot[:, None], -1
        ),
        axis=0,
    )
    message = jnp.concatenate(
        [wanted.astype(F32).reshape(groups, CAP), jnp.full((groups, 1), jnp.sum(vis_weight))], axis=1
    )
    message = lax.all_to_all(message, AXES, split_axis=0, concat_axis=0, tiled=True)
    requested = message[:, :CAP].astype(jnp.int32).reshape(-1)
    scale = (blocks * groups * nvis) / jnp.sum(message[:, CAP])
    chosen = jnp.take(model_tiles, jnp.maximum(requested, 0), axis=0, mode="clip")
    chosen = chosen.reshape((groups, CAP) + tile_shape)
    arrived = lax.all_to_all(chosen, AXES, split_axis=0, concat_axis=0, tiled=True)
    arrived = arrived.reshape((groups * CAP,) + tile_shape)
    left, leftt, right = plane_matrices(w_kernels)
    residual, outgoing = degrid_grid(
        position, w_plane, vis_obs, uv_coords, vis_weight, arrived, left, leftt, right
    )
    outgoing = outgoing.reshape((groups, CAP) + tile_shape)
    returned = lax.all_to_all(outgoing, AXES, split_axis=0, concat_axis=0, tiled=True)
    returned = returned.reshape((groups * CAP,) + tile_shape)
    slots = jnp.where(requested < 0, owned, requested)
    return residual, sum_slots(slots, scale.reshape(1), returned, owned)


def solution(mesh):
    return jax.shard_map(
        shards,
        mesh=mesh,
        in_specs=(
            P(AXES, None, None, None),
            P(AXES, None, None),
            P(AXES, None),
            P(AXES, None),
            P(AXES),
            P(AXES),
            P(AXES, None, None, None),
            P(),
        ),
        out_specs=(P(AXES, None, None, None), P(AXES, None, None, None)),
        check_vma=False,
    )
```

time: 771 us -> 289 us (0.37)
  other arithmetic: 241 us -> 13.9 us
  matrix products: 182 us -> 2.85 us
  Pallas kernels: 0 us -> 144 us
  local copies, waits for them, and re-layouts: 141 us -> 18.7 us
  blocking collectives: 134 us -> 20.9 us
  waiting for transfers between devices: 48.8 us -> 75.1 us
    dot_general x385 -> x1, matrix products: 182 us -> 2.85 us  [plane_matrices(): jnp.einsum('zcmk,cmq->zkq', w_kernels, jnp.asarray(spread, BF), preferred...]
    pallas_call x0 -> x2, Pallas kernels: none -> 144 us  [the longest x1 137 us: degrid_grid(): pl.pallas_call(block_kernel, grid_spec=pltpu.PrefetchScalarGridSpec(num_s...]
    cos x16 -> x0, other arithmetic: 117 us -> none  [phasors(): return (jnp.cos(angles), jnp.sin(angles))]
    psum x4 -> x0, blocking collectives: 113 us -> none  [by_axis(): return functools.reduce(lax.psum, axes, shard)]
    squeeze x144 -> x0, local copies, waits for them, and re-layouts: 47 us -> none  [the longest x32 29.4 us: shards(): lax.map(process, (split_blocks(tile_rows), split_blocks(kernels), split_b...]
    dynamic_update_slice x32 -> x0, other arithmetic: 39.7 us -> none  [shards(): lax.map(process, (split_blocks(tile_rows), split_blocks(kernels), split_b...]
    all_to_all x2, waiting for transfers between devices: 48.8 us -> 75.1 us  [the longest x1 50 us: shards(): lax.all_to_all(outgoing, AXES, split_axis=0, concat_axis=0, tiled=True)]
    slice x16 -> x0, other arithmetic: 21 us -> none  [complex_product(): right_side[:, 0]]
  transfers between devices with their start and end apart: 2 -> 2, of which waited for: 1 -> 2; matrix products, arithmetic and copies ran while one was open for 1% -> 9% of each run, Pallas kernels for 0% -> 0%
where the time goes in v1:
time: 289 us; the launch traced here: 288 us
  Pallas kernels  144 us (50%)
  waiting for transfers between devices  75.1 us (26%)
  blocking collectives  20.9 us (7%)
  local copies, waits for them, and re-layouts  18.7 us (6%)
  other arithmetic  13.9 us (5%)
  starting transfers between devices  11.3 us (4%)
    pallas_call x1, Pallas kernels, degrid_grid(): pl.pallas_call(block_kernel, grid_spec=pltpu.PrefetchScalarGridSpec(num_s...  137 us
    all_to_all x1, waiting for transfers between devices, shards(): lax.all_to_all(outgoing, AXES, split_axis=0, concat_axis=0, tiled=True)  50 us
    all_to_all x1, waiting for transfers between devices, shards(): lax.all_to_all(chosen, AXES, split_axis=0, concat_axis=0, tiled=True)  25.1 us
    all_to_all x1, blocking collectives, shards(): lax.all_to_all(message, AXES, split_axis=0, concat_axis=0, tiled=True)  20.9 us
    another operation x4, local copies, waits for them, and re-layouts, plane_matrices(): jnp.stack([top.astype(BF), (grid - top).astype(BF)], axis=1)  11.5 us
    pallas_call x1, Pallas kernels, sum_slots(): pl.pallas_call(sum_kernel, grid_spec=pltpu.PrefetchScalarGridSpec(num_sca...  7.33 us
    select_n x1, other arithmetic, plane_matrices(): jnp.where(jnp.asarray(mask), grid[:, :, :, None, :, :], jnp.zeros((), BF))  6 us
  transfers between devices with their start and end apart: 2, of which 2 were waited for; matrix products, arithmetic and copies ran while one was open for 9% of the time, Pallas kernels for 0%

profile of v1, /device:TPU:1, one launch (start us, length us, event | category | flops | bytes accessed | tf_op | source)
XLA Modules:
  0.0 288.5 jit_solution(6548777631656604003)
XLA Ops:
  0.6 1.0 convert_reduce_fusion
  1.6 0.7 fusion.4
  2.3 0.8 select_reduce_fusion
  3.2 1.8 reduce_sum.31
  5.0 0.7 concatenate.16
  5.7 20.9 %all_to_all.22 = f32[128,1,3]{2,1,0:T(1,128)S(1)} all-to-all(f32[128,1,3]{2,1,0:T(1,128)S(1)} %bitcast.45), channel_id=1, replica_groups=mesh['facet'=8,'vis'=16] {'facet','vis'}, dimensions={0} | all-to-all | bytes 3072 | tf_op jit(solution)/shard_map/all_to_all | solution.py:328
  26.8 3.1 %gather_fusion = bf16[256,2,32,128]{3,2,1,0:T(8,128)(2,1)} fusion(bf16[64,2,32,128]{3,2,1,0:T(8,128)(2,1)S(1)} %copy-done, s32[1024]{0:T(1024)S(1)} %pad_clamp_fusion), kind=kCustom, calls=%fused_computation | custom fusion | bytes 8389632 | tf_op jit(solution)/shard_map/jit(_take)/gather | solution.py:331
  29.9 5.7 %all-to-all-start.1 = ((bf16[128,2,2,32,128]{4,3,2,1,0:T(8,128)(2,1)}), bf16[128,2,2,32,128]{4,3,2,1,0:T(8,128)(2,1)}, u32[]{:S(2)}, u32[]{:S(2)}) async-start(bf16[128,2,2,32,128]{4,3,2,1,0:T(8,128)(2,1)} %bitcast.40), calls=%async_computation.1 | async-start | bytes 8388608 | tf_op jit(solution)/shard_map/all_to_all | solution.py:333
  37.2 1.0 copy.36.left_ref
  38.3 2.9 reduce-precision_convert_fusion
  41.2 4.4 %stack.9 = bf16[32,1,32,4,2,64]{5,4,3,2,0,1:T(2,128)(2,1)S(1)} reshape(bf16[32,32,512]{2,1,0:T(8,128)(2,1)} %get-tuple-element.8) | data formatting | bytes 2097152 | tf_op jit(solution)/shard_map/stack | solution.py:222
  45.6 2.0 copy.34
  47.6 4.4 %stack.10 = bf16[32,1,32,4,2,64]{5,4,3,2,0,1:T(2,128)(2,1)S(1)} reshape(bf16[32,32,512]{2,1,0:T(8,128)(2,1)} %get-tuple-element.9) | data formatting | bytes 2097152 | tf_op jit(solution)/shard_map/stack | solution.py:222
  52.0 0.7 copy.35
  52.7 0.9 copy-done.1
  53.6 0.8 pad_maximum_fusion
  54.5 6.0 %bitcast_select_fusion.right_ref = bf16[32,8,256,64]{3,2,1,0:T(8,128)(2,1)} fusion(pred[256,64]{1,0:T(8,128)(4,1)S(1)} %bitcast.46, bf16[32,8,2,32,64]{4,3,2,1,0:T(8,128)(2,1)S(1)} %bitcast.39), kind=kLoop, calls=%fused_computation.1 | loop fusion | flops 4194304 | bytes 10502144 | tf_op jit(solution)/shard_map/jit(_where)/select_n | solution.py:226
  60.5 1.1 fusion.10.leftt_ref
  62.1 25.1 %all-to-all-done.1 = bf16[128,2,2,32,128]{4,3,2,1,0:T(8,128)(2,1)} async-done(((bf16[128,2,2,32,128]{4,3,2,1,0:T(8,128)(2,1)}), bf16[128,2,2,32,128]{4,3,2,1,0:T(8,128)(2,1)}, u32[]{:S(2)}, u32[]{:S(2)}) %all-to-all-start.1) | async-done | bytes 4194336 | tf_op jit(solution)/shard_map/all_to_all | solution.py:333
  87.2 136.8 %degrid_grid.1 = (f32[128,2,4,1024]{3,2,1,0:T(4,128)}, bf16[256,2,32,128]{3,2,1,0:T(8,128)(2,1)}) custom-call(s32[128]{0:T(128)} %multiply_add_fusion.pos_ref, s32[128]{0:T(128)} %plane_ref.1, f32[128,2,4,1024]{3,2,1,0:T(4,128)} %obs_ref.1, f32[128,2,1024]{2,1,0:T(2,128)} %uv_ref.1, f32[128,1024]{1,0:T(8,128)} %wgt_ref.1, ...), custom_call_target="tpu_custom_call" | custom-call | tf_op jit(solution)/shard_map/degrid_grid/pallas_call | solution.py:235
  224.0 5.6 %all-to-all-start.2 = ((bf16[128,2,2,32,128]{4,3,2,1,0:T(8,128)(2,1)}), bf16[128,2,2,32,128]{4,3,2,1,0:T(8,128)(2,1)}, u32[]{:S(2)}, u32[]{:S(2)}) async-start(bf16[128,2,2,32,128]{4,3,2,1,0:T(8,128)(2,1)} %bitcast.41), calls=%async_computation.2 | async-start | bytes 8388608 | tf_op jit(solution)/shard_map/all_to_all | solution.py:340
  229.8 0.7 slice_reduce_fusion
  231.2 50.0 %all-to-all-done.2 = bf16[128,2,2,32,128]{4,3,2,1,0:T(8,128)(2,1)} async-done(((bf16[128,2,2,32,128]{4,3,2,1,0:T(8,128)(2,1)}), bf16[128,2,2,32,128]{4,3,2,1,0:T(8,128)(2,1)}, u32[]{:S(2)}, u32[]{:S(2)}) %all-to-all-start.2) | async-done | bytes 4194336 | tf_op jit(solution)/shard_map/all_to_all | solution.py:340
  281.1 7.3 %sum_slots.1 = f32[64,2,32,128]{3,2,1,0:T(8,128)} custom-call(s32[256]{0:T(256)S(1)} %compare_select_fusion.slot_ref, f32[1]{0:T(128)} %bitcast.20.scale_ref, bf16[256,2,32,128]{3,2,1,0:T(8,128)(2,1)} %bitcast.22.part_ref), custom_call_target="tpu_custom_call" | custom-call | tf_op jit(solution)/shard_map/sum_slots/pallas_call | solution.py:294
  (36 shorter events, 2.6 us)
Async XLA Ops:
  0.6 26.1 %copy-start = (bf16[64,2,32,128]{3,2,1,0:T(8,128)(2,1)S(1)}, bf16[64,2,32,128]{3,2,1,0:T(8,128)(2,1)}, u32[]{:S(2)}) copy-start(bf16[64,2,32,128]{3,2,1,0:T(8,128)(2,1)} %param.17) | copy-start | bytes 3145732
  29.9 5.7 %copy-start.6 = (bf16[32,2,32,32]{3,2,1,0:T(8,128)(2,1)S(1)}, bf16[32,2,32,32]{3,2,1,0:T(8,128)(2,1)}, u32[]{:S(2)}) copy-start(bf16[32,2,32,32]{3,2,1,0:T(8,128)(2,1)} %param.18) | copy-start | bytes 393220
  29.9 57.3 %all-to-all-start.1 = ((bf16[128,2,2,32,128]{4,3,2,1,0:T(8,128)(2,1)}), bf16[128,2,2,32,128]{4,3,2,1,0:T(8,128)(2,1)}, u32[]{:S(2)}, u32[]{:S(2)}) async-start(bf16[128,2,2,32,128]{4,3,2,1,0:T(8,128)(2,1)} %bitcast.40), calls=%async_computation.1 | async-start | bytes 8388608 | tf_op jit(solution)/shard_map/all_to_all | solution.py:333
  35.6 2.7 copy-start.7
  36.9 4.2 %copy-start.2 = (bf16[32,32,32]{1,2,0:T(8,128)(2,1)}, bf16[32,32,32]{1,2,0:T(8,128)(2,1)S(1)}, u32[]{:S(2)}) copy-start(bf16[32,32,32]{1,2,0:T(8,128)(2,1)S(1)} %get-tuple-element.6) | copy-start | bytes 196612
  37.0 4.2 %copy-start.4 = (bf16[32,32,32]{1,2,0:T(8,128)(2,1)}, bf16[32,32,32]{1,2,0:T(8,128)(2,1)S(1)}, u32[]{:S(2)}) copy-start(bf16[32,32,32]{1,2,0:T(8,128)(2,1)S(1)} %get-tuple-element.7) | copy-start | bytes 196612
  52.0 1.6 copy-start.1
  53.6 0.8 copy-start.9
  54.5 6.0 %copy-start.3 = (bf16[32,32,32]{1,2,0:T(8,128)(2,1)S(1)}, bf16[32,32,32]{1,2,0:T(8,128)(2,1)}, u32[]{:S(2)}) copy-start(bf16[32,32,32]{1,2,0:T(8,128)(2,1)} %copy-done.2) | copy-start | bytes 196612
  54.5 6.0 %copy-start.5 = (bf16[32,32,32]{1,2,0:T(8,128)(2,1)S(1)}, bf16[32,32,32]{1,2,0:T(8,128)(2,1)}, u32[]{:S(2)}) copy-start(bf16[32,32,32]{1,2,0:T(8,128)(2,1)} %copy-done.4) | copy-start | bytes 196612
  54.5 7.1 %copy-start.8 = (s32[128,1]{0,1:T(1,128)S(1)}, s32[128,1]{0,1:T(1,128)}, u32[]{:S(2)}) copy-start(s32[128,1]{0,1:T(1,128)} %param.14) | copy-start | bytes 1540
  224.0 57.1 %all-to-all-start.2 = ((bf16[128,2,2,32,128]{4,3,2,1,0:T(8,128)(2,1)}), bf16[128,2,2,32,128]{4,3,2,1,0:T(8,128)(2,1)}, u32[]{:S(2)}, u32[]{:S(2)}) async-start(bf16[128,2,2,32,128]{4,3,2,1,0:T(8,128)(2,1)} %bitcast.41), calls=%async_computation.2 | async-start | bytes 8388608 | tf_op jit(solution)/shard_map/all_to_all | solution.py:340

commit v2 on v1

--- a/solution.py
+++ b/solution.py
@@ -51,14 +51,20 @@
     return jnp.dot(left, right, preferred_element_type=F32)
 
 
-def lay(table, row, pitch, value):
+def lay(table, row, value):
     for t in range(value.shape[1] // 128):
-        table[t, pl.ds(row, STEP, stride=pitch), :] = value[:, 128 * t:128 * t + 128]
-
-
-def rows_of(table, first, count, start, out_rows):
+        table[t, STEP * row:STEP * row + STEP, :] = value[:, 128 * t:128 * t + 128]
+
+
+def column(table, b, start):
+    pieces = [table[start // 128 + t, pl.ds(b, 32, stride=STEP), :] for t in range(CHUNK // 128)]
+    return jnp.concatenate(pieces, axis=1)
+
+
+def row_of(table, row, b, start, count):
+    first = STEP * row + b
     pieces = [
-        jnp.broadcast_to(table[start // 128 + t, first:first + count, :], (out_rows, 128))
+        jnp.broadcast_to(table[start // 128 + t, first:first + 1, :], (count, 128))
         for t in range(CHUNK // 128)
     ]
     return jnp.concatenate(pieces, axis=1)
@@ -71,22 +77,22 @@
 
 def tables(uv_ref, u_tab, v_tab, width):
     scale = -1.0 / width
-    a_one, b_one = half_turn(uv_ref[:, 0, :] * scale)
-    c_one, d_one = half_turn(uv_ref[:, 1, :] * scale)
-    phase_r = a_one * c_one - b_one * d_one
+    a_one, b_one = half_turn(uv_ref[0] * scale)
+    c_one, d_one = half_turn(uv_ref[1] * scale)
+    phase_r = (a_one * c_one - b_one * d_one)
     phase_i = -a_one * d_one - b_one * c_one
     half = width // 2
     twice = 4.0 * a_one * a_one - 2.0
     before, now = a_one, a_one
     before_s, now_s = -b_one, b_one
     for j in range(half):
-        lay(u_tab, j, width, now)
-        lay(u_tab, half + j, width, now_s)
+        lay(u_tab, j, now)
+        lay(u_tab, half + j, now_s)
         before, now = now, twice * now - before
         before_s, now_s = now_s, twice * now_s - before_s
 
     def put(row, value):
-        lay(v_tab, row, 16, value)
+        lay(v_tab, row, value)
 
     c_square = c_one * c_one
     turn = 4.0 * c_square - 2.0
@@ -96,8 +102,7 @@
     put(3, turn * d_one + d_one)
     r_one, i_one = 2.0 * c_square - 1.0, 2.0 * c_one * d_one
     r_two, i_two = 2.0 * r_one * r_one - 1.0, 2.0 * r_one * i_one
-    turn = 8.0 * r_two * r_two - 4.0
-    turn = 0.5 * turn
+    turn = 4.0 * r_two * r_two - 2.0
     before, now = r_two, r_two
     before_s, now_s = -i_two, i_two
     for n in range(4):
@@ -110,7 +115,36 @@
 
 
 def swap_parts(value):
-    return jnp.concatenate([value[4:8], value[0:4]], axis=0)
+    return pltpu.roll(value, 4, 0)
+
+
+def forward(b, tile, left_k, right_top, right_rest, coef):
+    left = nn_dot(left_k, tile.reshape(64, 128))
+    r_up, r_lo, i_up, i_lo = left[0:16], left[16:32], left[32:48], left[48:64]
+    left = jnp.concatenate(
+        [
+            jnp.concatenate([r_up + r_lo, i_lo - i_up], axis=0),
+            jnp.concatenate([i_up + i_lo, r_up - r_lo], axis=0),
+        ],
+        axis=1,
+    )
+    top, rest = split(left)
+    found = nn_dot(jnp.concatenate([top, rest], axis=0), right_top)
+    found = found[:32] + found[32:] + nn_dot(top, right_rest)
+    for r in range(4):
+        coef[b, 32 * r:32 * r + 32, :] = found[:, 64 * r:64 * r + 64].astype(BF)
+
+
+def backward(grown, left_k, right_top, right_rest):
+    grown = jnp.concatenate([grown[32 * r:32 * r + 32] for r in range(4)], axis=1)
+    top, rest = split(grown)
+    back = nt_dot(jnp.concatenate([top, rest], axis=0), right_top)
+    back = back[:32] + back[32:] + nt_dot(top, right_rest)
+    a_r, b_r, a_i, b_i = back[:16, :128], back[16:, :128], back[:16, 128:], back[16:, 128:]
+    back = jnp.concatenate([a_r + b_i, a_r - b_i, a_i - b_r, a_i + b_r], axis=0)
+    top, rest = split(back)
+    contrib = nn_dot(left_k, jnp.concatenate([top, rest], axis=1))
+    return (contrib[:, :128] + contrib[:, 128:]).astype(BF).reshape(2, 32, 128)
 
 
 def block_kernel(pos_ref, plane_ref, obs_ref, uv_ref, wgt_ref, tile_ref, left_ref, leftt_ref, right_ref,
@@ -119,71 +153,52 @@
     step = pl.program_id(0)
     tables(uv_ref, u_tab, v_tab, width)
     sign = jnp.where(lax.broadcasted_iota(jnp.int32, (8, CHUNK), 0) < 4, -1.0, 1.0).astype(F32)
-    for b in range(STEP):
+
+    def first(b):
         index = step * STEP + b
         plane = plane_ref[index]
-        tile = tile_ref[pos_ref[index]].reshape(64, 128)
-        left = nn_dot(left_ref[plane], tile)
-        r_up, r_lo, i_up, i_lo = left[0:16], left[16:32], left[32:48], left[48:64]
-        left = jnp.concatenate(
-            [
-                jnp.concatenate([r_up + r_lo, i_lo - i_up], axis=0),
-                jnp.concatenate([i_up + i_lo, r_up - r_lo], axis=0),
-            ],
-            axis=1,
-        )
-        top, rest = split(left)
-        both = jnp.concatenate([top, rest], axis=0)
-        for r in range(4):
-            found = nn_dot(both, right_ref[plane, r])
-            found = found[:32] + found[32:] + nn_dot(top, right_ref[plane, 4 + r])
-            coef[b, 32 * r:32 * r + 32, :] = found.astype(BF)
-    for b in range(STEP):
+        forward(b, tile_ref[pos_ref[index]], left_ref[plane], right_ref[plane, 0], right_ref[plane, 1], coef)
+
+    def products(b):
         for start in range(0, 1024, CHUNK):
             lanes = slice(start, start + CHUNK)
-            table = rows_of(u_tab, width * b, width, start, width)
+            table = column(u_tab, b, start)
             for r in range(4):
-                row = rows_of(v_tab, 16 * b + r, 1, start, width)
+                row = row_of(v_tab, r, b, start, width)
                 prod[b, width * r:width * r + width, lanes] = (table * row).astype(BF)
-        spread_rows = coef[b]
+
+    def middle(b):
         for start in range(0, 1024, CHUNK):
             lanes = slice(start, start + CHUNK)
-            spread = tn_dot(spread_rows, prod[b, :, lanes])
-
-            def row_of(r):
-                return rows_of(v_tab, 16 * b + r, 1, start, 8)
-
-            total = spread[0:8] * row_of(4)
+            spread = tn_dot(coef[b], prod[b, :, lanes])
+            rows = [row_of(v_tab, 4 + g, b, start, 8) for g in range(8)]
+            total = spread[0:8] * rows[0]
             for g in range(1, 8):
-                total = total + spread[8 * g:8 * g + 8] * row_of(4 + g)
-            phase_r, phase_i = row_of(12), row_of(13) * sign
-            total = (total * phase_r + swap_parts(total) * phase_i) * (1.0 / width)
-            seen = jnp.concatenate([obs_ref[b, 0, :, lanes], obs_ref[b, 1, :, lanes]], axis=0)
-            resid = seen - total
-            res_ref[b, 0, :, lanes] = resid[0:4]
-            res_ref[b, 1, :, lanes] = resid[4:8]
-            scaled = resid * (jnp.broadcast_to(wgt_ref[b:b + 1, lanes], (8, CHUNK)) * (1.0 / width))
+                total = total + spread[8 * g:8 * g + 8] * rows[g]
+            phase_r, phase_i = row_of(v_tab, 12, b, start, 8), row_of(v_tab, 13, b, start, 8) * sign
+            total = total * phase_r + swap_parts(total) * phase_i
+            resid = obs_ref[b, :, lanes] - total
+            res_ref[b, :, lanes] = resid
+            scaled = resid * jnp.broadcast_to(wgt_ref[b:b + 1, lanes], (8, CHUNK))
             turned = scaled * phase_r - swap_parts(scaled) * phase_i
             for g in range(0, 8, 2):
-                pair = jnp.concatenate([turned * row_of(4 + g), turned * row_of(5 + g)], axis=0)
+                pair = jnp.concatenate([turned * rows[g], turned * rows[g + 1]], axis=0)
                 vis[b, 8 * g:8 * g + 16, lanes] = pair.astype(BF)
         grown[b] = nt_dot(prod[b], vis[b])
-    for b in range(STEP):
+
+    def last(b):
         index = step * STEP + b
         plane = plane_ref[index]
-        back = None
-        for r in range(4):
-            top, rest = split(grown[b, 32 * r:32 * r + 32, :])
-            both = jnp.concatenate([top, rest], axis=0)
-            found = nt_dot(both, right_ref[plane, r])
-            found = found[:32] + found[32:] + nt_dot(top, right_ref[plane, 4 + r])
-            back = found if back is None else back + found
-        a_r, b_r, a_i, b_i = back[:16, :128], back[16:, :128], back[:16, 128:], back[16:, 128:]
-        back = jnp.concatenate([a_r + b_i, a_r - b_i, a_i - b_r, a_i + b_r], axis=0)
-        top, rest = split(back)
-        contrib = nn_dot(leftt_ref[plane], jnp.concatenate([top, rest], axis=1))
-        contrib = contrib[:, :128] + contrib[:, 128:]
-        out_ref[pos_ref[index]] = contrib.astype(BF).reshape(2, 32, 128)
+        out_ref[pos_ref[index]] = backward(grown[b], leftt_ref[plane], right_ref[plane, 0], right_ref[plane, 1])
+
+    for turn in range(STEP + 2):
+        if turn < STEP:
+            first(turn)
+            products(turn)
+        if 0 <= turn - 1 < STEP:
+            middle(turn - 1)
+        if 0 <= turn - 2 < STEP:
+            last(turn - 2)
 
 
 def plane_matrices(w_kernels):
@@ -201,7 +216,7 @@
                     m1 = 4 + n if s1 > 0 else 3 - n
                     m2 = 2 + i if s3 > 0 else 1 - i
                     mix[r, g, 4 * m1 + m2] = (1j * s3 if r >= 2 else 1) * (1j * s1 if g >= 4 else 1)
-    spread = np.zeros((2, width, 4, 2, 8, 2, 4), np.float32)
+    spread = np.zeros((2, width, 2, 4, 8, 2, 4), np.float32)
     for into in range(2):
         for outof in range(2):
             for src in range(2):
@@ -215,31 +230,34 @@
                     value = -factor.imag
                 else:
                     value = factor.real
-                spread[src, :, :, into, :, outof, :] = value.transpose(2, 0, 1)[:, :, :, None]
-    spread = spread.reshape(2, width, 4 * 2 * 64)
+                spread[src, :, into, :, :, outof, :] = value.transpose(2, 0, 1)[:, :, :, None]
+    spread = spread.reshape(2, width, 512)
     grid = jnp.einsum("zcmk,cmq->zkq", w_kernels, jnp.asarray(spread, BF), preferred_element_type=F32)
+    grid = grid * (1.0 / width)
     top = lax.reduce_precision(grid, 8, 7)
-    grid = jnp.stack([top.astype(BF), (grid - top).astype(BF)], axis=1).reshape(planes, 2, width, 4, 2, 64).transpose(0, 1, 3, 4, 2, 5)
-    grid = grid.reshape(planes, 8, 2, width, 64)
-    pol = np.arange(64) % 4
+    grid = jnp.stack([top.astype(BF), (grid - top).astype(BF)], axis=1)
+    grid = grid.reshape(planes, 2, width, 2, 256).transpose(0, 1, 3, 2, 4)
+    pol = np.arange(256) % 4
     mask = (pol[None, :] == np.arange(4)[:, None])[None, None, None, :, None, :]
     right = jnp.where(jnp.asarray(mask), grid[:, :, :, None, :, :], jnp.zeros((), BF))
-    right = right.reshape(planes, 8, 256, 64)
+    right = right.reshape(planes, 2, 256, 256)
     return left, left.transpose(0, 2, 1), right
 
 
 def degrid_grid(position, w_plane, vis_obs, uv_coords, vis_weight, arrived, left, leftt, right):
     blocks = vis_obs.shape[0]
     grid = blocks // STEP
+    vis_obs = vis_obs.reshape(blocks, 8, 1024)
+    uv_coords = uv_coords.transpose(1, 0, 2)
     whole = lambda *shape: pl.BlockSpec(shape, lambda i, *_: (0,) * len(shape), pipeline_mode=pl.Buffered(1))
-    return pl.pallas_call(
+    residual, outgoing = pl.pallas_call(
         block_kernel,
         grid_spec=pltpu.PrefetchScalarGridSpec(
             num_scalar_prefetch=2,
             grid=(grid,),
             in_specs=[
-                pl.BlockSpec((STEP, 2, 4, 1024), lambda i, *_: (i, 0, 0, 0)),
-                pl.BlockSpec((STEP, 2, 1024), lambda i, *_: (i, 0, 0)),
+                pl.BlockSpec((STEP, 8, 1024), lambda i, *_: (i, 0, 0)),
+                pl.BlockSpec((2, STEP, 1024), lambda i, *_: (0, i, 0)),
                 pl.BlockSpec((STEP, 1024), lambda i, *_: (i, 0)),
                 whole(*arrived.shape),
                 whole(*left.shape),
@@ -247,12 +265,12 @@
                 whole(*right.shape),
             ],
             out_specs=[
-                pl.BlockSpec((STEP, 2, 4, 1024), lambda i, *_: (i, 0, 0, 0)),
+                pl.BlockSpec((STEP, 8, 1024), lambda i, *_: (i, 0, 0)),
                 whole(*arrived.shape),
             ],
             scratch_shapes=[
-                pltpu.VMEM((8, STEP * 32, 128), F32),
-                pltpu.VMEM((8, STEP * 16, 128), F32),
+                pltpu.VMEM((8, 32 * STEP, 128), F32),
+                pltpu.VMEM((8, 16 * STEP, 128), F32),
                 pltpu.VMEM((STEP, 128, 1024), BF),
                 pltpu.VMEM((STEP, 128, 64), F32),
                 pltpu.VMEM((STEP, 128, 64), BF),
@@ -266,6 +284,7 @@
         compiler_params=pltpu.CompilerParams(vmem_limit_bytes=60 << 20),
         name="degrid_grid",
     )(position, w_plane, vis_obs, uv_coords, vis_weight, arrived, left, leftt, right)
+    return residual.reshape(blocks, 2, 4, 1024), outgoing
 
 
 def sum_kernel(slot_ref, scale_ref, part_ref, out_ref, total):

time: 289 us -> 221 us (0.76)
  Pallas kernels: 144 us -> 76.4 us
  waiting for transfers between devices: 75.1 us -> 70.6 us
  local copies, waits for them, and re-layouts: 18.7 us -> 22.1 us
    pallas_call x1, Pallas kernels: 137 us -> 69 us  [degrid_grid(): pl.pallas_call(block_kernel, grid_spec=pltpu.PrefetchScalarGridSpec(num_s...]
    reshape x0 -> x2, local copies, waits for them, and re-layouts: none -> 10.4 us  [the longest x1 5.28 us: degrid_grid(): vis_obs = vis_obs.reshape(blocks, 8, 1024)]
    another operation x4 -> x2, local copies, waits for them, and re-layouts: 11.5 us -> 2.45 us  [plane_matrices(): grid = jnp.stack([top.astype(BF), (grid - top).astype(BF)], axis=1)]
    all_to_all x1, waiting for transfers between devices: 50 us -> 44.8 us  [shards(): lax.all_to_all(outgoing, AXES, split_axis=0, concat_axis=0, tiled=True)]
    transpose x0 -> x1, other arithmetic: none -> 4.36 us  [plane_matrices(): grid = grid.reshape(planes, 2, width, 2, 256).transpose(0, 1, 3, 2, 4)]
  transfers between devices with their start and end apart: 2 -> 2, of which waited for: 2 -> 2; matrix products, arithmetic and copies ran while one was open for 9% -> 14% of each run, Pallas kernels for 0% -> 0%
where the time goes in v2:
time: 221 us
  Pallas kernels  76.4 us (35%)
  waiting for transfers between devices  70.6 us (32%)
  local copies, waits for them, and re-layouts  22.1 us (10%)
  blocking collectives  20.9 us (9%)
  other arithmetic  15.3 us (7%)
  starting transfers between devices  11.3 us (5%)
  matrix products  2.51 us (1%)
    pallas_call x1, Pallas kernels, degrid_grid(): pl.pallas_call(block_kernel, grid_spec=pltpu.PrefetchScalarGridSpec(num_s...  69 us
    all_to_all x1, waiting for transfers between devices, shards(): lax.all_to_all(outgoing, AXES, split_axis=0, concat_axis=0, tiled=True)  44.8 us
    all_to_all x1, waiting for transfers between devices, shards(): lax.all_to_all(chosen, AXES, split_axis=0, concat_axis=0, tiled=True)  25.8 us
    all_to_all x1, blocking collectives, shards(): lax.all_to_all(message, AXES, split_axis=0, concat_axis=0, tiled=True)  20.9 us
    pallas_call x1, Pallas kernels, sum_slots(): pl.pallas_call(sum_kernel, grid_spec=pltpu.PrefetchScalarGridSpec(num_sca...  7.35 us
    all_to_all x1, starting transfers between devices, shards(): lax.all_to_all(chosen, AXES, split_axis=0, concat_axis=0, tiled=True)  5.65 us
    all_to_all x1, starting transfers between devices, shards(): lax.all_to_all(outgoing, AXES, split_axis=0, concat_axis=0, tiled=True)  5.6 us
    reshape x1, local copies, waits for them, and re-layouts, degrid_grid(): vis_obs = vis_obs.reshape(blocks, 8, 1024)  5.28 us
  transfers between devices with their start and end apart: 2, of which 2 were waited for; matrix products, arithmetic and copies ran while one was open for 14% of the time, Pallas kernels for 0%

profile of v2, /device:TPU:1, one launch (start us, length us, event | category | flops | bytes accessed | tf_op | source)
XLA Modules:
  0.0 220.6 jit_solution(5772905170755256210)
XLA Ops:
  0.6 1.0 convert_reduce_fusion
  1.6 0.7 fusion.4
  2.3 0.8 select_reduce_fusion
  3.2 1.8 reduce_sum.31
  5.0 0.7 concatenate.16
  5.7 20.9 %all_to_all.22 = f32[128,1,3]{2,1,0:T(1,128)S(1)} all-to-all(f32[128,1,3]{2,1,0:T(1,128)S(1)} %bitcast.52), channel_id=1, replica_groups=mesh['facet'=8,'vis'=16] {'facet','vis'}, dimensions={0} | all-to-all | bytes 3072 | tf_op jit(solution)/shard_map/all_to_all | solution.py:347
  26.8 3.0 %gather_fusion = bf16[256,2,32,128]{3,2,1,0:T(8,128)(2,1)} fusion(bf16[64,2,32,128]{3,2,1,0:T(8,128)(2,1)S(1)} %copy-done, s32[1024]{0:T(1024)S(1)} %pad_clamp_fusion), kind=kCustom, calls=%fused_computation | custom fusion | bytes 8389632 | tf_op jit(solution)/shard_map/jit(_take)/gather | solution.py:350
  29.8 5.7 %all-to-all-start.1 = ((bf16[128,2,2,32,128]{4,3,2,1,0:T(8,128)(2,1)}), bf16[128,2,2,32,128]{4,3,2,1,0:T(8,128)(2,1)}, u32[]{:S(2)}, u32[]{:S(2)}) async-start(bf16[128,2,2,32,128]{4,3,2,1,0:T(8,128)(2,1)} %bitcast.45), calls=%async_computation.1 | async-start | bytes 8388608 | tf_op jit(solution)/shard_map/all_to_all | solution.py:352
  37.2 1.0 copy.38.left_ref
  38.2 2.5 %copy.44 = f32[128,2,1024]{2,0,1:T(8,128)} copy(f32[128,2,1024]{2,1,0:T(2,128)} %param.12) | data formatting | bytes 2097152 | tf_op args[1]
  40.7 2.5 %reduce-precision_convert_fusion = (bf16[32,32,512]{2,1,0:T(8,128)(2,1)}, bf16[32,32,512]{2,1,0:T(8,128)(2,1)S(1)}) fusion(bf16[2,32,512,1]{2,1,0,3:T(8,128)(2,1)S(1)} %copy-done.6, bf16[32,2,32,32]{3,2,1,0:T(8,128)(2,1)} %param.18), kind=kOutput, calls=%fused_computation.3 | convolution fusion | flops 69730304 | bytes 2293760 | tf_op jit(solution)/shard_map/zcmk,cmq->zkq/dot_general | solution.py:235
  43.2 1.3 stack.9
  44.6 1.1 stack.10
  45.7 4.4 %maximum_bitcast_fusion = bf16[32,2,2,32,256]{4,2,3,0,1:T(2,128)(2,1)S(1)} fusion(bf16[32,1,32,2,256]{4,3,2,0,1:T(2,128)(2,1)} %stack.10, bf16[32,1,32,2,256]{4,3,2,0,1:T(2,128)(2,1)S(1)} %stack.9), kind=kLoop, calls=%fused_computation.5 | loop fusion | flops 1048576 | bytes 4194304 | tf_op jit(solution)/shard_map/transpose | solution.py:239
  50.6 5.3 %reshape.57.obs_ref = f32[128,8,1024]{2,1,0:T(8,128)} reshape(f32[128,2,4,1024]{3,2,1,0:T(4,128)} %param.11) | data formatting | bytes 8388608 | tf_op jit(solution)/shard_map/reshape | solution.py:250
  55.9 3.8 %bitcast_select_fusion.right_ref = bf16[32,2,256,256]{3,2,1,0:T(8,128)(2,1)} fusion(pred[256,256]{1,0:T(8,128)(4,1)S(1)} %bitcast.51, bf16[32,2,2,32,256]{4,3,2,1,0:T(8,128)(2,1)S(1)} %copy.37), kind=kLoop, calls=%fused_computation.1 | loop fusion | flops 4194304 | bytes 10551296 | tf_op jit(solution)/shard_map/jit(_where)/select_n | solution.py:242
  59.7 1.1 fusion.10.leftt_ref
  61.3 25.8 %all-to-all-done.1 = bf16[128,2,2,32,128]{4,3,2,1,0:T(8,128)(2,1)} async-done(((bf16[128,2,2,32,128]{4,3,2,1,0:T(8,128)(2,1)}), bf16[128,2,2,32,128]{4,3,2,1,0:T(8,128)(2,1)}, u32[]{:S(2)}, u32[]{:S(2)}) %all-to-all-start.1) | async-done | bytes 4194336 | tf_op jit(solution)/shard_map/all_to_all | solution.py:352
  87.1 69.0 %degrid_grid.1 = (f32[128,8,1024]{2,1,0:T(8,128)}, bf16[256,2,32,128]{3,2,1,0:T(8,128)(2,1)}) custom-call(s32[128]{0:T(128)} %multiply_add_fusion.pos_ref, s32[128]{0:T(128)} %plane_ref.1, f32[128,8,1024]{2,1,0:T(8,128)} %reshape.57.obs_ref, f32[2,128,1024]{2,1,0:T(8,128)} %bitcast.46, f32[128,1024]{1,0:T(8,128)} %wgt_ref.1, ...), custom_call_target="tpu_custom_call" | custom-call | tf_op jit(solution)/shard_map/degrid_grid/pallas_call | solution.py:253
  156.1 5.6 %all-to-all-start.2 = ((bf16[128,2,2,32,128]{4,3,2,1,0:T(8,128)(2,1)}), bf16[128,2,2,32,128]{4,3,2,1,0:T(8,128)(2,1)}, u32[]{:S(2)}, u32[]{:S(2)}) async-start(bf16[128,2,2,32,128]{4,3,2,1,0:T(8,128)(2,1)} %bitcast.47), calls=%async_computation.2 | async-start | bytes 8388608 | tf_op jit(solution)/shard_map/all_to_all | solution.py:359
  161.9 0.7 slice_reduce_fusion
  163.3 5.2 %reshape.60 = f32[128,2,4,1024]{3,2,1,0:T(4,128)} reshape(f32[128,8,1024]{2,1,0:T(8,128)} %get-tuple-element.4) | data formatting | bytes 8388608 | tf_op jit(solution)/shard_map/reshape | solution.py:287
  168.4 44.8 %all-to-all-done.2 = bf16[128,2,2,32,128]{4,3,2,1,0:T(8,128)(2,1)} async-done(((bf16[128,2,2,32,128]{4,3,2,1,0:T(8,128)(2,1)}), bf16[128,2,2,32,128]{4,3,2,1,0:T(8,128)(2,1)}, u32[]{:S(2)}, u32[]{:S(2)}) %all-to-all-start.2) | async-done | bytes 4194336 | tf_op jit(solution)/shard_map/all_to_all | solution.py:359
  213.2 7.3 %sum_slots.1 = f32[64,2,32,128]{3,2,1,0:T(8,128)} custom-call(s32[256]{0:T(256)S(1)} %compare_select_fusion.slot_ref, f32[1]{0:T(128)} %bitcast.19.scale_ref, bf16[256,2,32,128]{3,2,1,0:T(8,128)(2,1)} %bitcast.21.part_ref), custom_call_target="tpu_custom_call" | custom-call | tf_op jit(solution)/shard_map/sum_slots/pallas_call | solution.py:313
  (36 shorter events, 3.1 us)
Async XLA Ops:
  0.6 26.1 %copy-start = (bf16[64,2,32,128]{3,2,1,0:T(8,128)(2,1)S(1)}, bf16[64,2,32,128]{3,2,1,0:T(8,128)(2,1)}, u32[]{:S(2)}) copy-start(bf16[64,2,32,128]{3,2,1,0:T(8,128)(2,1)} %param.17) | copy-start | bytes 3145732
  29.8 5.7 %copy-start.5 = (bf16[32,2,32,32]{3,2,1,0:T(8,128)(2,1)S(1)}, bf16[32,2,32,32]{3,2,1,0:T(8,128)(2,1)}, u32[]{:S(2)}) copy-start(bf16[32,2,32,32]{3,2,1,0:T(8,128)(2,1)} %param.18) | copy-start | bytes 393220
  29.8 57.3 %all-to-all-start.1 = ((bf16[128,2,2,32,128]{4,3,2,1,0:T(8,128)(2,1)}), bf16[128,2,2,32,128]{4,3,2,1,0:T(8,128)(2,1)}, u32[]{:S(2)}, u32[]{:S(2)}) async-start(bf16[128,2,2,32,128]{4,3,2,1,0:T(8,128)(2,1)} %bitcast.45), calls=%async_computation.1 | async-start | bytes 8388608 | tf_op jit(solution)/shard_map/all_to_all | solution.py:352
  36.2 4.5 %copy-start.6 = (bf16[2,32,512,1]{2,1,0,3:T(8,128)(2,1)S(1)}, bf16[2,32,512,1]{2,1,0,3:T(8,128)(2,1)}, u32[]{:S(2)}) copy-start(bf16[2,32,512,1]{2,1,0,3:T(8,128)(2,1)} %constant.32) | copy-start | bytes 196612
  36.9 6.4 %copy-start.1 = (bf16[32,32,32]{1,2,0:T(8,128)(2,1)}, bf16[32,32,32]{1,2,0:T(8,128)(2,1)S(1)}, u32[]{:S(2)}) copy-start(bf16[32,32,32]{1,2,0:T(8,128)(2,1)S(1)} %get-tuple-element.6) | copy-start | bytes 196612
  36.9 6.4 %copy-start.3 = (bf16[32,32,32]{1,2,0:T(8,128)(2,1)}, bf16[32,32,32]{1,2,0:T(8,128)(2,1)S(1)}, u32[]{:S(2)}) copy-start(bf16[32,32,32]{1,2,0:T(8,128)(2,1)S(1)} %get-tuple-element.7) | copy-start | bytes 196612
  50.5 5.3 %copy-start.8 = (pred[4,256]{1,0:T(4,128)(4,1)S(1)}, pred[4,256]{1,0:T(4,128)(4,1)}, u32[]{:S(2)}) copy-start(pred[4,256]{1,0:T(4,128)(4,1)} %constant.31) | copy-start | bytes 3076
  55.9 3.8 %copy-start.2 = (bf16[32,32,32]{1,2,0:T(8,128)(2,1)S(1)}, bf16[32,32,32]{1,2,0:T(8,128)(2,1)}, u32[]{:S(2)}) copy-start(bf16[32,32,32]{1,2,0:T(8,128)(2,1)} %copy-done.1) | copy-start | bytes 196612
  55.9 3.8 %copy-start.4 = (bf16[32,32,32]{1,2,0:T(8,128)(2,1)S(1)}, bf16[32,32,32]{1,2,0:T(8,128)(2,1)}, u32[]{:S(2)}) copy-start(bf16[32,32,32]{1,2,0:T(8,128)(2,1)} %copy-done.3) | copy-start | bytes 196612
  55.9 4.9 %copy-start.7 = (s32[128,1]{0,1:T(1,128)S(1)}, s32[128,1]{0,1:T(1,128)}, u32[]{:S(2)}) copy-start(s32[128,1]{0,1:T(1,128)} %param.14) | copy-start | bytes 1540
  156.1 57.1 %all-to-all-start.2 = ((bf16[128,2,2,32,128]{4,3,2,1,0:T(8,128)(2,1)}), bf16[128,2,2,32,128]{4,3,2,1,0:T(8,128)(2,1)}, u32[]{:S(2)}, u32[]{:S(2)}) async-start(bf16[128,2,2,32,128]{4,3,2,1,0:T(8,128)(2,1)} %bitcast.47), calls=%async_computation.2 | async-start | bytes 8388608 | tf_op jit(solution)/shard_map/all_to_all | solution.py:359

commit v3 on v2

--- a/solution.py
+++ b/solution.py
@@ -7,7 +7,6 @@
 from jax.sharding import PartitionSpec as P
 
 AXES = ("facet", "vis")
-CAP = 2
 
 BF = jnp.bfloat16
 F32 = jnp.float32
@@ -147,8 +146,10 @@
     return (contrib[:, :128] + contrib[:, 128:]).astype(BF).reshape(2, 32, 128)
 
 
-def block_kernel(pos_ref, plane_ref, obs_ref, uv_ref, wgt_ref, tile_ref, left_ref, leftt_ref, right_ref,
-                 res_ref, out_ref, u_tab, v_tab, prod, grown, coef, vis):
+def block_kernel(order_ref, pos_ref, plane_ref, *refs):
+    obs_refs = refs[:STEP]
+    uv_ref, wgt_ref, tile_ref, left_ref, leftt_ref, right_ref = refs[STEP:STEP + 6]
+    res_ref, out_ref, u_tab, v_tab, prod, grown, coef, vis = refs[-8:]
     width = 32
     step = pl.program_id(0)
     tables(uv_ref, u_tab, v_tab, width)
@@ -177,7 +178,8 @@
                 total = total + spread[8 * g:8 * g + 8] * rows[g]
             phase_r, phase_i = row_of(v_tab, 12, b, start, 8), row_of(v_tab, 13, b, start, 8) * sign
             total = total * phase_r + swap_parts(total) * phase_i
-            resid = obs_ref[b, :, lanes] - total
+            seen = jnp.concatenate([obs_refs[b][0, 0, :, lanes], obs_refs[b][0, 1, :, lanes]], axis=0)
+            resid = seen - total
             res_ref[b, :, lanes] = resid
             scaled = resid * jnp.broadcast_to(wgt_ref[b:b + 1, lanes], (8, CHUNK))
             turned = scaled * phase_r - swap_parts(scaled) * phase_i
@@ -244,29 +246,43 @@
     return left, left.transpose(0, 2, 1), right
 
 
-def degrid_grid(position, w_plane, vis_obs, uv_coords, vis_weight, arrived, left, leftt, right):
+def degrid_grid(phase, order, position, planes, vis_obs, uv_coords, vis_weight, arrived, matrices, residual):
     blocks = vis_obs.shape[0]
-    grid = blocks // STEP
-    vis_obs = vis_obs.reshape(blocks, 8, 1024)
-    uv_coords = uv_coords.transpose(1, 0, 2)
-    whole = lambda *shape: pl.BlockSpec(shape, lambda i, *_: (0,) * len(shape), pipeline_mode=pl.Buffered(1))
-    residual, outgoing = pl.pallas_call(
+    count = order.shape[0]
+    left, leftt, right = matrices
+
+    def whole(array):
+        zeros = (0,) * array.ndim
+        return pl.BlockSpec(array.shape, lambda i, *_: zeros, pipeline_mode=pl.Buffered(1))
+
+    def obs_spec(b):
+        return pl.BlockSpec((1, 2, 4, 1024), lambda i, order_ref, *_: (order_ref[i * STEP + b], 0, 0, 0))
+
+    steps = count // STEP
+    first = phase * steps
+    operands = [vis_obs] * STEP + [uv_coords, vis_weight, arrived, left, leftt, right]
+    in_specs = [obs_spec(b) for b in range(STEP)] + [
+        pl.BlockSpec((2, STEP, 1024), lambda i, *_: (0, i + first, 0)),
+        pl.BlockSpec((STEP, 1024), lambda i, *_: (i + first, 0)),
+        whole(arrived),
+        whole(left),
+        whole(leftt),
+        whole(right),
+    ]
+    aliases = {}
+    if residual is not None:
+        operands.append(residual)
+        in_specs.append(pl.BlockSpec(memory_space=pl.ANY))
+        aliases = {3 + len(operands) - 1: 0}
+    return pl.pallas_call(
         block_kernel,
         grid_spec=pltpu.PrefetchScalarGridSpec(
-            num_scalar_prefetch=2,
-            grid=(grid,),
-            in_specs=[
-                pl.BlockSpec((STEP, 8, 1024), lambda i, *_: (i, 0, 0)),
-                pl.BlockSpec((2, STEP, 1024), lambda i, *_: (0, i, 0)),
-                pl.BlockSpec((STEP, 1024), lambda i, *_: (i, 0)),
-                whole(*arrived.shape),
-                whole(*left.shape),
-                whole(*leftt.shape),
-                whole(*right.shape),
-            ],
+            num_scalar_prefetch=3,
+            grid=(steps,),
+            in_specs=in_specs,
             out_specs=[
-                pl.BlockSpec((STEP, 8, 1024), lambda i, *_: (i, 0, 0)),
-                whole(*arrived.shape),
+                pl.BlockSpec((STEP, 8, 1024), lambda i, *_: (i + first, 0, 0)),
+                whole(arrived),
             ],
             scratch_shapes=[
                 pltpu.VMEM((8, 32 * STEP, 128), F32),
@@ -278,22 +294,23 @@
             ],
         ),
         out_shape=[
-            jax.ShapeDtypeStruct(vis_obs.shape, F32),
+            jax.ShapeDtypeStruct((blocks, 8, 1024), F32),
             jax.ShapeDtypeStruct(arrived.shape, BF),
         ],
-        compiler_params=pltpu.CompilerParams(vmem_limit_bytes=60 << 20),
-        name="degrid_grid",
-    )(position, w_plane, vis_obs, uv_coords, vis_weight, arrived, left, leftt, right)
-    return residual.reshape(blocks, 2, 4, 1024), outgoing
-
-
-def sum_kernel(slot_ref, scale_ref, part_ref, out_ref, total):
+        input_output_aliases=aliases,
+        compiler_params=pltpu.CompilerParams(vmem_limit_bytes=63 << 20),
+        cost_estimate=pl.CostEstimate(flops=count * 80_000_000, bytes_accessed=count * 120_000, transcendentals=0),
+        name=f"degrid_grid_{phase}",
+    )(order, position, planes, *operands)
+
+
+def sum_kernel(slot_ref, scale_ref, part_ref, start_ref, out_ref, total):
     step = pl.program_id(0)
     count = part_ref.shape[0]
 
     @pl.when(step == 0)
     def _():
-        total[...] = jnp.zeros_like(total)
+        total[...] = start_ref[...]
 
     def add(i, carry):
         slot = slot_ref[step * count + i]
@@ -307,7 +324,7 @@
         out_ref[...] = total[: out_ref.shape[0]] * scale_ref[0]
 
 
-def sum_slots(slots, scale, parts, owned):
+def sum_slots(slots, scale, parts, start, rows):
     count = parts.shape[0] // 8
     shape = parts.shape[1:]
     return pl.pallas_call(
@@ -315,51 +332,90 @@
         grid_spec=pltpu.PrefetchScalarGridSpec(
             num_scalar_prefetch=2,
             grid=(8,),
-            in_specs=[pl.BlockSpec((count,) + shape, lambda i, *_: (i, 0, 0, 0))],
-            out_specs=pl.BlockSpec((owned,) + shape, lambda i, *_: (0, 0, 0, 0)),
-            scratch_shapes=[pltpu.VMEM((owned + 1,) + shape, F32)],
+            in_specs=[
+                pl.BlockSpec((count,) + shape, lambda i, *_: (i, 0, 0, 0)),
+                pl.BlockSpec(start.shape, lambda i, *_: (0, 0, 0, 0), pipeline_mode=pl.Buffered(1)),
+            ],
+            out_specs=pl.BlockSpec((rows,) + shape, lambda i, *_: (0, 0, 0, 0), pipeline_mode=pl.Buffered(1)),
+            scratch_shapes=[pltpu.VMEM(start.shape, F32)],
         ),
-        out_shape=jax.ShapeDtypeStruct((owned,) + shape, F32),
-        compiler_params=pltpu.CompilerParams(vmem_limit_bytes=32 << 20),
+        out_shape=jax.ShapeDtypeStruct((rows,) + shape, F32),
+        compiler_params=pltpu.CompilerParams(vmem_limit_bytes=63 << 20),
+        cost_estimate=pl.CostEstimate(flops=4_000_000, bytes_accessed=6_000_000, transcendentals=0),
         name="sum_slots",
-    )(slots, scale, parts)
+    )(slots, scale, parts, start)
+
+
+def plan(target, blocks):
+    same = target[:, None] == target[None, :]
+    earlier = np.arange(blocks)[:, None] > np.arange(blocks)[None, :]
+    rank = jnp.sum(same & earlier, axis=1, dtype=jnp.int32)
+    double = jnp.sum(same, axis=1, dtype=jnp.int32) > 1
+    singles = jnp.sum(earlier & ~double[None, :], axis=1, dtype=jnp.int32)
+    spare = blocks // 2 - jnp.sum(double, dtype=jnp.int32) // 2
+    phase = jnp.where(double, rank, (singles >= spare).astype(jnp.int32))
+    return phase, earlier
 
 
 def shards(vis_obs, uv_coords, vis_weight, block_group, tile_slot, w_plane, model_tiles, w_kernels):
     blocks, nvis = vis_weight.shape
     groups = lax.axis_size(AXES)
     owned = model_tiles.shape[0]
-    tile_shape = model_tiles.shape[1:]
+    half = blocks // 2
     target = block_group[:, 0]
-    same = target[:, None] == target[None, :]
-    earlier = np.arange(blocks)[:, None] > np.arange(blocks)[None, :]
-    rank = jnp.sum(same & earlier, axis=1, dtype=jnp.int32)
-    position = target * CAP + rank
+    phase, earlier = plan(target, blocks)
+    slot = jnp.arange(2 * groups, dtype=jnp.int32)
     wanted = jnp.max(
-        jnp.where(
-            position[:, None] == jnp.arange(groups * CAP, dtype=jnp.int32)[None, :], tile_slot[:, None], -1
-        ),
-        axis=0,
-    )
+        jnp.where((target + phase * groups)[None, :] == slot[:, None], tile_slot[None, :], -1), axis=1
+    ).reshape(2, groups)
     message = jnp.concatenate(
-        [wanted.astype(F32).reshape(groups, CAP), jnp.full((groups, 1), jnp.sum(vis_weight))], axis=1
+        [wanted.astype(F32).T, jnp.full((groups, 1), jnp.sum(vis_weight))], axis=1
     )
     message = lax.all_to_all(message, AXES, split_axis=0, concat_axis=0, tiled=True)
-    requested = message[:, :CAP].astype(jnp.int32).reshape(-1)
-    scale = (blocks * groups * nvis) / jnp.sum(message[:, CAP])
-    chosen = jnp.take(model_tiles, jnp.maximum(requested, 0), axis=0, mode="clip")
-    chosen = chosen.reshape((groups, CAP) + tile_shape)
-    arrived = lax.all_to_all(chosen, AXES, split_axis=0, concat_axis=0, tiled=True)
-    arrived = arrived.reshape((groups * CAP,) + tile_shape)
-    left, leftt, right = plane_matrices(w_kernels)
-    residual, outgoing = degrid_grid(
-        position, w_plane, vis_obs, uv_coords, vis_weight, arrived, left, leftt, right
+    requested = message[:, :2].astype(jnp.int32)
+    scale = (blocks * groups * nvis) / jnp.sum(message[:, 2])
+
+    def exchange(array):
+        return lax.all_to_all(array, AXES, split_axis=0, concat_axis=0, tiled=True)
+
+    chosen = [
+        jnp.take(model_tiles, jnp.maximum(requested[:, turn], 0), axis=0, mode="clip")
+        for turn in range(2)
+    ]
+    arrived = [exchange(chosen[0])]
+    place = phase * half + jnp.sum(
+        earlier & (phase[:, None] == phase[None, :]), axis=1, dtype=jnp.int32
     )
-    outgoing = outgoing.reshape((groups, CAP) + tile_shape)
-    returned = lax.all_to_all(outgoing, AXES, split_axis=0, concat_axis=0, tiled=True)
-    returned = returned.reshape((groups * CAP,) + tile_shape)
+    at = place[None, :] == jnp.arange(blocks, dtype=jnp.int32)[:, None]
+
+    def ordered(values):
+        return jnp.sum(jnp.where(at, values[None, :], 0), axis=1, dtype=jnp.int32)
+
+    order = ordered(jnp.arange(blocks, dtype=jnp.int32))
+    position = ordered(target)
+    planes = ordered(w_plane)
+    uv_sorted = jnp.take(uv_coords.transpose(1, 0, 2), order, axis=1, mode="clip")
+    weight_sorted = jnp.take(vis_weight, order, axis=0, mode="clip")
+    matrices = plane_matrices(w_kernels)
+    late, matrices, uv_sorted, weight_sorted, order, position, planes = lax.optimization_barrier(
+        (chosen[1], matrices, uv_sorted, weight_sorted, order, position, planes)
+    )
+    arrived.append(exchange(late))
+    residual = None
+    returned = []
+    for turn in range(2):
+        part = slice(turn * half, turn * half + half)
+        residual, outgoing = degrid_grid(
+            turn, order[part], position[part], planes[part], vis_obs, uv_sorted, weight_sorted,
+            arrived[turn], matrices, residual
+        )
+        returned.append(exchange(outgoing))
+    residual = jnp.take(residual, place, axis=0, mode="clip").reshape(vis_obs.shape)
     slots = jnp.where(requested < 0, owned, requested)
-    return residual, sum_slots(slots, scale.reshape(1), returned, owned)
+    start = jnp.zeros((owned + 1,) + model_tiles.shape[1:], F32)
+    one = jnp.ones((1,), F32)
+    partial = sum_slots(slots[:, 0], one, returned[0], start, owned + 1)
+    return residual, sum_slots(slots[:, 1], scale.reshape(1), returned[1], partial, owned)
 
 
 def solution(mesh):

time: 221 us -> 212 us (0.959)
  waiting for transfers between devices: 70.6 us -> 11.5 us
  starting transfers between devices: 11.3 us -> 33 us
  Pallas kernels: 76.4 us -> 91.4 us
  local copies, waits for them, and re-layouts: 22.1 us -> 30.5 us
  between operations: 1.56 us -> 4.19 us
    all_to_all x2 -> x4, waiting for transfers between devices: 70.6 us -> 11.5 us  [exchange(): return lax.all_to_all(array, AXES, split_axis=0, concat_axis=0, tiled=True)]
    all_to_all x2 -> x4, starting transfers between devices: 11.3 us -> 33 us  [exchange(): return lax.all_to_all(array, AXES, split_axis=0, concat_axis=0, tiled=True)]
    gather x1 -> x6, local copies, waits for them, and re-layouts: 3.04 us -> 15 us  [the longest x1 4.93 us: shards(): jnp.take(residual, place, axis=0, mode='clip').reshape(vis_obs.shape)]
    pallas_call x1 -> x2, Pallas kernels: 69 us -> 76.6 us  [degrid_grid(): pl.pallas_call(block_kernel, grid_spec=pltpu.PrefetchScalarGridSpec(num_s...]
    pallas_call x1 -> x2, Pallas kernels: 7.35 us -> 14.8 us  [sum_slots(): pl.pallas_call(sum_kernel, grid_spec=pltpu.PrefetchScalarGridSpec(num_sca...]
    reshape x3 -> x1, local copies, waits for them, and re-layouts: 10.6 us -> 5.16 us  [shards(): jnp.take(residual, place, axis=0, mode='clip').reshape(vis_obs.shape)]
    unnamed x21 -> x18, local copies, waits for them, and re-layouts: 3.14 us -> 0.79 us
  transfers between devices with their start and end apart: 2 -> 4, of which waited for: 2 -> 2; matrix products, arithmetic and copies ran while one was open for 14% -> 19% of each run, Pallas kernels for 0% -> 40%
where the time goes in v3:
time: 212 us; the launch traced here: 211 us
  Pallas kernels  91.4 us (43%)
  starting transfers between devices  33 us (16%)
  local copies, waits for them, and re-layouts  30.5 us (14%)
  blocking collectives  20.9 us (10%)
  other arithmetic  17.1 us (8%)
  waiting for transfers between devices  11.5 us (5%)
  between operations  4.19 us (2%)
  matrix products  2.52 us (1%)
    pallas_call x2, Pallas kernels, degrid_grid(): pl.pallas_call(block_kernel, grid_spec=pltpu.PrefetchScalarGridSpec(num_s...  76.6 us
    all_to_all x4, starting transfers between devices, exchange(): return lax.all_to_all(array, AXES, split_axis=0, concat_axis=0, tiled=True)  33 us
    all_to_all x1, blocking collectives, shards(): lax.all_to_all(message, AXES, split_axis=0, concat_axis=0, tiled=True)  20.9 us
    pallas_call x2, Pallas kernels, sum_slots(): pl.pallas_call(sum_kernel, grid_spec=pltpu.PrefetchScalarGridSpec(num_sca...  14.8 us
    all_to_all x4, waiting for transfers between devices, exchange(): return lax.all_to_all(array, AXES, split_axis=0, concat_axis=0, tiled=True)  11.5 us
    reshape x1, local copies, waits for them, and re-layouts, shards(): jnp.take(residual, place, axis=0, mode='clip').reshape(vis_obs.shape)  5.16 us
    gather x1, local copies, waits for them, and re-layouts, shards(): jnp.take(residual, place, axis=0, mode='clip').reshape(vis_obs.shape)  4.93 us
    transpose x1, other arithmetic, plane_matrices(): grid = grid.reshape(planes, 2, width, 2, 256).transpose(0, 1, 3, 2, 4)  4.68 us
  transfers between devices with their start and end apart: 4, of which 2 were waited for; matrix products, arithmetic and copies ran while one was open for 19% of the time, Pallas kernels for 40%

profile of v3, /device:TPU:1, one launch (start us, length us, event | category | flops | bytes accessed | tf_op | source)
XLA Modules:
  0.0 211.1 jit_solution(14170689622107063958)
XLA Ops:
  7.2 1.8 reduce_sum.96
  9.8 20.9 %all_to_all.32 = f32[128,1,3]{2,1,0:T(1,128)S(1)} all-to-all(f32[128,1,3]{2,1,0:T(1,128)S(1)} %copy.42), channel_id=1, replica_groups=mesh['facet'=8,'vis'=16] {'facet','vis'}, dimensions={0} | all-to-all | bytes 3072 | tf_op jit(solution)/shard_map/all_to_all | solution.py:374
  30.9 2.1 %gather_fusion.3 = bf16[128,2,32,128]{3,2,1,0:T(8,128)(2,1)} fusion(bf16[64,2,32,128]{3,2,1,0:T(8,128)(2,1)S(1)} %copy-done.1, s32[1024]{0:T(1024)S(1)} %pad_clamp_fusion.1), kind=kCustom, calls=%fused_computation.3 | custom fusion | bytes 4194816 | tf_op jit(solution)/shard_map/jit(_take)/gather | solution.py:382
  33.0 5.6 %all-to-all-start.2 = ((bf16[128,2,32,128]{3,2,1,0:T(8,128)(2,1)}), bf16[128,2,32,128]{3,2,1,0:T(8,128)(2,1)}, u32[]{:S(2)}, u32[]{:S(2)}) async-start(bf16[128,2,32,128]{3,2,1,0:T(8,128)(2,1)} %gather_fusion.3), calls=%async_computation.2 | async-start | bytes 4194304 | tf_op jit(solution)/shard_map/all_to_all | solution.py:379
  39.0 1.6 gather_fusion.2
  40.6 3.0 %gather_fusion.1 = f32[128,2,1024]{2,1,0:T(2,128)S(1)} fusion(f32[2,128,1024]{2,0,1:T(2,128)} %bitcast.41, s32[1024]{0:T(1024)S(1)} %pad_clamp_fusion.2), kind=kCustom, calls=%fused_computation.1 | custom fusion | bytes 2097664 | tf_op jit(solution)/shard_map/jit(_take)/gather | solution.py:397
  43.6 1.3 copy.55
  45.9 2.5 %reduce-precision_convert_fusion = (bf16[32,32,512]{2,1,0:T(8,128)(2,1)S(1)}, bf16[32,32,512]{2,1,0:T(8,128)(2,1)}) fusion(bf16[2,32,512,1]{2,1,0,3:T(8,128)(2,1)S(1)} %copy-done.4, bf16[32,2,32,32]{3,2,1,0:T(8,128)(2,1)} %param.18), kind=kOutput, calls=%fused_computation.7 | convolution fusion | flops 69730304 | bytes 2293760 | tf_op jit(solution)/shard_map/zcmk,cmq->zkq/dot_general | solution.py:237
  48.4 2.1 %stack.10 = bf16[32,1,32,2,256]{4,3,2,0,1:T(2,128)(2,1)} reshape(bf16[32,32,512]{2,1,0:T(8,128)(2,1)} %get-tuple-element.42) | data formatting | bytes 2097152 | tf_op jit(solution)/shard_map/stack | solution.py:240
  51.7 4.7 %maximum_bitcast_fusion = bf16[32,2,2,32,256]{4,2,3,0,1:T(2,128)(2,1)S(1)} fusion(bf16[32,1,32,2,256]{4,3,2,0,1:T(2,128)(2,1)} %stack.10, bf16[32,1,32,2,256]{4,3,2,0,1:T(2,128)(2,1)} %stack.9), kind=kLoop, calls=%fused_computation.9 | loop fusion | flops 1048576 | bytes 4194304 | tf_op jit(solution)/shard_map/transpose | solution.py:241
  57.1 3.8 %bitcast_select_fusion.refs_13_ = bf16[32,2,256,256]{3,2,1,0:T(8,128)(2,1)} fusion(pred[256,256]{1,0:T(8,128)(4,1)S(1)} %bitcast.45, bf16[32,2,2,32,256]{4,3,2,1,0:T(8,128)(2,1)S(1)} %copy.46), kind=kLoop, calls=%fused_computation.5 | loop fusion | flops 4194304 | bytes 10551296 | tf_op jit(solution)/shard_map/jit(_where)/select_n | solution.py:244
  62.5 2.1 %gather_fusion = bf16[128,2,32,128]{3,2,1,0:T(8,128)(2,1)} fusion(bf16[64,2,32,128]{3,2,1,0:T(8,128)(2,1)S(1)} %copy-done.1, s32[1024]{0:T(1024)S(1)} %pad_clamp_fusion.3), kind=kCustom, calls=%fused_computation | custom fusion | bytes 4194816 | tf_op jit(solution)/shard_map/jit(_take)/gather | solution.py:382
  64.7 3.4 %all-to-all-done.2.refs_10_ = bf16[128,2,32,128]{3,2,1,0:T(8,128)(2,1)} async-done(((bf16[128,2,32,128]{3,2,1,0:T(8,128)(2,1)}), bf16[128,2,32,128]{3,2,1,0:T(8,128)(2,1)}, u32[]{:S(2)}, u32[]{:S(2)}) %all-to-all-start.2) | async-done | bytes 2097184 | tf_op jit(solution)/shard_map/all_to_all | solution.py:379
  68.1 6.9 %all-to-all-start.1 = ((bf16[128,2,32,128]{3,2,1,0:T(8,128)(2,1)}), bf16[128,2,32,128]{3,2,1,0:T(8,128)(2,1)}, u32[]{:S(2)}, u32[]{:S(2)}) async-start(bf16[128,2,32,128]{3,2,1,0:T(8,128)(2,1)} %gather_fusion), calls=%async_computation.1 | async-start | bytes 4194304 | tf_op jit(solution)/shard_map/all_to_all | solution.py:379
  77.3 38.3 %degrid_grid_0.1 = (f32[128,8,1024]{2,1,0:T(8,128)}, bf16[128,2,32,128]{3,2,1,0:T(8,128)(2,1)}) custom-call(s32[64]{0:T(128)} %get-tuple-element.49.order_ref, s32[64]{0:T(128)} %get-tuple-element.52.pos_ref, s32[64]{0:T(128)} %get-tuple-element.45.plane_ref, f32[128,2,4,1024]{3,2,1,0:T(4,128)} %refs_7_.3, f32[128,2,4,1024]{3,2,1,0:T(4,128)} %refs_7_.3, ...), custom_call_target="tpu_custom_call" | custom-call | flops 5120000000 | bytes 7680000 | tf_op jit(solution)/shard_map/degrid_grid_0/pallas_call | solution.py:277
  115.6 10.2 %all-to-all-start.4 = ((bf16[128,2,32,128]{3,2,1,0:T(8,128)(2,1)}), bf16[128,2,32,128]{3,2,1,0:T(8,128)(2,1)}, u32[]{:S(2)}, u32[]{:S(2)}) async-start(bf16[128,2,32,128]{3,2,1,0:T(8,128)(2,1)} %get-tuple-element.27), calls=%async_computation.4 | async-start | bytes 4194304 | tf_op jit(solution)/shard_map/all_to_all | solution.py:379
  125.9 38.3 %degrid_grid_1.1 = (f32[128,8,1024]{2,1,0:T(8,128)}, bf16[128,2,32,128]{3,2,1,0:T(8,128)(2,1)}) custom-call(s32[64]{0:T(128)} %get-tuple-element.50.order_ref, s32[64]{0:T(128)} %get-tuple-element.51.pos_ref, s32[64]{0:T(128)} %get-tuple-element.46.plane_ref, f32[128,2,4,1024]{3,2,1,0:T(4,128)} %refs_7_.3, ...), custom_call_target="tpu_custom_call", output_to_operand_aliasing={{0}: (17, {})} | custom-call | flops 5120000000 | bytes 7680000 | tf_op jit(solution)/shard_map/degrid_grid_1/pallas_call | solution.py:277
  164.2 10.2 %all-to-all-start.3 = ((bf16[128,2,32,128]{3,2,1,0:T(8,128)(2,1)}), bf16[128,2,32,128]{3,2,1,0:T(8,128)(2,1)}, u32[]{:S(2)}, u32[]{:S(2)}) async-start(bf16[128,2,32,128]{3,2,1,0:T(8,128)(2,1)} %get-tuple-element.26), calls=%async_computation.3 | async-start | bytes 4194304 | tf_op jit(solution)/shard_map/all_to_all | solution.py:379
  176.6 4.9 %gather_fusion.4 = f32[128,8,1024]{2,1,0:T(8,128)} fusion(f32[128,8,1024]{2,1,0:T(8,128)} %get-tuple-element.25, s32[1024]{0:T(1024)S(1)} %pad_clamp_fusion), kind=kCustom, calls=%fused_computation.4 | custom fusion | bytes 8389120 | tf_op jit(solution)/shard_map/jit(_take)/gather | solution.py:413
  181.5 5.2 %reshape.110 = f32[128,2,4,1024]{3,2,1,0:T(4,128)} reshape(f32[128,8,1024]{2,1,0:T(8,128)} %gather_fusion.4) | data formatting | bytes 8388608 | tf_op jit(solution)/shard_map/reshape | solution.py:413
  186.7 1.6 broadcast_in_dim.106.start_ref
  188.3 7.4 %sum_slots.2.start_ref = f32[65,2,32,128]{3,2,1,0:T(8,128)} custom-call(s32[128]{0:T(128)} %get-tuple-element.28.slot_ref, f32[1]{0:T(128)} %constant.42.clone.1.scale_ref, bf16[128,2,32,128]{3,2,1,0:T(8,128)(2,1)} %all-to-all-done.4.part_ref, f32[65,2,32,128]{3,2,1,0:T(8,128)} %broadcast_in_dim.106.start_ref), custom_call_target="tpu_custom_call" | custom-call | flops 4000000 | bytes 6000000 | tf_op jit(solution)/shard_map/sum_slots/pallas_call | solution.py:330
  195.7 8.0 %all-to-all-done.3.part_ref = bf16[128,2,32,128]{3,2,1,0:T(8,128)(2,1)} async-done(((bf16[128,2,32,128]{3,2,1,0:T(8,128)(2,1)}), bf16[128,2,32,128]{3,2,1,0:T(8,128)(2,1)}, u32[]{:S(2)}, u32[]{:S(2)}) %all-to-all-start.3) | async-done | bytes 2097184 | tf_op jit(solution)/shard_map/all_to_all | solution.py:379
  203.8 7.4 %sum_slots.3 = f32[64,2,32,128]{3,2,1,0:T(8,128)} custom-call(s32[128]{0:T(128)} %get-tuple-element.29.slot_ref, f32[1]{0:T(128)} %bitcast.17.scale_ref, bf16[128,2,32,128]{3,2,1,0:T(8,128)(2,1)} %all-to-all-done.3.part_ref, f32[65,2,32,128]{3,2,1,0:T(8,128)} %sum_slots.2.start_ref), custom_call_target="tpu_custom_call" | custom-call | flops 4000000 | bytes 6000000 | tf_op jit(solution)/shard_map/sum_slots/pallas_call | solution.py:330
  (53 shorter events, 13.5 us)
Async XLA Ops:
  0.6 30.2 %copy-start.1 = (bf16[64,2,32,128]{3,2,1,0:T(8,128)(2,1)S(1)}, bf16[64,2,32,128]{3,2,1,0:T(8,128)(2,1)}, u32[]{:S(2)}) copy-start(bf16[64,2,32,128]{3,2,1,0:T(8,128)(2,1)} %param.17) | copy-start | bytes 3145732
  33.0 5.6 %copy-start.3 = (pred[128,128]{1,0:T(32,128)(4,1)S(1)}, pred[128,128]{1,0:T(32,128)(4,1)}, u32[]{:S(2)}) copy-start(pred[128,128]{1,0:T(32,128)(4,1)} %constant.43.clone) | copy-start | bytes 49156
  33.0 5.8 %copy-start.5 = (s32[128,1]{0,1:T(1,128)S(1)}, s32[128,1]{0,1:T(1,128)}, u32[]{:S(2)}) copy-start(s32[128,1]{0,1:T(1,128)} %param.14) | copy-start | bytes 1540
  33.0 5.8 %copy-start.7 = (s32[128]{0:T(128)S(1)}, s32[128]{0:T(128)}, u32[]{:S(2)}) copy-start(s32[128]{0:T(128)} %param.16) | copy-start | bytes 1540
  33.0 6.0 %copy-start = (f32[128,1024]{1,0:T(8,128)S(1)}, f32[128,1024]{1,0:T(8,128)}, u32[]{:S(2)}) copy-start(f32[128,1024]{1,0:T(8,128)} %param.13) | copy-start | bytes 1572868
  33.0 35.1 %all-to-all-start.2 = ((bf16[128,2,32,128]{3,2,1,0:T(8,128)(2,1)}), bf16[128,2,32,128]{3,2,1,0:T(8,128)(2,1)}, u32[]{:S(2)}, u32[]{:S(2)}) async-start(bf16[128,2,32,128]{3,2,1,0:T(8,128)(2,1)} %gather_fusion.3), calls=%async_computation.2 | async-start | bytes 4194304 | tf_op jit(solution)/shard_map/all_to_all | solution.py:379
  40.6 4.3 %copy-start.2 = (bf16[32,2,32,32]{3,2,1,0:T(8,128)(2,1)S(1)}, bf16[32,2,32,32]{3,2,1,0:T(8,128)(2,1)}, u32[]{:S(2)}) copy-start(bf16[32,2,32,32]{3,2,1,0:T(8,128)(2,1)} %param.18) | copy-start | bytes 393220
  44.9 1.0 copy-start.4
  56.4 0.7 copy-start.6
  68.1 47.5 %all-to-all-start.1 = ((bf16[128,2,32,128]{3,2,1,0:T(8,128)(2,1)}), bf16[128,2,32,128]{3,2,1,0:T(8,128)(2,1)}, u32[]{:S(2)}, u32[]{:S(2)}) async-start(bf16[128,2,32,128]{3,2,1,0:T(8,128)(2,1)} %gather_fusion), calls=%async_computation.1 | async-start | bytes 4194304 | tf_op jit(solution)/shard_map/all_to_all | solution.py:379
  115.6 48.5 %all-to-all-start.4 = ((bf16[128,2,32,128]{3,2,1,0:T(8,128)(2,1)}), bf16[128,2,32,128]{3,2,1,0:T(8,128)(2,1)}, u32[]{:S(2)}, u32[]{:S(2)}) async-start(bf16[128,2,32,128]{3,2,1,0:T(8,128)(2,1)} %get-tuple-element.27), calls=%async_computation.4 | async-start | bytes 4194304 | tf_op jit(solution)/shard_map/all_to_all | solution.py:379
  164.2 39.6 %all-to-all-start.3 = ((bf16[128,2,32,128]{3,2,1,0:T(8,128)(2,1)}), bf16[128,2,32,128]{3,2,1,0:T(8,128)(2,1)}, u32[]{:S(2)}, u32[]{:S(2)}) async-start(bf16[128,2,32,128]{3,2,1,0:T(8,128)(2,1)} %get-tuple-element.26), calls=%async_computation.3 | async-start | bytes 4194304 | tf_op jit(solution)/shard_map/all_to_all | solution.py:379

commit v4 on v3

--- a/solution.py
+++ b/solution.py
@@ -117,48 +117,78 @@
     return pltpu.roll(value, 4, 0)
 
 
-def forward(b, tile, left_k, right_top, right_rest, coef):
-    left = nn_dot(left_k, tile.reshape(64, 128))
-    r_up, r_lo, i_up, i_lo = left[0:16], left[16:32], left[32:48], left[48:64]
-    left = jnp.concatenate(
-        [
-            jnp.concatenate([r_up + r_lo, i_lo - i_up], axis=0),
-            jnp.concatenate([i_up + i_lo, r_up - r_lo], axis=0),
-        ],
-        axis=1,
-    )
-    top, rest = split(left)
-    found = nn_dot(jnp.concatenate([top, rest], axis=0), right_top)
-    found = found[:32] + found[32:] + nn_dot(top, right_rest)
-    for r in range(4):
-        coef[b, 32 * r:32 * r + 32, :] = found[:, 64 * r:64 * r + 64].astype(BF)
-
-
-def backward(grown, left_k, right_top, right_rest):
-    grown = jnp.concatenate([grown[32 * r:32 * r + 32] for r in range(4)], axis=1)
-    top, rest = split(grown)
-    back = nt_dot(jnp.concatenate([top, rest], axis=0), right_top)
-    back = back[:32] + back[32:] + nt_dot(top, right_rest)
-    a_r, b_r, a_i, b_i = back[:16, :128], back[16:, :128], back[:16, 128:], back[16:, 128:]
-    back = jnp.concatenate([a_r + b_i, a_r - b_i, a_i - b_r, a_i + b_r], axis=0)
-    top, rest = split(back)
-    contrib = nn_dot(left_k, jnp.concatenate([top, rest], axis=1))
-    return (contrib[:, :128] + contrib[:, 128:]).astype(BF).reshape(2, 32, 128)
+def forward(tiles, lefts, tops, rests):
+    found = [nn_dot(k, tile.reshape(64, 128)) for k, tile in zip(lefts, tiles)]
+    pairs = []
+    for left in found:
+        r_up, r_lo, i_up, i_lo = left[0:16], left[16:32], left[32:48], left[48:64]
+        left = jnp.concatenate(
+            [
+                jnp.concatenate([r_up + r_lo, i_lo - i_up], axis=0),
+                jnp.concatenate([i_up + i_lo, r_up - r_lo], axis=0),
+            ],
+            axis=1,
+        )
+        pairs.append(split(left))
+    large = [nn_dot(jnp.concatenate(pair, axis=0), m) for pair, m in zip(pairs, tops)]
+    tiny = [nn_dot(pair[0], m) for pair, m in zip(pairs, rests)]
+    return [(x[:32] + x[32:] + y).astype(BF) for x, y in zip(large, tiny)]
+
+
+def backward(growns, lefts, tops, rests):
+    pairs = [
+        split(jnp.concatenate([grown[32 * r:32 * r + 32] for r in range(4)], axis=1)) for grown in growns
+    ]
+    large = [nt_dot(jnp.concatenate(pair, axis=0), m) for pair, m in zip(pairs, tops)]
+    tiny = [nt_dot(pair[0], m) for pair, m in zip(pairs, rests)]
+    halves = []
+    for x, y in zip(large, tiny):
+        back = x[:32] + x[32:] + y
+        a_r, b_r, a_i, b_i = back[:16, :128], back[16:, :128], back[:16, 128:], back[16:, 128:]
+        back = jnp.concatenate([a_r + b_i, a_r - b_i, a_i - b_r, a_i + b_r], axis=0)
+        halves.append(jnp.concatenate(split(back), axis=1))
+    parts = [nn_dot(k, half) for k, half in zip(lefts, halves)]
+    return [(part[:, :128] + part[:, 128:]).astype(BF).reshape(2, 32, 128) for part in parts]
 
 
 def block_kernel(order_ref, pos_ref, plane_ref, *refs):
-    obs_refs = refs[:STEP]
-    uv_ref, wgt_ref, tile_ref, left_ref, leftt_ref, right_ref = refs[STEP:STEP + 6]
-    res_ref, out_ref, u_tab, v_tab, prod, grown, coef, vis = refs[-8:]
+    obs_ref, uv_ref, wgt_ref, tile_ref, left_ref, leftt_ref, right_ref = refs[:7]
+    res_ref, out_ref, u_tab, v_tab, prod, grown, coef, vis, seen_buf, seen_sem = refs[-10:]
     width = 32
     step = pl.program_id(0)
+    now = lax.rem(step, 2)
+
+    def fetch(turn, side):
+        for b in range(STEP):
+            pltpu.make_async_copy(
+                obs_ref.at[order_ref[turn * STEP + b]], seen_buf.at[side, b], seen_sem.at[side]
+            ).start()
+
+    @pl.when(step == 0)
+    def _():
+        fetch(0, 0)
+
+    @pl.when(step + 1 < pl.num_programs(0))
+    def _():
+        fetch(step + 1, 1 - now)
+
+    pltpu.make_async_copy(obs_ref.at[pl.ds(0, STEP)], seen_buf.at[now], seen_sem.at[now]).wait()
     tables(uv_ref, u_tab, v_tab, width)
     sign = jnp.where(lax.broadcasted_iota(jnp.int32, (8, CHUNK), 0) < 4, -1.0, 1.0).astype(F32)
 
-    def first(b):
-        index = step * STEP + b
-        plane = plane_ref[index]
-        forward(b, tile_ref[pos_ref[index]], left_ref[plane], right_ref[plane, 0], right_ref[plane, 1], coef)
+    def matrices_of(blocks, own):
+        planes = [plane_ref[step * STEP + b] for b in blocks]
+        return (
+            [own[plane] for plane in planes],
+            [right_ref[plane, 0] for plane in planes],
+            [right_ref[plane, 1] for plane in planes],
+        )
+
+    def first(blocks):
+        tiles = [tile_ref[pos_ref[step * STEP + b]] for b in blocks]
+        for b, found in zip(blocks, forward(tiles, *matrices_of(blocks, left_ref))):
+            for r in range(4):
+                coef[b, 32 * r:32 * r + 32, :] = found[:, 64 * r:64 * r + 64]
 
     def products(b):
         for start in range(0, 1024, CHUNK):
@@ -178,7 +208,7 @@
                 total = total + spread[8 * g:8 * g + 8] * rows[g]
             phase_r, phase_i = row_of(v_tab, 12, b, start, 8), row_of(v_tab, 13, b, start, 8) * sign
             total = total * phase_r + swap_parts(total) * phase_i
-            seen = jnp.concatenate([obs_refs[b][0, 0, :, lanes], obs_refs[b][0, 1, :, lanes]], axis=0)
+            seen = jnp.concatenate([seen_buf[now, b, 0, :, lanes], seen_buf[now, b, 1, :, lanes]], axis=0)
             resid = seen - total
             res_ref[b, :, lanes] = resid
             scaled = resid * jnp.broadcast_to(wgt_ref[b:b + 1, lanes], (8, CHUNK))
@@ -188,19 +218,16 @@
                 vis[b, 8 * g:8 * g + 16, lanes] = pair.astype(BF)
         grown[b] = nt_dot(prod[b], vis[b])
 
-    def last(b):
-        index = step * STEP + b
-        plane = plane_ref[index]
-        out_ref[pos_ref[index]] = backward(grown[b], leftt_ref[plane], right_ref[plane, 0], right_ref[plane, 1])
-
-    for turn in range(STEP + 2):
-        if turn < STEP:
-            first(turn)
-            products(turn)
-        if 0 <= turn - 1 < STEP:
-            middle(turn - 1)
-        if 0 <= turn - 2 < STEP:
-            last(turn - 2)
+    def last(blocks):
+        done = backward([grown[b] for b in blocks], *matrices_of(blocks, leftt_ref))
+        for b, part in zip(blocks, done):
+            out_ref[pos_ref[step * STEP + b]] = part
+
+    first(list(range(STEP)))
+    for b in range(STEP):
+        products(b)
+        middle(b)
+    last(list(range(STEP)))
 
 
 def plane_matrices(w_kernels):
@@ -255,13 +282,11 @@
         zeros = (0,) * array.ndim
         return pl.BlockSpec(array.shape, lambda i, *_: zeros, pipeline_mode=pl.Buffered(1))
 
-    def obs_spec(b):
-        return pl.BlockSpec((1, 2, 4, 1024), lambda i, order_ref, *_: (order_ref[i * STEP + b], 0, 0, 0))
-
     steps = count // STEP
     first = phase * steps
-    operands = [vis_obs] * STEP + [uv_coords, vis_weight, arrived, left, leftt, right]
-    in_specs = [obs_spec(b) for b in range(STEP)] + [
+    operands = [vis_obs, uv_coords, vis_weight, arrived, left, leftt, right]
+    in_specs = [
+        pl.BlockSpec(memory_space=pl.ANY),
         pl.BlockSpec((2, STEP, 1024), lambda i, *_: (0, i + first, 0)),
         pl.BlockSpec((STEP, 1024), lambda i, *_: (i + first, 0)),
         whole(arrived),
@@ -291,6 +316,8 @@
                 pltpu.VMEM((STEP, 128, 64), F32),
                 pltpu.VMEM((STEP, 128, 64), BF),
                 pltpu.VMEM((STEP, 64, 1024), BF),
+                pltpu.VMEM((2, STEP, 2, 4, 1024), F32),
+                pltpu.SemaphoreType.DMA((2,)),
             ],
         ),
         out_shape=[

time: 212 us -> 197 us (0.929)
  Pallas kernels: 91.4 us -> 75.7 us
    pallas_call x2, Pallas kernels: 76.6 us -> 60.9 us  [degrid_grid(): pl.pallas_call(block_kernel, grid_spec=pltpu.PrefetchScalarGridSpec(num_s...]
  transfers between devices with their start and end apart: 4 -> 4, of which waited for: 2 -> 2; matrix products, arithmetic and copies ran while one was open for 19% -> 21% of each run, Pallas kernels for 40% -> 35%
where the time goes in v4:
time: 197 us; the launch traced here: 195 us
  Pallas kernels  75.7 us (38%)
  starting transfers between devices  33.1 us (17%)
  local copies, waits for them, and re-layouts  30.5 us (15%)
  blocking collectives  20.9 us (11%)
  other arithmetic  17.1 us (9%)
  waiting for transfers between devices  11.5 us (6%)
  between operations  4.2 us (2%)
  matrix products  2.52 us (1%)
    pallas_call x2, Pallas kernels, degrid_grid(): pl.pallas_call(block_kernel, grid_spec=pltpu.PrefetchScalarGridSpec(num_s...  60.9 us
    all_to_all x4, starting transfers between devices, exchange(): return lax.all_to_all(array, AXES, split_axis=0, concat_axis=0, tiled=True)  33.1 us
    all_to_all x1, blocking collectives, shards(): lax.all_to_all(message, AXES, split_axis=0, concat_axis=0, tiled=True)  20.9 us
    pallas_call x2, Pallas kernels, sum_slots(): pl.pallas_call(sum_kernel, grid_spec=pltpu.PrefetchScalarGridSpec(num_sca...  14.8 us
    all_to_all x4, waiting for transfers between devices, exchange(): return lax.all_to_all(array, AXES, split_axis=0, concat_axis=0, tiled=True)  11.5 us
    reshape x1, local copies, waits for them, and re-layouts, shards(): jnp.take(residual, place, axis=0, mode='clip').reshape(vis_obs.shape)  5.16 us
    gather x1, local copies, waits for them, and re-layouts, shards(): jnp.take(residual, place, axis=0, mode='clip').reshape(vis_obs.shape)  4.93 us
    transpose x1, other arithmetic, plane_matrices(): grid = grid.reshape(planes, 2, width, 2, 256).transpose(0, 1, 3, 2, 4)  4.68 us
  transfers between devices with their start and end apart: 4, of which 2 were waited for; matrix products, arithmetic and copies ran while one was open for 21% of the time, Pallas kernels for 35%

profile of v4, /device:TPU:1, one launch (start us, length us, event | category | flops | bytes accessed | tf_op | source)
XLA Modules:
  0.0 195.5 jit_solution(13818075839083274020)
XLA Ops:
  7.2 1.8 reduce_sum.96
  9.8 20.9 %all_to_all.32 = f32[128,1,3]{2,1,0:T(1,128)S(1)} all-to-all(f32[128,1,3]{2,1,0:T(1,128)S(1)} %copy.42), channel_id=1, replica_groups=mesh['facet'=8,'vis'=16] {'facet','vis'}, dimensions={0} | all-to-all | bytes 3072 | tf_op jit(solution)/shard_map/all_to_all | solution.py:401
  30.9 2.1 %gather_fusion.3 = bf16[128,2,32,128]{3,2,1,0:T(8,128)(2,1)} fusion(bf16[64,2,32,128]{3,2,1,0:T(8,128)(2,1)S(1)} %copy-done.1, s32[1024]{0:T(1024)S(1)} %pad_clamp_fusion.1), kind=kCustom, calls=%fused_computation.3 | custom fusion | bytes 4194816 | tf_op jit(solution)/shard_map/jit(_take)/gather | solution.py:409
  33.0 5.6 %all-to-all-start.2 = ((bf16[128,2,32,128]{3,2,1,0:T(8,128)(2,1)}), bf16[128,2,32,128]{3,2,1,0:T(8,128)(2,1)}, u32[]{:S(2)}, u32[]{:S(2)}) async-start(bf16[128,2,32,128]{3,2,1,0:T(8,128)(2,1)} %gather_fusion.3), calls=%async_computation.2 | async-start | bytes 4194304 | tf_op jit(solution)/shard_map/all_to_all | solution.py:406
  39.0 1.6 gather_fusion.2
  40.6 3.0 %gather_fusion.1 = f32[128,2,1024]{2,1,0:T(2,128)S(1)} fusion(f32[2,128,1024]{2,0,1:T(2,128)} %bitcast.41, s32[1024]{0:T(1024)S(1)} %pad_clamp_fusion.2), kind=kCustom, calls=%fused_computation.1 | custom fusion | bytes 2097664 | tf_op jit(solution)/shard_map/jit(_take)/gather | solution.py:424
  43.6 1.3 copy.55
  45.9 2.5 %reduce-precision_convert_fusion = (bf16[32,32,512]{2,1,0:T(8,128)(2,1)S(1)}, bf16[32,32,512]{2,1,0:T(8,128)(2,1)}) fusion(bf16[2,32,512,1]{2,1,0,3:T(8,128)(2,1)S(1)} %copy-done.4, bf16[32,2,32,32]{3,2,1,0:T(8,128)(2,1)} %param.18), kind=kOutput, calls=%fused_computation.7 | convolution fusion | flops 69730304 | bytes 2293760 | tf_op jit(solution)/shard_map/zcmk,cmq->zkq/dot_general | solution.py:264
  48.4 2.1 %stack.10 = bf16[32,1,32,2,256]{4,3,2,0,1:T(2,128)(2,1)} reshape(bf16[32,32,512]{2,1,0:T(8,128)(2,1)} %get-tuple-element.42) | data formatting | bytes 2097152 | tf_op jit(solution)/shard_map/stack | solution.py:267
  51.7 4.7 %maximum_bitcast_fusion = bf16[32,2,2,32,256]{4,2,3,0,1:T(2,128)(2,1)S(1)} fusion(bf16[32,1,32,2,256]{4,3,2,0,1:T(2,128)(2,1)} %stack.10, bf16[32,1,32,2,256]{4,3,2,0,1:T(2,128)(2,1)} %stack.9), kind=kLoop, calls=%fused_computation.9 | loop fusion | flops 1048576 | bytes 4194304 | tf_op jit(solution)/shard_map/transpose | solution.py:268
  57.1 3.8 %bitcast_select_fusion.refs_6_ = bf16[32,2,256,256]{3,2,1,0:T(8,128)(2,1)} fusion(pred[256,256]{1,0:T(8,128)(4,1)S(1)} %bitcast.45, bf16[32,2,2,32,256]{4,3,2,1,0:T(8,128)(2,1)S(1)} %copy.46), kind=kLoop, calls=%fused_computation.5 | loop fusion | flops 4194304 | bytes 10551296 | tf_op jit(solution)/shard_map/jit(_where)/select_n | solution.py:271
  62.5 2.1 %gather_fusion = bf16[128,2,32,128]{3,2,1,0:T(8,128)(2,1)} fusion(bf16[64,2,32,128]{3,2,1,0:T(8,128)(2,1)S(1)} %copy-done.1, s32[1024]{0:T(1024)S(1)} %pad_clamp_fusion.3), kind=kCustom, calls=%fused_computation | custom fusion | bytes 4194816 | tf_op jit(solution)/shard_map/jit(_take)/gather | solution.py:409
  64.7 3.4 %all-to-all-done.2.refs_3_ = bf16[128,2,32,128]{3,2,1,0:T(8,128)(2,1)} async-done(((bf16[128,2,32,128]{3,2,1,0:T(8,128)(2,1)}), bf16[128,2,32,128]{3,2,1,0:T(8,128)(2,1)}, u32[]{:S(2)}, u32[]{:S(2)}) %all-to-all-start.2) | async-done | bytes 2097184 | tf_op jit(solution)/shard_map/all_to_all | solution.py:406
  68.1 6.9 %all-to-all-start.1 = ((bf16[128,2,32,128]{3,2,1,0:T(8,128)(2,1)}), bf16[128,2,32,128]{3,2,1,0:T(8,128)(2,1)}, u32[]{:S(2)}, u32[]{:S(2)}) async-start(bf16[128,2,32,128]{3,2,1,0:T(8,128)(2,1)} %gather_fusion), calls=%async_computation.1 | async-start | bytes 4194304 | tf_op jit(solution)/shard_map/all_to_all | solution.py:406
  77.3 30.5 %degrid_grid_0.1 = (f32[128,8,1024]{2,1,0:T(8,128)}, bf16[128,2,32,128]{3,2,1,0:T(8,128)(2,1)}) custom-call(s32[64]{0:T(128)} %get-tuple-element.49.order_ref, s32[64]{0:T(128)} %get-tuple-element.52.pos_ref, s32[64]{0:T(128)} %get-tuple-element.45.plane_ref, f32[128,2,4,1024]{3,2,1,0:T(4,128)} %refs_0_.3, f32[2,128,1024]{2,1,0:T(8,128)} %bitcast.39, ...), custom_call_target="tpu_custom_call" | custom-call | flops 5120000000 | bytes 7680000 | tf_op jit(solution)/shard_map/degrid_grid_0/pallas_call | solution.py:302
  107.8 10.2 %all-to-all-start.4 = ((bf16[128,2,32,128]{3,2,1,0:T(8,128)(2,1)}), bf16[128,2,32,128]{3,2,1,0:T(8,128)(2,1)}, u32[]{:S(2)}, u32[]{:S(2)}) async-start(bf16[128,2,32,128]{3,2,1,0:T(8,128)(2,1)} %get-tuple-element.27), calls=%async_computation.4 | async-start | bytes 4194304 | tf_op jit(solution)/shard_map/all_to_all | solution.py:406
  118.0 30.4 %degrid_grid_1.1 = (f32[128,8,1024]{2,1,0:T(8,128)}, bf16[128,2,32,128]{3,2,1,0:T(8,128)(2,1)}) custom-call(s32[64]{0:T(128)} %get-tuple-element.50.order_ref, s32[64]{0:T(128)} %get-tuple-element.51.pos_ref, s32[64]{0:T(128)} %get-tuple-element.46.plane_ref, f32[128,2,4,1024]{3,2,1,0:T(4,128)} %refs_0_.3, ...), custom_call_target="tpu_custom_call", output_to_operand_aliasing={{0}: (10, {})} | custom-call | flops 5120000000 | bytes 7680000 | tf_op jit(solution)/shard_map/degrid_grid_1/pallas_call | solution.py:302
  148.5 10.3 %all-to-all-start.3 = ((bf16[128,2,32,128]{3,2,1,0:T(8,128)(2,1)}), bf16[128,2,32,128]{3,2,1,0:T(8,128)(2,1)}, u32[]{:S(2)}, u32[]{:S(2)}) async-start(bf16[128,2,32,128]{3,2,1,0:T(8,128)(2,1)} %get-tuple-element.26), calls=%async_computation.3 | async-start | bytes 4194304 | tf_op jit(solution)/shard_map/all_to_all | solution.py:406
  160.9 4.9 %gather_fusion.4 = f32[128,8,1024]{2,1,0:T(8,128)} fusion(f32[128,8,1024]{2,1,0:T(8,128)} %get-tuple-element.25, s32[1024]{0:T(1024)S(1)} %pad_clamp_fusion), kind=kCustom, calls=%fused_computation.4 | custom fusion | bytes 8389120 | tf_op jit(solution)/shard_map/jit(_take)/gather | solution.py:440
  165.9 5.2 %reshape.110 = f32[128,2,4,1024]{3,2,1,0:T(4,128)} reshape(f32[128,8,1024]{2,1,0:T(8,128)} %gather_fusion.4) | data formatting | bytes 8388608 | tf_op jit(solution)/shard_map/reshape | solution.py:440
  171.0 1.6 broadcast_in_dim.106.start_ref
  172.6 7.4 %sum_slots.2.start_ref = f32[65,2,32,128]{3,2,1,0:T(8,128)} custom-call(s32[128]{0:T(128)} %get-tuple-element.28.slot_ref, f32[1]{0:T(128)} %constant.42.clone.1.scale_ref, bf16[128,2,32,128]{3,2,1,0:T(8,128)(2,1)} %all-to-all-done.4.part_ref, f32[65,2,32,128]{3,2,1,0:T(8,128)} %broadcast_in_dim.106.start_ref), custom_call_target="tpu_custom_call" | custom-call | flops 4000000 | bytes 6000000 | tf_op jit(solution)/shard_map/sum_slots/pallas_call | solution.py:357
  180.0 8.1 %all-to-all-done.3.part_ref = bf16[128,2,32,128]{3,2,1,0:T(8,128)(2,1)} async-done(((bf16[128,2,32,128]{3,2,1,0:T(8,128)(2,1)}), bf16[128,2,32,128]{3,2,1,0:T(8,128)(2,1)}, u32[]{:S(2)}, u32[]{:S(2)}) %all-to-all-start.3) | async-done | bytes 2097184 | tf_op jit(solution)/shard_map/all_to_all | solution.py:406
  188.1 7.4 %sum_slots.3 = f32[64,2,32,128]{3,2,1,0:T(8,128)} custom-call(s32[128]{0:T(128)} %get-tuple-element.29.slot_ref, f32[1]{0:T(128)} %bitcast.17.scale_ref, bf16[128,2,32,128]{3,2,1,0:T(8,128)(2,1)} %all-to-all-done.3.part_ref, f32[65,2,32,128]{3,2,1,0:T(8,128)} %sum_slots.2.start_ref), custom_call_target="tpu_custom_call" | custom-call | flops 4000000 | bytes 6000000 | tf_op jit(solution)/shard_map/sum_slots/pallas_call | solution.py:357
  (53 shorter events, 13.5 us)
Async XLA Ops:
  0.6 30.2 %copy-start.1 = (bf16[64,2,32,128]{3,2,1,0:T(8,128)(2,1)S(1)}, bf16[64,2,32,128]{3,2,1,0:T(8,128)(2,1)}, u32[]{:S(2)}) copy-start(bf16[64,2,32,128]{3,2,1,0:T(8,128)(2,1)} %param.17) | copy-start | bytes 3145732
  33.0 5.6 %copy-start.3 = (pred[128,128]{1,0:T(32,128)(4,1)S(1)}, pred[128,128]{1,0:T(32,128)(4,1)}, u32[]{:S(2)}) copy-start(pred[128,128]{1,0:T(32,128)(4,1)} %constant.43.clone) | copy-start | bytes 49156
  33.0 5.8 %copy-start.5 = (s32[128,1]{0,1:T(1,128)S(1)}, s32[128,1]{0,1:T(1,128)}, u32[]{:S(2)}) copy-start(s32[128,1]{0,1:T(1,128)} %param.14) | copy-start | bytes 1540
  33.0 5.8 %copy-start.7 = (s32[128]{0:T(128)S(1)}, s32[128]{0:T(128)}, u32[]{:S(2)}) copy-start(s32[128]{0:T(128)} %param.16) | copy-start | bytes 1540
  33.0 6.0 %copy-start = (f32[128,1024]{1,0:T(8,128)S(1)}, f32[128,1024]{1,0:T(8,128)}, u32[]{:S(2)}) copy-start(f32[128,1024]{1,0:T(8,128)} %param.13) | copy-start | bytes 1572868
  33.0 35.1 %all-to-all-start.2 = ((bf16[128,2,32,128]{3,2,1,0:T(8,128)(2,1)}), bf16[128,2,32,128]{3,2,1,0:T(8,128)(2,1)}, u32[]{:S(2)}, u32[]{:S(2)}) async-start(bf16[128,2,32,128]{3,2,1,0:T(8,128)(2,1)} %gather_fusion.3), calls=%async_computation.2 | async-start | bytes 4194304 | tf_op jit(solution)/shard_map/all_to_all | solution.py:406
  40.6 4.3 %copy-start.2 = (bf16[32,2,32,32]{3,2,1,0:T(8,128)(2,1)S(1)}, bf16[32,2,32,32]{3,2,1,0:T(8,128)(2,1)}, u32[]{:S(2)}) copy-start(bf16[32,2,32,32]{3,2,1,0:T(8,128)(2,1)} %param.18) | copy-start | bytes 393220
  44.9 1.0 copy-start.4
  56.4 0.7 copy-start.6
  68.1 39.7 %all-to-all-start.1 = ((bf16[128,2,32,128]{3,2,1,0:T(8,128)(2,1)}), bf16[128,2,32,128]{3,2,1,0:T(8,128)(2,1)}, u32[]{:S(2)}, u32[]{:S(2)}) async-start(bf16[128,2,32,128]{3,2,1,0:T(8,128)(2,1)} %gather_fusion), calls=%async_computation.1 | async-start | bytes 4194304 | tf_op jit(solution)/shard_map/all_to_all | solution.py:406
  107.8 40.7 %all-to-all-start.4 = ((bf16[128,2,32,128]{3,2,1,0:T(8,128)(2,1)}), bf16[128,2,32,128]{3,2,1,0:T(8,128)(2,1)}, u32[]{:S(2)}, u32[]{:S(2)}) async-start(bf16[128,2,32,128]{3,2,1,0:T(8,128)(2,1)} %get-tuple-element.27), calls=%async_computation.4 | async-start | bytes 4194304 | tf_op jit(solution)/shard_map/all_to_all | solution.py:406
  148.5 39.6 %all-to-all-start.3 = ((bf16[128,2,32,128]{3,2,1,0:T(8,128)(2,1)}), bf16[128,2,32,128]{3,2,1,0:T(8,128)(2,1)}, u32[]{:S(2)}, u32[]{:S(2)}) async-start(bf16[128,2,32,128]{3,2,1,0:T(8,128)(2,1)} %get-tuple-element.26), calls=%async_computation.3 | async-start | bytes 4194304 | tf_op jit(solution)/shard_map/all_to_all | solution.py:406

commit v5 on v4

--- a/solution.py
+++ b/solution.py
@@ -373,15 +373,108 @@
     )(slots, scale, parts, start)
 
 
-def plan(target, blocks):
-    same = target[:, None] == target[None, :]
-    earlier = np.arange(blocks)[:, None] > np.arange(blocks)[None, :]
-    rank = jnp.sum(same & earlier, axis=1, dtype=jnp.int32)
-    double = jnp.sum(same, axis=1, dtype=jnp.int32) > 1
-    singles = jnp.sum(earlier & ~double[None, :], axis=1, dtype=jnp.int32)
-    spare = blocks // 2 - jnp.sum(double, dtype=jnp.int32) // 2
-    phase = jnp.where(double, rank, (singles >= spare).astype(jnp.int32))
-    return phase, earlier
+def ask_kernel(column_ref, row_ref, weight_ref, message_out, plan_ref, ready, held, send_sem, recv_sem):
+    blocks = row_ref.shape[1]
+    facets, size = lax.axis_size("facet"), lax.axis_size("vis")
+    groups = facets * size
+    me = lax.axis_index("facet") * size + lax.axis_index("vis")
+    barrier = pltpu.get_barrier_semaphore()
+
+    def device(turn):
+        peer = lax.rem(me + turn, groups)
+        return peer, (peer // size, lax.rem(peer, size))
+
+    def greet(turn, carry):
+        pl.semaphore_signal(barrier, inc=1, device_id=device(turn)[1], device_id_type=pl.DeviceIdType.MESH)
+        return carry
+
+    lax.fori_loop(1, groups, greet, 0)
+
+    square = (blocks, blocks)
+    down = lax.broadcasted_iota(jnp.int32, square, 0)
+    across = lax.broadcasted_iota(jnp.int32, square, 1)
+    one, zero = jnp.ones(square, F32), jnp.zeros(square, F32)
+    target_c, plane_c = column_ref[:, 0:1], column_ref[:, 1:2]
+    target_r, slot_r = row_ref[0:1], row_ref[1:2]
+    same = jnp.where(target_c == target_r, one, zero)
+    before = jnp.where(down < across, one, zero)
+    equal = jnp.where(down == across, one, zero)
+    rank = jnp.sum(same * before, axis=0, keepdims=True)
+    double_r = jnp.where(jnp.sum(same, axis=0, keepdims=True) > 1.5, 1.0, 0.0)
+    single_c = jnp.where(jnp.sum(same, axis=1, keepdims=True) > 1.5, 0.0, 1.0)
+    ahead = jnp.sum(before * single_c, axis=0, keepdims=True)
+    spare = 0.5 * blocks - 0.5 * jnp.sum(double_r, axis=1, keepdims=True)
+    phase_r = double_r * rank + (1.0 - double_r) * jnp.where(ahead > spare - 0.5, 1.0, 0.0)
+    asked = []
+    for turn in range(2):
+        mine = (down == target_r) & (jnp.abs(phase_r - turn) < 0.5)
+        asked.append(jnp.max(jnp.where(mine, slot_r.astype(F32), -1.0), axis=1, keepdims=True))
+    weight = jnp.sum(jnp.sum(weight_ref[...], axis=0, keepdims=True), axis=1, keepdims=True)
+    ready[...] = jnp.where(across == 0, asked[0], jnp.where(across == 1, asked[1], weight))
+
+    phase_c = jnp.sum(equal * phase_r, axis=1, keepdims=True)
+    alike = jnp.where(jnp.abs(phase_c - phase_r) < 0.5, one, zero)
+    place_r = phase_r * (0.5 * blocks) + jnp.sum(before * alike, axis=0, keepdims=True)
+    place_c = jnp.sum(equal * place_r, axis=1, keepdims=True)
+    at = jnp.where(jnp.abs(place_c - across.astype(F32)) < 0.5, one, zero)
+    rows = [
+        place_r,
+        jnp.sum(at * down.astype(F32), axis=0, keepdims=True),
+        jnp.sum(at * target_c.astype(F32), axis=0, keepdims=True),
+        jnp.sum(at * plane_c.astype(F32), axis=0, keepdims=True),
+    ]
+    plan_ref[...] = jnp.concatenate(rows + rows, axis=0).astype(jnp.int32)
+
+    pl.semaphore_wait(barrier, groups - 1)
+
+    def push(turn, carry):
+        peer, where = device(turn)
+        pltpu.make_async_remote_copy(
+            src_ref=ready.at[pl.ds(peer, 1)],
+            dst_ref=held.at[pl.ds(me, 1)],
+            send_sem=send_sem,
+            recv_sem=recv_sem,
+            device_id=where,
+            device_id_type=pl.DeviceIdType.MESH,
+        ).start()
+        return carry
+
+    lax.fori_loop(1, groups, push, 0)
+    everything = pltpu.make_async_remote_copy(
+        src_ref=ready.at[pl.ds(0, groups - 1)],
+        dst_ref=held.at[pl.ds(0, groups - 1)],
+        send_sem=send_sem,
+        recv_sem=recv_sem,
+        device_id=device(1)[1],
+        device_id_type=pl.DeviceIdType.MESH,
+    )
+    everything.wait_send()
+    everything.wait_recv()
+    message_out[...] = jnp.where(down == me, ready[...], held[...])
+
+
+def ask(block_group, tile_slot, w_plane, vis_weight):
+    blocks = tile_slot.shape[0]
+    groups = lax.axis_size(AXES)
+    columns = jnp.concatenate([block_group, w_plane[:, None]], axis=1)
+    rows = jnp.stack([block_group[:, 0], tile_slot])
+    return pl.pallas_call(
+        ask_kernel,
+        in_specs=[pl.BlockSpec(memory_space=pltpu.VMEM)] * 3,
+        out_specs=[pl.BlockSpec(memory_space=pltpu.VMEM)] * 2,
+        out_shape=[
+            jax.ShapeDtypeStruct((groups, 128), F32),
+            jax.ShapeDtypeStruct((8, blocks), jnp.int32),
+        ],
+        scratch_shapes=[
+            pltpu.VMEM((groups, 128), F32),
+            pltpu.VMEM((groups, 128), F32),
+            pltpu.SemaphoreType.DMA,
+            pltpu.SemaphoreType.DMA,
+        ],
+        compiler_params=pltpu.CompilerParams(collective_id=0, has_side_effects=True),
+        name="ask",
+    )(columns, rows, vis_weight)
 
 
 def shards(vis_obs, uv_coords, vis_weight, block_group, tile_slot, w_plane, model_tiles, w_kernels):
@@ -389,16 +482,8 @@
     groups = lax.axis_size(AXES)
     owned = model_tiles.shape[0]
     half = blocks // 2
-    target = block_group[:, 0]
-    phase, earlier = plan(target, blocks)
-    slot = jnp.arange(2 * groups, dtype=jnp.int32)
-    wanted = jnp.max(
-        jnp.where((target + phase * groups)[None, :] == slot[:, None], tile_slot[None, :], -1), axis=1
-    ).reshape(2, groups)
-    message = jnp.concatenate(
-        [wanted.astype(F32).T, jnp.full((groups, 1), jnp.sum(vis_weight))], axis=1
-    )
-    message = lax.all_to_all(message, AXES, split_axis=0, concat_axis=0, tiled=True)
+    message, plan = ask(block_group, tile_slot, w_plane, vis_weight)
+    place, order, position, planes = plan[0], plan[1], plan[2], plan[3]
     requested = message[:, :2].astype(jnp.int32)
     scale = (blocks * groups * nvis) / jnp.sum(message[:, 2])
 
@@ -410,17 +495,6 @@
         for turn in range(2)
     ]
     arrived = [exchange(chosen[0])]
-    place = phase * half + jnp.sum(
-        earlier & (phase[:, None] == phase[None, :]), axis=1, dtype=jnp.int32
-    )
-    at = place[None, :] == jnp.arange(blocks, dtype=jnp.int32)[:, None]
-
-    def ordered(values):
-        return jnp.sum(jnp.where(at, values[None, :], 0), axis=1, dtype=jnp.int32)
-
-    order = ordered(jnp.arange(blocks, dtype=jnp.int32))
-    position = ordered(target)
-    planes = ordered(w_plane)
     uv_sorted = jnp.take(uv_coords.transpose(1, 0, 2), order, axis=1, mode="clip")
     weight_sorted = jnp.take(vis_weight, order, axis=0, mode="clip")
     matrices = plane_matrices(w_kernels)

time: 197 us -> 190 us (0.964)
  blocking collectives: 20.9 us -> 0 us
  Pallas kernels: 75.7 us -> 94.2 us
  other arithmetic: 17.1 us -> 13.5 us
  between operations: 4.2 us -> 1.59 us
  waiting for transfers between devices: 11.5 us -> 13.6 us
    all_to_all x1 -> x0, blocking collectives: 20.9 us -> none  [shards(): lax.all_to_all(message, AXES, split_axis=0, concat_axis=0, tiled=True)]
    pallas_call x0 -> x1, Pallas kernels: none -> 18.6 us  [ask(): pl.pallas_call(ask_kernel, in_specs=[pl.BlockSpec(memory_space=pltpu.VMEM...]
    reduce_sum x6 -> x0, other arithmetic: 4.58 us -> none  [the longest x1 1.78 us: shards(): jnp.sum(vis_weight)]
    all_to_all x4, waiting for transfers between devices: 11.5 us -> 13.6 us  [exchange(): return lax.all_to_all(array, AXES, split_axis=0, concat_axis=0, tiled=True)]
  transfers between devices with their start and end apart: 4 -> 4, of which waited for: 2 -> 2; matrix products, arithmetic and copies ran while one was open for 21% -> 21% of each run, Pallas kernels for 35% -> 36%
where the time goes in v5:
time: 190 us; the launch traced here: 189 us
  Pallas kernels  94.2 us (50%)
  starting transfers between devices  33.6 us (18%)
  local copies, waits for them, and re-layouts  31.2 us (16%)
  waiting for transfers between devices  13.6 us (7%)
  other arithmetic  13.5 us (7%)
    pallas_call x2, Pallas kernels, degrid_grid(): pl.pallas_call(block_kernel, grid_spec=pltpu.PrefetchScalarGridSpec(num_s...  60.8 us
    all_to_all x4, starting transfers between devices, exchange(): return lax.all_to_all(array, AXES, split_axis=0, concat_axis=0, tiled=True)  33.6 us
    pallas_call x1, Pallas kernels, ask(): pl.pallas_call(ask_kernel, in_specs=[pl.BlockSpec(memory_space=pltpu.VMEM...  18.6 us
    pallas_call x2, Pallas kernels, sum_slots(): pl.pallas_call(sum_kernel, grid_spec=pltpu.PrefetchScalarGridSpec(num_sca...  14.8 us
    all_to_all x4, waiting for transfers between devices, exchange(): return lax.all_to_all(array, AXES, split_axis=0, concat_axis=0, tiled=True)  13.6 us
    gather x2, local copies, waits for them, and re-layouts, shards(): jnp.take(model_tiles, jnp.maximum(requested[:, turn], 0), axis=0, mode='c...  5.49 us
    reshape x1, local copies, waits for them, and re-layouts, shards(): jnp.take(residual, place, axis=0, mode='clip').reshape(vis_obs.shape)  5.16 us
    gather x1, local copies, waits for them, and re-layouts, shards(): jnp.take(residual, place, axis=0, mode='clip').reshape(vis_obs.shape)  4.95 us
  transfers between devices with their start and end apart: 4, of which 2 were waited for; matrix products, arithmetic and copies ran while one was open for 21% of the time, Pallas kernels for 36%

profile of v5, /device:TPU:1, one launch (start us, length us, event | category | flops | bytes accessed | tf_op | source)
XLA Modules:
  0.0 189.2 jit_solution(3704307962571108103)
XLA Ops:
  2.1 1.2 pad_add_fusion.1.row_ref
  3.3 18.6 %ask.1 = (f32[128,128]{1,0:T(8,128)}, s32[8,128]{1,0:T(8,128)}) custom-call(s32[128,2]{1,0:T(8,128)} %copy.30.column_ref, s32[2,128]{1,0:T(2,128)} %pad_add_fusion.1.row_ref, f32[128,1024]{1,0:T(8,128)} %weight_ref.1), custom_call_target="tpu_custom_call" | custom-call | tf_op jit(solution)/shard_map/ask/pallas_call | solution.py:461
  23.0 3.4 %gather_fusion.3 = bf16[128,2,32,128]{3,2,1,0:T(8,128)(2,1)} fusion(bf16[64,2,32,128]{3,2,1,0:T(8,128)(2,1)} %param.16, s32[1024]{0:T(1024)S(1)} %pad_clamp_fusion.1), kind=kCustom, calls=%fused_computation.3 | custom fusion | bytes 4194816 | tf_op jit(solution)/shard_map/jit(_take)/gather | solution.py:494
  26.3 7.3 %all-to-all-start.1 = ((bf16[128,2,32,128]{3,2,1,0:T(8,128)(2,1)}), bf16[128,2,32,128]{3,2,1,0:T(8,128)(2,1)}, u32[]{:S(2)}, u32[]{:S(2)}) async-start(bf16[128,2,32,128]{3,2,1,0:T(8,128)(2,1)} %gather_fusion.3), calls=%async_computation.1 | async-start | bytes 4194304 | tf_op jit(solution)/shard_map/all_to_all | solution.py:491
  34.7 1.6 gather_fusion.2
  36.4 3.0 %gather_fusion.1 = f32[128,2,1024]{2,1,0:T(2,128)S(1)} fusion(f32[2,128,1024]{2,0,1:T(2,128)} %bitcast.43, s32[1024]{0:T(1024)S(1)} %pad_clamp_fusion.2), kind=kCustom, calls=%fused_computation.1 | custom fusion | bytes 2097664 | tf_op jit(solution)/shard_map/jit(_take)/gather | solution.py:498
  39.4 1.3 copy.43
  40.7 2.1 %gather_fusion = bf16[128,2,32,128]{3,2,1,0:T(8,128)(2,1)} fusion(bf16[64,2,32,128]{3,2,1,0:T(8,128)(2,1)S(1)} %copy-done.1, s32[1024]{0:T(1024)S(1)} %pad_clamp_fusion.3), kind=kCustom, calls=%fused_computation | custom fusion | bytes 4194816 | tf_op jit(solution)/shard_map/jit(_take)/gather | solution.py:494
  42.9 1.5 reduce-precision_convert_fusion
  44.4 1.3 stack.17
  46.9 4.4 %maximum_bitcast_fusion = bf16[32,2,2,32,256]{4,2,3,0,1:T(2,128)(2,1)S(1)} fusion(bf16[32,1,32,2,256]{4,3,2,0,1:T(2,128)(2,1)} %stack.18, bf16[32,1,32,2,256]{4,3,2,0,1:T(2,128)(2,1)S(1)} %stack.17), kind=kLoop, calls=%fused_computation.9 | loop fusion | flops 1048576 | bytes 4194304 | tf_op jit(solution)/shard_map/transpose | solution.py:268
  51.9 3.8 %bitcast_select_fusion.refs_6_ = bf16[32,2,256,256]{3,2,1,0:T(8,128)(2,1)} fusion(pred[256,256]{1,0:T(8,128)(4,1)S(1)} %bitcast.44, bf16[32,2,2,32,256]{4,3,2,1,0:T(8,128)(2,1)S(1)} %copy.34), kind=kLoop, calls=%fused_computation.5 | loop fusion | flops 4194304 | bytes 10551296 | tf_op jit(solution)/shard_map/jit(_where)/select_n | solution.py:271
  57.4 5.6 %all-to-all-done.1.refs_3_ = bf16[128,2,32,128]{3,2,1,0:T(8,128)(2,1)} async-done(((bf16[128,2,32,128]{3,2,1,0:T(8,128)(2,1)}), bf16[128,2,32,128]{3,2,1,0:T(8,128)(2,1)}, u32[]{:S(2)}, u32[]{:S(2)}) %all-to-all-start.1) | async-done | bytes 2097184 | tf_op jit(solution)/shard_map/all_to_all | solution.py:491
  63.0 5.7 %all-to-all-start = ((bf16[128,2,32,128]{3,2,1,0:T(8,128)(2,1)}), bf16[128,2,32,128]{3,2,1,0:T(8,128)(2,1)}, u32[]{:S(2)}, u32[]{:S(2)}) async-start(bf16[128,2,32,128]{3,2,1,0:T(8,128)(2,1)} %gather_fusion), calls=%async_computation | async-start | bytes 4194304 | tf_op jit(solution)/shard_map/all_to_all | solution.py:491
  71.0 30.4 %degrid_grid_0.1 = (f32[128,8,1024]{2,1,0:T(8,128)}, bf16[128,2,32,128]{3,2,1,0:T(8,128)(2,1)}) custom-call(s32[64]{0:T(128)} %get-tuple-element.50.order_ref, s32[64]{0:T(128)} %get-tuple-element.53.pos_ref, s32[64]{0:T(128)} %get-tuple-element.46.plane_ref, f32[128,2,4,1024]{3,2,1,0:T(4,128)} %refs_0_.3, f32[2,128,1024]{2,1,0:T(8,128)} %bitcast.41, ...), custom_call_target="tpu_custom_call" | custom-call | flops 5120000000 | bytes 7680000 | tf_op jit(solution)/shard_map/degrid_grid_0/pallas_call | solution.py:302
  101.4 10.4 %all-to-all-start.3 = ((bf16[128,2,32,128]{3,2,1,0:T(8,128)(2,1)}), bf16[128,2,32,128]{3,2,1,0:T(8,128)(2,1)}, u32[]{:S(2)}, u32[]{:S(2)}) async-start(bf16[128,2,32,128]{3,2,1,0:T(8,128)(2,1)} %get-tuple-element.31), calls=%async_computation.3 | async-start | bytes 4194304 | tf_op jit(solution)/shard_map/all_to_all | solution.py:491
  111.8 30.4 %degrid_grid_1.1 = (f32[128,8,1024]{2,1,0:T(8,128)}, bf16[128,2,32,128]{3,2,1,0:T(8,128)(2,1)}) custom-call(s32[64]{0:T(128)} %get-tuple-element.51.order_ref, s32[64]{0:T(128)} %get-tuple-element.52.pos_ref, s32[64]{0:T(128)} %get-tuple-element.47.plane_ref, f32[128,2,4,1024]{3,2,1,0:T(4,128)} %refs_0_.3, ...), custom_call_target="tpu_custom_call", output_to_operand_aliasing={{0}: (10, {})} | custom-call | flops 5120000000 | bytes 7680000 | tf_op jit(solution)/shard_map/degrid_grid_1/pallas_call | solution.py:302
  142.2 10.3 %all-to-all-start.2 = ((bf16[128,2,32,128]{3,2,1,0:T(8,128)(2,1)}), bf16[128,2,32,128]{3,2,1,0:T(8,128)(2,1)}, u32[]{:S(2)}, u32[]{:S(2)}) async-start(bf16[128,2,32,128]{3,2,1,0:T(8,128)(2,1)} %get-tuple-element.30), calls=%async_computation.2 | async-start | bytes 4194304 | tf_op jit(solution)/shard_map/all_to_all | solution.py:491
  154.7 5.0 %gather_fusion.4 = f32[128,8,1024]{2,1,0:T(8,128)} fusion(f32[128,8,1024]{2,1,0:T(8,128)} %get-tuple-element.29, s32[1024]{0:T(1024)S(1)} %pad_clamp_fusion), kind=kCustom, calls=%fused_computation.4 | custom fusion | bytes 8389120 | tf_op jit(solution)/shard_map/jit(_take)/gather | solution.py:514
  159.6 5.2 %reshape.21 = f32[128,2,4,1024]{3,2,1,0:T(4,128)} reshape(f32[128,8,1024]{2,1,0:T(8,128)} %gather_fusion.4) | data formatting | bytes 8388608 | tf_op jit(solution)/shard_map/reshape | solution.py:514
  164.8 1.6 broadcast_in_dim.63.start_ref
  166.4 7.4 %sum_slots.2.start_ref = f32[65,2,32,128]{3,2,1,0:T(8,128)} custom-call(s32[128]{0:T(128)} %get-tuple-element.32.slot_ref, f32[1]{0:T(128)} %constant.6.clone.1.scale_ref, bf16[128,2,32,128]{3,2,1,0:T(8,128)(2,1)} %all-to-all-done.3.part_ref, f32[65,2,32,128]{3,2,1,0:T(8,128)} %broadcast_in_dim.63.start_ref), custom_call_target="tpu_custom_call" | custom-call | flops 4000000 | bytes 6000000 | tf_op jit(solution)/shard_map/sum_slots/pallas_call | solution.py:357
  173.8 8.0 %all-to-all-done.2.part_ref = bf16[128,2,32,128]{3,2,1,0:T(8,128)(2,1)} async-done(((bf16[128,2,32,128]{3,2,1,0:T(8,128)(2,1)}), bf16[128,2,32,128]{3,2,1,0:T(8,128)(2,1)}, u32[]{:S(2)}, u32[]{:S(2)}) %all-to-all-start.2) | async-done | bytes 2097184 | tf_op jit(solution)/shard_map/all_to_all | solution.py:491
  181.8 7.4 %sum_slots.3 = f32[64,2,32,128]{3,2,1,0:T(8,128)} custom-call(s32[128]{0:T(128)} %get-tuple-element.33.slot_ref, f32[1]{0:T(128)} %bitcast.19.scale_ref, bf16[128,2,32,128]{3,2,1,0:T(8,128)(2,1)} %all-to-all-done.2.part_ref, f32[65,2,32,128]{3,2,1,0:T(8,128)} %sum_slots.2.start_ref), custom_call_target="tpu_custom_call" | custom-call | flops 4000000 | bytes 6000000 | tf_op jit(solution)/shard_map/sum_slots/pallas_call | solution.py:357
  (44 shorter events, 10.9 us)
Async XLA Ops:
  26.3 7.3 %copy-start.2 = (bf16[32,2,32,32]{3,2,1,0:T(8,128)(2,1)S(1)}, bf16[32,2,32,32]{3,2,1,0:T(8,128)(2,1)}, u32[]{:S(2)}) copy-start(bf16[32,2,32,32]{3,2,1,0:T(8,128)(2,1)} %param.17) | copy-start | bytes 393220
  26.3 36.7 %all-to-all-start.1 = ((bf16[128,2,32,128]{3,2,1,0:T(8,128)(2,1)}), bf16[128,2,32,128]{3,2,1,0:T(8,128)(2,1)}, u32[]{:S(2)}, u32[]{:S(2)}) async-start(bf16[128,2,32,128]{3,2,1,0:T(8,128)(2,1)} %gather_fusion.3), calls=%async_computation.1 | async-start | bytes 4194304 | tf_op jit(solution)/shard_map/all_to_all | solution.py:491
  33.6 1.1 copy-start.7
  33.7 1.1 copy-start
  36.4 4.3 %copy-start.1 = (bf16[64,2,32,128]{3,2,1,0:T(8,128)(2,1)S(1)}, bf16[64,2,32,128]{3,2,1,0:T(8,128)(2,1)}, u32[]{:S(2)}) copy-start(bf16[64,2,32,128]{3,2,1,0:T(8,128)(2,1)} %param.16) | copy-start | bytes 3145732
  40.7 2.2 %copy-start.3 = (bf16[32,2,32,32]{3,2,1,0:T(8,128)(2,1)S(1)}, bf16[32,2,32,32]{3,2,1,0:T(8,128)(2,1)}, u32[]{:S(2)}) copy-start(bf16[32,2,32,32]{3,2,1,0:T(8,128)(2,1)} %param.17) | copy-start | bytes 393220
  40.7 2.2 %copy-start.5 = (bf16[2,32,512,1]{2,1,0,3:T(8,128)(2,1)S(1)}, bf16[2,32,512,1]{2,1,0,3:T(8,128)(2,1)}, u32[]{:S(2)}) copy-start(bf16[2,32,512,1]{2,1,0,3:T(8,128)(2,1)} %constant.24) | copy-start | bytes 196612
  51.2 0.7 copy-start.6
  63.0 38.4 %all-to-all-start = ((bf16[128,2,32,128]{3,2,1,0:T(8,128)(2,1)}), bf16[128,2,32,128]{3,2,1,0:T(8,128)(2,1)}, u32[]{:S(2)}, u32[]{:S(2)}) async-start(bf16[128,2,32,128]{3,2,1,0:T(8,128)(2,1)} %gather_fusion), calls=%async_computation | async-start | bytes 4194304 | tf_op jit(solution)/shard_map/all_to_all | solution.py:491
  101.4 40.8 %all-to-all-start.3 = ((bf16[128,2,32,128]{3,2,1,0:T(8,128)(2,1)}), bf16[128,2,32,128]{3,2,1,0:T(8,128)(2,1)}, u32[]{:S(2)}, u32[]{:S(2)}) async-start(bf16[128,2,32,128]{3,2,1,0:T(8,128)(2,1)} %get-tuple-element.31), calls=%async_computation.3 | async-start | bytes 4194304 | tf_op jit(solution)/shard_map/all_to_all | solution.py:491
  142.2 10.3 %copy-start.4 = (f32[128,128]{1,0:T(8,128)S(1)}, f32[128,128]{1,0:T(8,128)}, u32[]{:S(2)}) copy-start(f32[128,128]{1,0:T(8,128)} %get-tuple-element.17) | copy-start | bytes 196612
  142.2 39.6 %all-to-all-start.2 = ((bf16[128,2,32,128]{3,2,1,0:T(8,128)(2,1)}), bf16[128,2,32,128]{3,2,1,0:T(8,128)(2,1)}, u32[]{:S(2)}, u32[]{:S(2)}) async-start(bf16[128,2,32,128]{3,2,1,0:T(8,128)(2,1)} %get-tuple-element.30), calls=%async_computation.2 | async-start | bytes 4194304 | tf_op jit(solution)/shard_map/all_to_all | solution.py:491

commit v6 on v5

--- a/solution.py
+++ b/solution.py
@@ -11,7 +11,7 @@
 BF = jnp.bfloat16
 F32 = jnp.float32
 STEP = 8
-CHUNK = 256
+CHUNK = 512
 
 
 def even_fit(func, terms):
@@ -131,8 +131,7 @@
         )
         pairs.append(split(left))
     large = [nn_dot(jnp.concatenate(pair, axis=0), m) for pair, m in zip(pairs, tops)]
-    tiny = [nn_dot(pair[0], m) for pair, m in zip(pairs, rests)]
-    return [(x[:32] + x[32:] + y).astype(BF) for x, y in zip(large, tiny)]
+    return [(x[:32] + x[32:]).astype(BF) for x in large]
 
 
 def backward(growns, lefts, tops, rests):
@@ -331,50 +330,49 @@
     )(order, position, planes, *operands)
 
 
-def sum_kernel(slot_ref, scale_ref, part_ref, start_ref, out_ref, total):
+def sum_kernel(slot_ref, part_ref, start_ref, out_ref):
     step = pl.program_id(0)
     count = part_ref.shape[0]
 
     @pl.when(step == 0)
     def _():
-        total[...] = start_ref[...]
+        out_ref[...] = start_ref[...]
 
     def add(i, carry):
         slot = slot_ref[step * count + i]
-        total[slot] = total[slot] + part_ref[i].astype(F32)
+        part = jnp.where(slot >= 0, part_ref[i].astype(F32), 0.0)
+        row = jnp.maximum(slot, 0)
+        out_ref[row] = out_ref[row] + part
         return carry
 
-    lax.fori_loop(0, count, add, 0, unroll=4)
-
-    @pl.when(step == pl.num_programs(0) - 1)
-    def _():
-        out_ref[...] = total[: out_ref.shape[0]] * scale_ref[0]
-
-
-def sum_slots(slots, scale, parts, start, rows):
-    count = parts.shape[0] // 8
+    lax.fori_loop(0, count, add, 0, unroll=8)
+
+
+def sum_slots(slots, parts, start):
+    steps = 2
+    count = parts.shape[0] // steps
     shape = parts.shape[1:]
+
+    def whole():
+        return pl.BlockSpec(start.shape, lambda i, *_: (0, 0, 0, 0), pipeline_mode=pl.Buffered(1))
+
     return pl.pallas_call(
         sum_kernel,
         grid_spec=pltpu.PrefetchScalarGridSpec(
-            num_scalar_prefetch=2,
-            grid=(8,),
-            in_specs=[
-                pl.BlockSpec((count,) + shape, lambda i, *_: (i, 0, 0, 0)),
-                pl.BlockSpec(start.shape, lambda i, *_: (0, 0, 0, 0), pipeline_mode=pl.Buffered(1)),
-            ],
-            out_specs=pl.BlockSpec((rows,) + shape, lambda i, *_: (0, 0, 0, 0), pipeline_mode=pl.Buffered(1)),
-            scratch_shapes=[pltpu.VMEM(start.shape, F32)],
+            num_scalar_prefetch=1,
+            grid=(steps,),
+            in_specs=[pl.BlockSpec((count,) + shape, lambda i, *_: (i, 0, 0, 0)), whole()],
+            out_specs=whole(),
         ),
-        out_shape=jax.ShapeDtypeStruct((rows,) + shape, F32),
+        out_shape=jax.ShapeDtypeStruct(start.shape, F32),
         compiler_params=pltpu.CompilerParams(vmem_limit_bytes=63 << 20),
         cost_estimate=pl.CostEstimate(flops=4_000_000, bytes_accessed=6_000_000, transcendentals=0),
         name="sum_slots",
-    )(slots, scale, parts, start)
-
-
-def ask_kernel(column_ref, row_ref, weight_ref, message_out, plan_ref, ready, held, send_sem, recv_sem):
-    blocks = row_ref.shape[1]
+    )(slots, parts, start)
+
+
+def ask_kernel(target_ref, slot_ref, plane_ref, weight_ref, message_out, sorted_ref, ready, held, send_sem, recv_sem):
+    blocks = target_ref.shape[1]
     facets, size = lax.axis_size("facet"), lax.axis_size("vis")
     groups = facets * size
     me = lax.axis_index("facet") * size + lax.axis_index("vis")
@@ -394,11 +392,15 @@
     down = lax.broadcasted_iota(jnp.int32, square, 0)
     across = lax.broadcasted_iota(jnp.int32, square, 1)
     one, zero = jnp.ones(square, F32), jnp.zeros(square, F32)
-    target_c, plane_c = column_ref[:, 0:1], column_ref[:, 1:2]
-    target_r, slot_r = row_ref[0:1], row_ref[1:2]
-    same = jnp.where(target_c == target_r, one, zero)
     before = jnp.where(down < across, one, zero)
     equal = jnp.where(down == across, one, zero)
+
+    def turned(row):
+        return jnp.sum(equal * row, axis=1, keepdims=True)
+
+    target_r, slot_r = target_ref[...].astype(F32), slot_ref[...].astype(F32)
+    target_c, plane_c = turned(target_r), turned(plane_ref[...].astype(F32))
+    same = jnp.where(jnp.abs(target_c - target_r) < 0.5, one, zero)
     rank = jnp.sum(same * before, axis=0, keepdims=True)
     double_r = jnp.where(jnp.sum(same, axis=0, keepdims=True) > 1.5, 1.0, 0.0)
     single_c = jnp.where(jnp.sum(same, axis=1, keepdims=True) > 1.5, 0.0, 1.0)
@@ -407,23 +409,23 @@
     phase_r = double_r * rank + (1.0 - double_r) * jnp.where(ahead > spare - 0.5, 1.0, 0.0)
     asked = []
     for turn in range(2):
-        mine = (down == target_r) & (jnp.abs(phase_r - turn) < 0.5)
-        asked.append(jnp.max(jnp.where(mine, slot_r.astype(F32), -1.0), axis=1, keepdims=True))
+        mine = (jnp.abs(down.astype(F32) - target_r) < 0.5) & (jnp.abs(phase_r - turn) < 0.5)
+        asked.append(jnp.max(jnp.where(mine, slot_r, -1.0), axis=1, keepdims=True))
     weight = jnp.sum(jnp.sum(weight_ref[...], axis=0, keepdims=True), axis=1, keepdims=True)
     ready[...] = jnp.where(across == 0, asked[0], jnp.where(across == 1, asked[1], weight))
 
-    phase_c = jnp.sum(equal * phase_r, axis=1, keepdims=True)
+    phase_c = turned(phase_r)
     alike = jnp.where(jnp.abs(phase_c - phase_r) < 0.5, one, zero)
     place_r = phase_r * (0.5 * blocks) + jnp.sum(before * alike, axis=0, keepdims=True)
-    place_c = jnp.sum(equal * place_r, axis=1, keepdims=True)
+    place_c = turned(place_r)
     at = jnp.where(jnp.abs(place_c - across.astype(F32)) < 0.5, one, zero)
     rows = [
         place_r,
         jnp.sum(at * down.astype(F32), axis=0, keepdims=True),
-        jnp.sum(at * target_c.astype(F32), axis=0, keepdims=True),
-        jnp.sum(at * plane_c.astype(F32), axis=0, keepdims=True),
+        jnp.sum(at * target_c, axis=0, keepdims=True),
+        jnp.sum(at * plane_c, axis=0, keepdims=True),
     ]
-    plan_ref[...] = jnp.concatenate(rows + rows, axis=0).astype(jnp.int32)
+    sorted_ref[...] = jnp.concatenate(rows + rows, axis=0).astype(jnp.int32)
 
     pl.semaphore_wait(barrier, groups - 1)
 
@@ -456,11 +458,10 @@
 def ask(block_group, tile_slot, w_plane, vis_weight):
     blocks = tile_slot.shape[0]
     groups = lax.axis_size(AXES)
-    columns = jnp.concatenate([block_group, w_plane[:, None]], axis=1)
-    rows = jnp.stack([block_group[:, 0], tile_slot])
+    rows = [array.reshape(1, blocks) for array in (block_group, tile_slot, w_plane)]
     return pl.pallas_call(
         ask_kernel,
-        in_specs=[pl.BlockSpec(memory_space=pltpu.VMEM)] * 3,
+        in_specs=[pl.BlockSpec(memory_space=pltpu.VMEM)] * 4,
         out_specs=[pl.BlockSpec(memory_space=pltpu.VMEM)] * 2,
         out_shape=[
             jax.ShapeDtypeStruct((groups, 128), F32),
@@ -474,13 +475,12 @@
         ],
         compiler_params=pltpu.CompilerParams(collective_id=0, has_side_effects=True),
         name="ask",
-    )(columns, rows, vis_weight)
+    )(*rows, vis_weight)
 
 
 def shards(vis_obs, uv_coords, vis_weight, block_group, tile_slot, w_plane, model_tiles, w_kernels):
     blocks, nvis = vis_weight.shape
     groups = lax.axis_size(AXES)
-    owned = model_tiles.shape[0]
     half = blocks // 2
     message, plan = ask(block_group, tile_slot, w_plane, vis_weight)
     place, order, position, planes = plan[0], plan[1], plan[2], plan[3]
@@ -496,7 +496,7 @@
     ]
     arrived = [exchange(chosen[0])]
     uv_sorted = jnp.take(uv_coords.transpose(1, 0, 2), order, axis=1, mode="clip")
-    weight_sorted = jnp.take(vis_weight, order, axis=0, mode="clip")
+    weight_sorted = jnp.take(vis_weight, order, axis=0, mode="clip") * scale
     matrices = plane_matrices(w_kernels)
     late, matrices, uv_sorted, weight_sorted, order, position, planes = lax.optimization_barrier(
         (chosen[1], matrices, uv_sorted, weight_sorted, order, position, planes)
@@ -512,11 +512,8 @@
         )
         returned.append(exchange(outgoing))
     residual = jnp.take(residual, place, axis=0, mode="clip").reshape(vis_obs.shape)
-    slots = jnp.where(requested < 0, owned, requested)
-    start = jnp.zeros((owned + 1,) + model_tiles.shape[1:], F32)
-    one = jnp.ones((1,), F32)
-    partial = sum_slots(slots[:, 0], one, returned[0], start, owned + 1)
-    return residual, sum_slots(slots[:, 1], scale.reshape(1), returned[1], partial, owned)
+    partial = sum_slots(requested[:, 0], returned[0], jnp.zeros(model_tiles.shape, F32))
+    return residual, sum_slots(requested[:, 1], returned[1], partial)
 
 
 def solution(mesh):

time: 190 us -> 184 us (0.968)
  Pallas kernels: 94.2 us -> 86.2 us
  waiting for transfers between devices: 13.6 us -> 16.3 us
    pallas_call x2, Pallas kernels: 14.8 us -> 9.74 us  [sum_slots(): pl.pallas_call(sum_kernel, grid_spec=pltpu.PrefetchScalarGridSpec(num_sca...]
    pallas_call x2, Pallas kernels: 60.8 us -> 57.7 us  [degrid_grid(): pl.pallas_call(block_kernel, grid_spec=pltpu.PrefetchScalarGridSpec(num_s...]
    all_to_all x4, waiting for transfers between devices: 13.6 us -> 16.3 us  [exchange(): return lax.all_to_all(array, AXES, split_axis=0, concat_axis=0, tiled=True)]
  transfers between devices with their start and end apart: 4 -> 4, of which waited for: 2 -> 3; matrix products, arithmetic and copies ran while one was open for 21% -> 21% of each run, Pallas kernels for 36% -> 34%
where the time goes in v6:
time: 184 us; the launch traced here: 183 us
  Pallas kernels  86.2 us (47%)
  starting transfers between devices  34.4 us (19%)
  local copies, waits for them, and re-layouts  29.8 us (16%)
  waiting for transfers between devices  16.3 us (9%)
  other arithmetic  13 us (7%)
    pallas_call x2, Pallas kernels, degrid_grid(): pl.pallas_call(block_kernel, grid_spec=pltpu.PrefetchScalarGridSpec(num_s...  57.7 us
    all_to_all x4, starting transfers between devices, exchange(): return lax.all_to_all(array, AXES, split_axis=0, concat_axis=0, tiled=True)  34.4 us
    pallas_call x1, Pallas kernels, ask(): pl.pallas_call(ask_kernel, in_specs=[pl.BlockSpec(memory_space=pltpu.VMEM...  18.7 us
    all_to_all x4, waiting for transfers between devices, exchange(): return lax.all_to_all(array, AXES, split_axis=0, concat_axis=0, tiled=True)  16.3 us
    pallas_call x2, Pallas kernels, sum_slots(): pl.pallas_call(sum_kernel, grid_spec=pltpu.PrefetchScalarGridSpec(num_sca...  9.74 us
    gather x2, local copies, waits for them, and re-layouts, shards(): jnp.take(model_tiles, jnp.maximum(requested[:, turn], 0), axis=0, mode='c...  5.49 us
    reshape x1, local copies, waits for them, and re-layouts, shards(): jnp.take(residual, place, axis=0, mode='clip').reshape(vis_obs.shape)  5.16 us
    gather x1, local copies, waits for them, and re-layouts, shards(): jnp.take(residual, place, axis=0, mode='clip').reshape(vis_obs.shape)  4.96 us
  transfers between devices with their start and end apart: 4, of which 3 were waited for; matrix products, arithmetic and copies ran while one was open for 21% of the time, Pallas kernels for 34%

profile of v6, /device:TPU:1, one launch (start us, length us, event | category | flops | bytes accessed | tf_op | source)
XLA Modules:
  0.0 182.8 jit_solution(7736216584985661516)
XLA Ops:
  0.6 18.7 %ask.1 = (f32[128,128]{1,0:T(8,128)}, s32[8,128]{1,0:T(8,128)}) custom-call(s32[1,128]{1,0:T(1,128)} %bitcast.44, s32[1,128]{1,0:T(1,128)} %bitcast.45, s32[1,128]{1,0:T(1,128)} %bitcast.46, f32[128,1024]{1,0:T(8,128)} %weight_ref.1), custom_call_target="tpu_custom_call" | custom-call | tf_op jit(solution)/shard_map/ask/pallas_call | solution.py:462
  20.9 3.4 %gather_fusion.3 = bf16[128,2,32,128]{3,2,1,0:T(8,128)(2,1)} fusion(bf16[64,2,32,128]{3,2,1,0:T(8,128)(2,1)} %param.16, s32[1024]{0:T(1024)S(1)} %pad_clamp_fusion.1), kind=kCustom, calls=%fused_computation.3 | custom fusion | bytes 4194816 | tf_op jit(solution)/shard_map/jit(_take)/gather | solution.py:494
  24.2 7.3 %all-to-all-start.1 = ((bf16[128,2,32,128]{3,2,1,0:T(8,128)(2,1)}), bf16[128,2,32,128]{3,2,1,0:T(8,128)(2,1)}, u32[]{:S(2)}, u32[]{:S(2)}) async-start(bf16[128,2,32,128]{3,2,1,0:T(8,128)(2,1)} %gather_fusion.3), calls=%async_computation.1 | async-start | bytes 4194304 | tf_op jit(solution)/shard_map/all_to_all | solution.py:491
  32.6 1.6 gather_fusion.2
  34.2 3.0 %gather_fusion.1 = f32[128,2,1024]{2,1,0:T(2,128)S(1)} fusion(f32[2,128,1024]{2,0,1:T(2,128)} %bitcast.42, s32[1024]{0:T(1024)S(1)} %pad_clamp_fusion.2), kind=kCustom, calls=%fused_computation.1 | custom fusion | bytes 2097664 | tf_op jit(solution)/shard_map/jit(_take)/gather | solution.py:498
  37.2 1.3 copy.31
  38.6 2.1 %gather_fusion = bf16[128,2,32,128]{3,2,1,0:T(8,128)(2,1)} fusion(bf16[64,2,32,128]{3,2,1,0:T(8,128)(2,1)S(1)} %copy-done.1, s32[1024]{0:T(1024)S(1)} %pad_clamp_fusion.3), kind=kCustom, calls=%fused_computation | custom fusion | bytes 4194816 | tf_op jit(solution)/shard_map/jit(_take)/gather | solution.py:494
  40.7 1.5 reduce-precision_convert_fusion
  42.2 1.3 stack.10
  43.6 1.1 stack.9
  44.7 4.4 %maximum_bitcast_fusion = bf16[32,2,2,32,256]{4,2,3,0,1:T(2,128)(2,1)S(1)} fusion(bf16[32,1,32,2,256]{4,3,2,0,1:T(2,128)(2,1)S(1)} %stack.10, bf16[32,1,32,2,256]{4,3,2,0,1:T(2,128)(2,1)} %stack.9), kind=kLoop, calls=%fused_computation.9 | loop fusion | flops 1048576 | bytes 4194304 | tf_op jit(solution)/shard_map/transpose | solution.py:267
  51.3 3.8 %bitcast_select_fusion.refs_6_ = bf16[32,2,256,256]{3,2,1,0:T(8,128)(2,1)} fusion(pred[256,256]{1,0:T(8,128)(4,1)S(1)} %bitcast.43, bf16[32,2,2,32,256]{4,3,2,1,0:T(8,128)(2,1)S(1)} %copy.22), kind=kLoop, calls=%fused_computation.5 | loop fusion | flops 4194304 | bytes 10551296 | tf_op jit(solution)/shard_map/jit(_where)/select_n | solution.py:270
  57.7 3.1 %all-to-all-done.1.refs_3_ = bf16[128,2,32,128]{3,2,1,0:T(8,128)(2,1)} async-done(((bf16[128,2,32,128]{3,2,1,0:T(8,128)(2,1)}), bf16[128,2,32,128]{3,2,1,0:T(8,128)(2,1)}, u32[]{:S(2)}, u32[]{:S(2)}) %all-to-all-start.1) | async-done | bytes 2097184 | tf_op jit(solution)/shard_map/all_to_all | solution.py:491
  60.9 7.1 %all-to-all-start = ((bf16[128,2,32,128]{3,2,1,0:T(8,128)(2,1)}), bf16[128,2,32,128]{3,2,1,0:T(8,128)(2,1)}, u32[]{:S(2)}, u32[]{:S(2)}) async-start(bf16[128,2,32,128]{3,2,1,0:T(8,128)(2,1)} %gather_fusion), calls=%async_computation | async-start | bytes 4194304 | tf_op jit(solution)/shard_map/all_to_all | solution.py:491
  70.3 28.9 %degrid_grid_0.1 = (f32[128,8,1024]{2,1,0:T(8,128)}, bf16[128,2,32,128]{3,2,1,0:T(8,128)(2,1)}) custom-call(s32[64]{0:T(128)} %get-tuple-element.50.order_ref, s32[64]{0:T(128)} %get-tuple-element.53.pos_ref, s32[64]{0:T(128)} %get-tuple-element.46.plane_ref, f32[128,2,4,1024]{3,2,1,0:T(4,128)} %refs_0_.3, f32[2,128,1024]{2,1,0:T(8,128)} %bitcast.40, ...), custom_call_target="tpu_custom_call" | custom-call | flops 5120000000 | bytes 7680000 | tf_op jit(solution)/shard_map/degrid_grid_0/pallas_call | solution.py:301
  99.2 10.2 %all-to-all-start.3 = ((bf16[128,2,32,128]{3,2,1,0:T(8,128)(2,1)}), bf16[128,2,32,128]{3,2,1,0:T(8,128)(2,1)}, u32[]{:S(2)}, u32[]{:S(2)}) async-start(bf16[128,2,32,128]{3,2,1,0:T(8,128)(2,1)} %get-tuple-element.31), calls=%async_computation.3 | async-start | bytes 4194304 | tf_op jit(solution)/shard_map/all_to_all | solution.py:491
  109.4 28.9 %degrid_grid_1.1 = (f32[128,8,1024]{2,1,0:T(8,128)}, bf16[128,2,32,128]{3,2,1,0:T(8,128)(2,1)}) custom-call(s32[64]{0:T(128)} %get-tuple-element.51.order_ref, s32[64]{0:T(128)} %get-tuple-element.52.pos_ref, s32[64]{0:T(128)} %get-tuple-element.47.plane_ref, f32[128,2,4,1024]{3,2,1,0:T(4,128)} %refs_0_.3, ...), custom_call_target="tpu_custom_call", output_to_operand_aliasing={{0}: (10, {})} | custom-call | flops 5120000000 | bytes 7680000 | tf_op jit(solution)/shard_map/degrid_grid_1/pallas_call | solution.py:301
  138.7 9.8 %all-to-all-start.2 = ((bf16[128,2,32,128]{3,2,1,0:T(8,128)(2,1)}), bf16[128,2,32,128]{3,2,1,0:T(8,128)(2,1)}, u32[]{:S(2)}, u32[]{:S(2)}) async-start(bf16[128,2,32,128]{3,2,1,0:T(8,128)(2,1)} %get-tuple-element.30), calls=%async_computation.2 | async-start | bytes 4194304 | tf_op jit(solution)/shard_map/all_to_all | solution.py:491
  148.6 5.0 %gather_fusion.4 = f32[128,8,1024]{2,1,0:T(8,128)} fusion(f32[128,8,1024]{2,1,0:T(8,128)} %get-tuple-element.29, s32[1024]{0:T(1024)S(1)} %pad_clamp_fusion), kind=kCustom, calls=%fused_computation.4 | custom fusion | bytes 8389120 | tf_op jit(solution)/shard_map/jit(_take)/gather | solution.py:514
  153.5 5.2 %reshape.30 = f32[128,2,4,1024]{3,2,1,0:T(4,128)} reshape(f32[128,8,1024]{2,1,0:T(8,128)} %gather_fusion.4) | data formatting | bytes 8388608 | tf_op jit(solution)/shard_map/reshape | solution.py:514
  158.7 1.6 broadcast_in_dim.54.start_ref
  160.3 4.9 %sum_slots.2.start_ref = f32[64,2,32,128]{3,2,1,0:T(8,128)} custom-call(s32[128]{0:T(128)} %get-tuple-element.32.slot_ref, bf16[128,2,32,128]{3,2,1,0:T(8,128)(2,1)} %all-to-all-done.3.part_ref, f32[64,2,32,128]{3,2,1,0:T(8,128)} %broadcast_in_dim.54.start_ref), custom_call_target="tpu_custom_call" | custom-call | flops 4000000 | bytes 6000000 | tf_op jit(solution)/shard_map/sum_slots/pallas_call | solution.py:359
  165.2 12.7 %all-to-all-done.2.part_ref = bf16[128,2,32,128]{3,2,1,0:T(8,128)(2,1)} async-done(((bf16[128,2,32,128]{3,2,1,0:T(8,128)(2,1)}), bf16[128,2,32,128]{3,2,1,0:T(8,128)(2,1)}, u32[]{:S(2)}, u32[]{:S(2)}) %all-to-all-start.2) | async-done | bytes 2097184 | tf_op jit(solution)/shard_map/all_to_all | solution.py:491
  177.9 4.9 %sum_slots.3 = f32[64,2,32,128]{3,2,1,0:T(8,128)} custom-call(s32[128]{0:T(128)} %get-tuple-element.33.slot_ref, bf16[128,2,32,128]{3,2,1,0:T(8,128)(2,1)} %all-to-all-done.2.part_ref, f32[64,2,32,128]{3,2,1,0:T(8,128)} %sum_slots.2.start_ref), custom_call_target="tpu_custom_call" | custom-call | flops 4000000 | bytes 6000000 | tf_op jit(solution)/shard_map/sum_slots/pallas_call | solution.py:359
  (42 shorter events, 9.5 us)
Async XLA Ops:
  24.2 7.3 %copy-start.3 = (bf16[32,2,32,32]{3,2,1,0:T(8,128)(2,1)S(1)}, bf16[32,2,32,32]{3,2,1,0:T(8,128)(2,1)}, u32[]{:S(2)}) copy-start(bf16[32,2,32,32]{3,2,1,0:T(8,128)(2,1)} %param.17) | copy-start | bytes 393220
  24.2 36.6 %all-to-all-start.1 = ((bf16[128,2,32,128]{3,2,1,0:T(8,128)(2,1)}), bf16[128,2,32,128]{3,2,1,0:T(8,128)(2,1)}, u32[]{:S(2)}, u32[]{:S(2)}) async-start(bf16[128,2,32,128]{3,2,1,0:T(8,128)(2,1)} %gather_fusion.3), calls=%async_computation.1 | async-start | bytes 4194304 | tf_op jit(solution)/shard_map/all_to_all | solution.py:491
  31.5 1.1 copy-start.8
  31.6 1.1 copy-start
  34.2 4.3 %copy-start.1 = (bf16[64,2,32,128]{3,2,1,0:T(8,128)(2,1)S(1)}, bf16[64,2,32,128]{3,2,1,0:T(8,128)(2,1)}, u32[]{:S(2)}) copy-start(bf16[64,2,32,128]{3,2,1,0:T(8,128)(2,1)} %param.16) | copy-start | bytes 3145732
  38.5 2.2 %copy-start.4 = (bf16[32,2,32,32]{3,2,1,0:T(8,128)(2,1)S(1)}, bf16[32,2,32,32]{3,2,1,0:T(8,128)(2,1)}, u32[]{:S(2)}) copy-start(bf16[32,2,32,32]{3,2,1,0:T(8,128)(2,1)} %param.17) | copy-start | bytes 393220
  38.6 2.2 %copy-start.6 = (bf16[2,32,512,1]{2,1,0,3:T(8,128)(2,1)S(1)}, bf16[2,32,512,1]{2,1,0,3:T(8,128)(2,1)}, u32[]{:S(2)}) copy-start(bf16[2,32,512,1]{2,1,0,3:T(8,128)(2,1)} %constant.19) | copy-start | bytes 196612
  49.1 0.8 copy-start.5
  49.1 2.2 %copy-start.7 = (pred[4,256]{1,0:T(4,128)(4,1)S(1)}, pred[4,256]{1,0:T(4,128)(4,1)}, u32[]{:S(2)}) copy-start(pred[4,256]{1,0:T(4,128)(4,1)} %constant.18) | copy-start | bytes 3076
  55.3 1.6 copy-start.2
  60.9 38.3 %all-to-all-start = ((bf16[128,2,32,128]{3,2,1,0:T(8,128)(2,1)}), bf16[128,2,32,128]{3,2,1,0:T(8,128)(2,1)}, u32[]{:S(2)}, u32[]{:S(2)}) async-start(bf16[128,2,32,128]{3,2,1,0:T(8,128)(2,1)} %gather_fusion), calls=%async_computation | async-start | bytes 4194304 | tf_op jit(solution)/shard_map/all_to_all | solution.py:491
  99.2 39.6 %all-to-all-start.3 = ((bf16[128,2,32,128]{3,2,1,0:T(8,128)(2,1)}), bf16[128,2,32,128]{3,2,1,0:T(8,128)(2,1)}, u32[]{:S(2)}, u32[]{:S(2)}) async-start(bf16[128,2,32,128]{3,2,1,0:T(8,128)(2,1)} %get-tuple-element.31), calls=%async_computation.3 | async-start | bytes 4194304 | tf_op jit(solution)/shard_map/all_to_all | solution.py:491
  138.7 39.1 %all-to-all-start.2 = ((bf16[128,2,32,128]{3,2,1,0:T(8,128)(2,1)}), bf16[128,2,32,128]{3,2,1,0:T(8,128)(2,1)}, u32[]{:S(2)}, u32[]{:S(2)}) async-start(bf16[128,2,32,128]{3,2,1,0:T(8,128)(2,1)} %get-tuple-element.30), calls=%async_computation.2 | async-start | bytes 4194304 | tf_op jit(solution)/shard_map/all_to_all | solution.py:491

commit v7 on v6

--- a/solution.py
+++ b/solution.py
@@ -371,7 +371,7 @@
     )(slots, parts, start)
 
 
-def ask_kernel(target_ref, slot_ref, plane_ref, weight_ref, message_out, sorted_ref, ready, held, send_sem, recv_sem):
+def ask_kernel(target_ref, slot_ref, plane_ref, weight_ref, sorted_ref, ready, held, send_sem, recv_sem):
     blocks = target_ref.shape[1]
     facets, size = lax.axis_size("facet"), lax.axis_size("vis")
     groups = facets * size
@@ -382,11 +382,22 @@
         peer = lax.rem(me + turn, groups)
         return peer, (peer // size, lax.rem(peer, size))
 
-    def greet(turn, carry):
+    def greet(turn):
         pl.semaphore_signal(barrier, inc=1, device_id=device(turn)[1], device_id_type=pl.DeviceIdType.MESH)
-        return carry
-
-    lax.fori_loop(1, groups, greet, 0)
+
+    def every(action):
+        rounds = (groups - 1) // 7
+
+        def some(i, carry):
+            for j in range(1, 8):
+                action(i * 7 + j)
+            return carry
+
+        lax.fori_loop(0, rounds, some, 0)
+        for turn in range(rounds * 7 + 1, groups):
+            action(turn)
+
+    every(greet)
 
     square = (blocks, blocks)
     down = lax.broadcasted_iota(jnp.int32, square, 0)
@@ -425,11 +436,9 @@
         jnp.sum(at * target_c, axis=0, keepdims=True),
         jnp.sum(at * plane_c, axis=0, keepdims=True),
     ]
-    sorted_ref[...] = jnp.concatenate(rows + rows, axis=0).astype(jnp.int32)
-
     pl.semaphore_wait(barrier, groups - 1)
 
-    def push(turn, carry):
+    def push(turn):
         peer, where = device(turn)
         pltpu.make_async_remote_copy(
             src_ref=ready.at[pl.ds(peer, 1)],
@@ -439,9 +448,8 @@
             device_id=where,
             device_id_type=pl.DeviceIdType.MESH,
         ).start()
-        return carry
-
-    lax.fori_loop(1, groups, push, 0)
+
+    every(push)
     everything = pltpu.make_async_remote_copy(
         src_ref=ready.at[pl.ds(0, groups - 1)],
         dst_ref=held.at[pl.ds(0, groups - 1)],
@@ -452,7 +460,13 @@
     )
     everything.wait_send()
     everything.wait_recv()
-    message_out[...] = jnp.where(down == me, ready[...], held[...])
+    message = jnp.where(down == me, ready[...], held[...])
+    for column in range(2):
+        rows.append(jnp.sum(equal * message[:, column:column + 1], axis=0, keepdims=True))
+    total = jnp.sum(message[:, 2:3], axis=0, keepdims=True)
+    rows.append(jnp.broadcast_to(total, rows[0].shape))
+    rows.append(rows[0])
+    sorted_ref[...] = jnp.concatenate(rows, axis=0)
 
 
 def ask(block_group, tile_slot, w_plane, vis_weight):
@@ -462,11 +476,8 @@
     return pl.pallas_call(
         ask_kernel,
         in_specs=[pl.BlockSpec(memory_space=pltpu.VMEM)] * 4,
-        out_specs=[pl.BlockSpec(memory_space=pltpu.VMEM)] * 2,
-        out_shape=[
-            jax.ShapeDtypeStruct((groups, 128), F32),
-            jax.ShapeDtypeStruct((8, blocks), jnp.int32),
-        ],
+        out_specs=pl.BlockSpec(memory_space=pltpu.VMEM),
+        out_shape=jax.ShapeDtypeStruct((8, blocks), F32),
         scratch_shapes=[
             pltpu.VMEM((groups, 128), F32),
             pltpu.VMEM((groups, 128), F32),
@@ -482,38 +493,38 @@
     blocks, nvis = vis_weight.shape
     groups = lax.axis_size(AXES)
     half = blocks // 2
-    message, plan = ask(block_group, tile_slot, w_plane, vis_weight)
-    place, order, position, planes = plan[0], plan[1], plan[2], plan[3]
-    requested = message[:, :2].astype(jnp.int32)
-    scale = (blocks * groups * nvis) / jnp.sum(message[:, 2])
+    told = ask(block_group, tile_slot, w_plane, vis_weight)
+    scale = (blocks * groups * nvis) / told[6, 0]
+    place, order, position, planes = [told[row].astype(jnp.int32) for row in range(4)]
+    requested = [told[row].astype(jnp.int32) for row in (4, 5)]
 
     def exchange(array):
         return lax.all_to_all(array, AXES, split_axis=0, concat_axis=0, tiled=True)
 
     chosen = [
-        jnp.take(model_tiles, jnp.maximum(requested[:, turn], 0), axis=0, mode="clip")
+        jnp.take(model_tiles, jnp.maximum(requested[turn], 0), axis=0, mode="clip")
         for turn in range(2)
     ]
     arrived = [exchange(chosen[0])]
     uv_sorted = jnp.take(uv_coords.transpose(1, 0, 2), order, axis=1, mode="clip")
     weight_sorted = jnp.take(vis_weight, order, axis=0, mode="clip") * scale
     matrices = plane_matrices(w_kernels)
-    late, matrices, uv_sorted, weight_sorted, order, position, planes = lax.optimization_barrier(
-        (chosen[1], matrices, uv_sorted, weight_sorted, order, position, planes)
+    indices = [[values[:half], values[half:]] for values in (order, position, planes)]
+    late, matrices, uv_sorted, weight_sorted, indices = lax.optimization_barrier(
+        (chosen[1], matrices, uv_sorted, weight_sorted, indices)
     )
     arrived.append(exchange(late))
     residual = None
     returned = []
     for turn in range(2):
-        part = slice(turn * half, turn * half + half)
         residual, outgoing = degrid_grid(
-            turn, order[part], position[part], planes[part], vis_obs, uv_sorted, weight_sorted,
+            turn, *[values[turn] for values in indices], vis_obs, uv_sorted, weight_sorted,
             arrived[turn], matrices, residual
         )
         returned.append(exchange(outgoing))
     residual = jnp.take(residual, place, axis=0, mode="clip").reshape(vis_obs.shape)
-    partial = sum_slots(requested[:, 0], returned[0], jnp.zeros(model_tiles.shape, F32))
-    return residual, sum_slots(requested[:, 1], returned[1], partial)
+    partial = sum_slots(requested[0], returned[0], jnp.zeros(model_tiles.shape, F32))
+    return residual, sum_slots(requested[1], returned[1], partial)
 
 
 def solution(mesh):

time: 184 us -> 182 us (0.989)
  transfers between devices with their start and end apart: 4 -> 4, of which waited for: 3 -> 3; matrix products, arithmetic and copies ran while one was open for 21% -> 22% of each run, Pallas kernels for 34% -> 35%
where the time goes in v7:
time: 182 us; the launch traced here: 181 us
  Pallas kernels  85.5 us (47%)
  starting transfers between devices  35.4 us (19%)
  local copies, waits for them, and re-layouts  30 us (16%)
  waiting for transfers between devices  15 us (8%)
  other arithmetic  12.1 us (7%)
    pallas_call x2, Pallas kernels, degrid_grid(): pl.pallas_call(block_kernel, grid_spec=pltpu.PrefetchScalarGridSpec(num_s...  57.8 us
    all_to_all x4, starting transfers between devices, exchange(): return lax.all_to_all(array, AXES, split_axis=0, concat_axis=0, tiled=True)  35.4 us
    pallas_call x1, Pallas kernels, ask(): pl.pallas_call(ask_kernel, in_specs=[pl.BlockSpec(memory_space=pltpu.VMEM...  18.1 us
    all_to_all x4, waiting for transfers between devices, exchange(): return lax.all_to_all(array, AXES, split_axis=0, concat_axis=0, tiled=True)  15 us
    pallas_call x2, Pallas kernels, sum_slots(): pl.pallas_call(sum_kernel, grid_spec=pltpu.PrefetchScalarGridSpec(num_sca...  9.71 us
    gather x2, local copies, waits for them, and re-layouts, shards(): jnp.take(model_tiles, jnp.maximum(requested[turn], 0), axis=0, mode='clip')  5.49 us
    reshape x1, local copies, waits for them, and re-layouts, shards(): jnp.take(residual, place, axis=0, mode='clip').reshape(vis_obs.shape)  5.16 us
    gather x1, local copies, waits for them, and re-layouts, shards(): jnp.take(residual, place, axis=0, mode='clip').reshape(vis_obs.shape)  4.95 us
  transfers between devices with their start and end apart: 4, of which 3 were waited for; matrix products, arithmetic and copies ran while one was open for 22% of the time, Pallas kernels for 35%

profile of v7, /device:TPU:1, one launch (start us, length us, event | category | flops | bytes accessed | tf_op | source)
XLA Modules:
  0.0 181.0 jit_solution(12483684013954125125)
XLA Ops:
  0.6 18.1 %ask.1 = f32[8,128]{1,0:T(8,128)} custom-call(s32[1,128]{1,0:T(1,128)} %bitcast.61, s32[1,128]{1,0:T(1,128)} %bitcast.62, s32[1,128]{1,0:T(1,128)} %bitcast.63, f32[128,1024]{1,0:T(8,128)} %weight_ref.1), custom_call_target="tpu_custom_call" | custom-call | tf_op jit(solution)/shard_map/ask/pallas_call | solution.py:476
  19.5 3.4 %gather_fusion.3 = bf16[128,2,32,128]{3,2,1,0:T(8,128)(2,1)} fusion(bf16[64,2,32,128]{3,2,1,0:T(8,128)(2,1)} %param.16, s32[1024]{0:T(1024)S(1)} %pad_clamp_fusion.1), kind=kCustom, calls=%fused_computation.3 | custom fusion | bytes 4194816 | tf_op jit(solution)/shard_map/jit(_take)/gather | solution.py:505
  22.8 7.0 %all-to-all-start.1 = ((bf16[128,2,32,128]{3,2,1,0:T(8,128)(2,1)}), bf16[128,2,32,128]{3,2,1,0:T(8,128)(2,1)}, u32[]{:S(2)}, u32[]{:S(2)}) async-start(bf16[128,2,32,128]{3,2,1,0:T(8,128)(2,1)} %gather_fusion.3), calls=%async_computation.1 | async-start | bytes 4194304 | tf_op jit(solution)/shard_map/all_to_all | solution.py:502
  32.0 1.6 gather_fusion.2
  33.6 3.0 %gather_fusion.1 = f32[128,2,1024]{2,1,0:T(2,128)S(1)} fusion(f32[2,128,1024]{2,0,1:T(2,128)} %bitcast.59, s32[1024]{0:T(1024)S(1)} %pad_clamp_fusion.2), kind=kCustom, calls=%fused_computation.1 | custom fusion | bytes 2097664 | tf_op jit(solution)/shard_map/jit(_take)/gather | solution.py:509
  36.6 1.3 copy.31
  38.0 2.1 %gather_fusion = bf16[128,2,32,128]{3,2,1,0:T(8,128)(2,1)} fusion(bf16[64,2,32,128]{3,2,1,0:T(8,128)(2,1)S(1)} %copy-done.1, s32[1024]{0:T(1024)S(1)} %pad_clamp_fusion.3), kind=kCustom, calls=%fused_computation | custom fusion | bytes 4194816 | tf_op jit(solution)/shard_map/jit(_take)/gather | solution.py:505
  40.1 1.5 reduce-precision_convert_fusion
  41.6 1.3 stack.10
  43.0 1.1 stack.9
  44.1 4.4 %maximum_bitcast_fusion = bf16[32,2,2,32,256]{4,2,3,0,1:T(2,128)(2,1)S(1)} fusion(bf16[32,1,32,2,256]{4,3,2,0,1:T(2,128)(2,1)S(1)} %stack.10, bf16[32,1,32,2,256]{4,3,2,0,1:T(2,128)(2,1)} %stack.9), kind=kLoop, calls=%fused_computation.9 | loop fusion | flops 1048576 | bytes 4194304 | tf_op jit(solution)/shard_map/transpose | solution.py:267
  49.7 3.8 %bitcast_select_fusion.refs_6_ = bf16[32,2,256,256]{3,2,1,0:T(8,128)(2,1)} fusion(pred[256,256]{1,0:T(8,128)(4,1)S(1)} %bitcast.60, bf16[32,2,2,32,256]{4,3,2,1,0:T(8,128)(2,1)S(1)} %copy.22), kind=kLoop, calls=%fused_computation.5 | loop fusion | flops 4194304 | bytes 10551296 | tf_op jit(solution)/shard_map/jit(_where)/select_n | solution.py:270
  57.3 1.8 %all-to-all-done.1.refs_3_ = bf16[128,2,32,128]{3,2,1,0:T(8,128)(2,1)} async-done(((bf16[128,2,32,128]{3,2,1,0:T(8,128)(2,1)}), bf16[128,2,32,128]{3,2,1,0:T(8,128)(2,1)}, u32[]{:S(2)}, u32[]{:S(2)}) %all-to-all-start.1) | async-done | bytes 2097184 | tf_op jit(solution)/shard_map/all_to_all | solution.py:502
  59.1 8.4 %all-to-all-start = ((bf16[128,2,32,128]{3,2,1,0:T(8,128)(2,1)}), bf16[128,2,32,128]{3,2,1,0:T(8,128)(2,1)}, u32[]{:S(2)}, u32[]{:S(2)}) async-start(bf16[128,2,32,128]{3,2,1,0:T(8,128)(2,1)} %gather_fusion), calls=%async_computation | async-start | bytes 4194304 | tf_op jit(solution)/shard_map/all_to_all | solution.py:502
  68.6 28.9 %degrid_grid_0.1 = (f32[128,8,1024]{2,1,0:T(8,128)}, bf16[128,2,32,128]{3,2,1,0:T(8,128)(2,1)}) custom-call(s32[64]{0:T(128)} %get-tuple-element.27.order_ref, s32[64]{0:T(128)} %get-tuple-element.28.pos_ref, s32[64]{0:T(128)} %get-tuple-element.29.plane_ref, f32[128,2,4,1024]{3,2,1,0:T(4,128)} %refs_0_.3, f32[2,128,1024]{2,1,0:T(8,128)} %bitcast.57, ...), custom_call_target="tpu_custom_call" | custom-call | flops 5120000000 | bytes 7680000 | tf_op jit(solution)/shard_map/degrid_grid_0/pallas_call | solution.py:301
  97.5 10.2 %all-to-all-start.3 = ((bf16[128,2,32,128]{3,2,1,0:T(8,128)(2,1)}), bf16[128,2,32,128]{3,2,1,0:T(8,128)(2,1)}, u32[]{:S(2)}, u32[]{:S(2)}) async-start(bf16[128,2,32,128]{3,2,1,0:T(8,128)(2,1)} %get-tuple-element.33), calls=%async_computation.3 | async-start | bytes 4194304 | tf_op jit(solution)/shard_map/all_to_all | solution.py:502
  107.7 28.9 %degrid_grid_1.1 = (f32[128,8,1024]{2,1,0:T(8,128)}, bf16[128,2,32,128]{3,2,1,0:T(8,128)(2,1)}) custom-call(s32[64]{0:T(128)} %get-tuple-element.18.order_ref, s32[64]{0:T(128)} %get-tuple-element.19.pos_ref, s32[64]{0:T(128)} %get-tuple-element.20.plane_ref, f32[128,2,4,1024]{3,2,1,0:T(4,128)} %refs_0_.3, ...), custom_call_target="tpu_custom_call", output_to_operand_aliasing={{0}: (10, {})} | custom-call | flops 5120000000 | bytes 7680000 | tf_op jit(solution)/shard_map/degrid_grid_1/pallas_call | solution.py:301
  137.0 9.8 %all-to-all-start.2 = ((bf16[128,2,32,128]{3,2,1,0:T(8,128)(2,1)}), bf16[128,2,32,128]{3,2,1,0:T(8,128)(2,1)}, u32[]{:S(2)}, u32[]{:S(2)}) async-start(bf16[128,2,32,128]{3,2,1,0:T(8,128)(2,1)} %get-tuple-element.32), calls=%async_computation.2 | async-start | bytes 4194304 | tf_op jit(solution)/shard_map/all_to_all | solution.py:502
  146.9 5.0 %gather_fusion.4 = f32[128,8,1024]{2,1,0:T(8,128)} fusion(f32[128,8,1024]{2,1,0:T(8,128)} %get-tuple-element.31, s32[1024]{0:T(1024)S(1)} %pad_clamp_fusion), kind=kCustom, calls=%fused_computation.4 | custom fusion | bytes 8389120 | tf_op jit(solution)/shard_map/jit(_take)/gather | solution.py:525
  151.8 5.2 %reshape.95 = f32[128,2,4,1024]{3,2,1,0:T(4,128)} reshape(f32[128,8,1024]{2,1,0:T(8,128)} %gather_fusion.4) | data formatting | bytes 8388608 | tf_op jit(solution)/shard_map/reshape | solution.py:525
  157.0 1.6 broadcast_in_dim.48.start_ref
  158.6 4.9 %sum_slots.2.start_ref = f32[64,2,32,128]{3,2,1,0:T(8,128)} custom-call(s32[128]{0:T(128)} %get-tuple-element.40.slot_ref, bf16[128,2,32,128]{3,2,1,0:T(8,128)(2,1)} %all-to-all-done.3.part_ref, f32[64,2,32,128]{3,2,1,0:T(8,128)} %broadcast_in_dim.48.start_ref), custom_call_target="tpu_custom_call" | custom-call | flops 4000000 | bytes 6000000 | tf_op jit(solution)/shard_map/sum_slots/pallas_call | solution.py:359
  163.4 12.7 %all-to-all-done.2.part_ref = bf16[128,2,32,128]{3,2,1,0:T(8,128)(2,1)} async-done(((bf16[128,2,32,128]{3,2,1,0:T(8,128)(2,1)}), bf16[128,2,32,128]{3,2,1,0:T(8,128)(2,1)}, u32[]{:S(2)}, u32[]{:S(2)}) %all-to-all-start.2) | async-done | bytes 2097184 | tf_op jit(solution)/shard_map/all_to_all | solution.py:502
  176.2 4.8 %sum_slots.3 = f32[64,2,32,128]{3,2,1,0:T(8,128)} custom-call(s32[128]{0:T(128)} %get-tuple-element.42.slot_ref, bf16[128,2,32,128]{3,2,1,0:T(8,128)(2,1)} %all-to-all-done.2.part_ref, f32[64,2,32,128]{3,2,1,0:T(8,128)} %sum_slots.2.start_ref), custom_call_target="tpu_custom_call" | custom-call | flops 4000000 | bytes 6000000 | tf_op jit(solution)/shard_map/sum_slots/pallas_call | solution.py:359
  (39 shorter events, 8.7 us)
Async XLA Ops:
  22.8 7.0 %copy-start.3 = (bf16[32,2,32,32]{3,2,1,0:T(8,128)(2,1)S(1)}, bf16[32,2,32,32]{3,2,1,0:T(8,128)(2,1)}, u32[]{:S(2)}) copy-start(bf16[32,2,32,32]{3,2,1,0:T(8,128)(2,1)} %param.17) | copy-start | bytes 393220
  22.8 7.0 %copy-start.6 = (f32[8,128]{1,0:T(8,128)S(1)}, f32[8,128]{1,0:T(8,128)}, u32[]{:S(2)}) copy-start(f32[8,128]{1,0:T(8,128)} %ask.1) | copy-start | bytes 12292
  22.8 36.3 %all-to-all-start.1 = ((bf16[128,2,32,128]{3,2,1,0:T(8,128)(2,1)}), bf16[128,2,32,128]{3,2,1,0:T(8,128)(2,1)}, u32[]{:S(2)}, u32[]{:S(2)}) async-start(bf16[128,2,32,128]{3,2,1,0:T(8,128)(2,1)} %gather_fusion.3), calls=%async_computation.1 | async-start | bytes 4194304 | tf_op jit(solution)/shard_map/all_to_all | solution.py:502
  29.8 2.2 %copy-start = (f32[128,1024]{1,0:T(8,128)S(1)}, f32[128,1024]{1,0:T(8,128)}, u32[]{:S(2)}) copy-start(f32[128,1024]{1,0:T(8,128)} %weight_ref.1) | copy-start | bytes 1572868
  33.6 4.3 %copy-start.1 = (bf16[64,2,32,128]{3,2,1,0:T(8,128)(2,1)S(1)}, bf16[64,2,32,128]{3,2,1,0:T(8,128)(2,1)}, u32[]{:S(2)}) copy-start(bf16[64,2,32,128]{3,2,1,0:T(8,128)(2,1)} %param.16) | copy-start | bytes 3145732
  38.0 2.2 %copy-start.4 = (bf16[32,2,32,32]{3,2,1,0:T(8,128)(2,1)S(1)}, bf16[32,2,32,32]{3,2,1,0:T(8,128)(2,1)}, u32[]{:S(2)}) copy-start(bf16[32,2,32,32]{3,2,1,0:T(8,128)(2,1)} %param.17) | copy-start | bytes 393220
  38.0 2.2 %copy-start.5 = (bf16[2,32,512,1]{2,1,0,3:T(8,128)(2,1)S(1)}, bf16[2,32,512,1]{2,1,0,3:T(8,128)(2,1)}, u32[]{:S(2)}) copy-start(bf16[2,32,512,1]{2,1,0,3:T(8,128)(2,1)} %constant.19) | copy-start | bytes 196612
  48.5 1.2 copy-start.7
  53.6 2.9 %copy-start.2 = (f32[128,1024]{1,0:T(8,128)S(1)}, f32[128,1024]{1,0:T(8,128)}, u32[]{:S(2)}) copy-start(f32[128,1024]{1,0:T(8,128)} %gather_fusion.2) | copy-start | bytes 1572868
  59.1 38.3 %all-to-all-start = ((bf16[128,2,32,128]{3,2,1,0:T(8,128)(2,1)}), bf16[128,2,32,128]{3,2,1,0:T(8,128)(2,1)}, u32[]{:S(2)}, u32[]{:S(2)}) async-start(bf16[128,2,32,128]{3,2,1,0:T(8,128)(2,1)} %gather_fusion), calls=%async_computation | async-start | bytes 4194304 | tf_op jit(solution)/shard_map/all_to_all | solution.py:502
  97.5 39.6 %all-to-all-start.3 = ((bf16[128,2,32,128]{3,2,1,0:T(8,128)(2,1)}), bf16[128,2,32,128]{3,2,1,0:T(8,128)(2,1)}, u32[]{:S(2)}, u32[]{:S(2)}) async-start(bf16[128,2,32,128]{3,2,1,0:T(8,128)(2,1)} %get-tuple-element.33), calls=%async_computation.3 | async-start | bytes 4194304 | tf_op jit(solution)/shard_map/all_to_all | solution.py:502
  137.0 39.1 %all-to-all-start.2 = ((bf16[128,2,32,128]{3,2,1,0:T(8,128)(2,1)}), bf16[128,2,32,128]{3,2,1,0:T(8,128)(2,1)}, u32[]{:S(2)}, u32[]{:S(2)}) async-start(bf16[128,2,32,128]{3,2,1,0:T(8,128)(2,1)} %get-tuple-element.32), calls=%async_computation.2 | async-start | bytes 4194304 | tf_op jit(solution)/shard_map/all_to_all | solution.py:502
